TPU v7x, 32 devices: a whole 2x2x4 slice. The times are simulated.
32 devices in a mesh: dp: 4 (over x, core), seq: 8 (over z, y).
Axes of the slice: x: 2, y: 2, z: 4, core: 2. Of those that a mesh axis runs over, the one named last changes fastest.
Arguments:
- inputs: bfloat16 [4, 8192, 384], P('dp', 'seq'), may hold values from -6 to 6
- cotangent: bfloat16 [4, 8192, 384], P('dp', 'seq'), may hold values from -6 to 6
- first_dilated_kernel: bfloat16 [3, 384, 192], replicated, may hold values from -0.1875 to 0.1875
- first_pointwise_weight: bfloat16 [192, 384], replicated, may hold values from -0.4375 to 0.4375
- second_dilated_kernel: bfloat16 [3, 384, 192], replicated, may hold values from -0.1875 to 0.1875
- second_pointwise_weight: bfloat16 [192, 384], replicated, may hold values from -0.4375 to 0.4375
Outputs:
- input_gradient: bfloat16 [4, 8192, 384], P('dp', 'seq')
- conv_first_grad: float32 [3, 384, 192], P(None, 'dp')
- point_first_grad: float32 [192, 384], P(None, 'dp')
- conv_second_grad: float32 [3, 384, 192], P(None, 'dp')
- point_second_grad: float32 [192, 384], P(None, 'dp')
All inputs are finite; a program needn't handle non-finite values.
Results may differ from a plain program's by a relative error of at most 0.0071.
Values may be sent and summed in bfloat16 or wider, within the bound.
No kernel may reach another device: no remote copies, remote signals or barrier semaphores. Data moves between devices by JAX's collectives and lax.ppermute only.
A program may use at most 64 MiB of HBM per device.

v0:
```python
import math

import jax
import jax.numpy as jnp
from jax import lax
from jax.sharding import PartitionSpec as P

DILATION_ONE = 2048
DILATION_TWO = 4096


def passed_along(block, axis, distance):
    devices = range(lax.axis_size(axis))
    route = [(i - distance, i) for i in devices if i - distance in devices]
    return lax.ppermute(block, axis, route)


def gelu_parts(values):
    coeff = math.sqrt(2.0 / math.pi)
    inner = coeff * (values + 0.044715 * values * values * values)
    tanh_val = jnp.tanh(inner)
    value = 0.5 * values * (1.0 + tanh_val)
    slope = 0.5 * (1.0 + tanh_val) + 0.5 * values * (1.0 - tanh_val * tanh_val) * coeff * (
        1.0 + 3.0 * 0.044715 * values * values
    )
    return (value, slope)


def matmul(left, right):
    return jnp.dot(left, right, preferred_element_type=jnp.float32)


def flatten(array):
    return array.reshape(-1, array.shape[-1])


def act_taps(act, shard_hops):
    after_rows = passed_along(act, "seq", -shard_hops)
    before_rows = passed_along(act, "seq", shard_hops)
    return (after_rows, before_rows)


def grad_taps(pre_grad, shard_hops):
    after_rows = passed_along(pre_grad, "seq", -shard_hops)
    before_rows = passed_along(pre_grad, "seq", shard_hops)
    return (after_rows, before_rows)


def residual_block_forward(state, kernel, pointwise, shard_hops, want_output):
    act = gelu_parts(state.astype(jnp.float32))[0].astype(jnp.bfloat16)
    after_rows, before_rows = act_taps(act, shard_hops)
    pre = (
        matmul(flatten(before_rows), kernel[0])
        + matmul(flatten(act), kernel[1])
        + matmul(flatten(after_rows), kernel[2])
    )
    mid_val, pre_slope = gelu_parts(pre)
    mid = mid_val.astype(jnp.bfloat16)
    output = None
    if want_output:
        output = (
            (flatten(state).astype(jnp.float32) + matmul(mid, pointwise))
            .astype(jnp.bfloat16)
            .reshape(state.shape)
        )
    return (output, act, pre_slope, mid)


def residual_block_backward(state, upstream, kernel, pointwise, shard_hops, act, pre_slope, mid):
    upstream_flat = flatten(upstream)
    mid_grad = matmul(upstream_flat, pointwise.T)
    pre_grad = (mid_grad * pre_slope).astype(jnp.bfloat16)
    pre_grad_full = pre_grad.reshape(state.shape[0], state.shape[1], pre_grad.shape[-1])
    after_rows, before_rows = grad_taps(pre_grad_full, shard_hops)
    after_flat = flatten(after_rows)
    before_flat = flatten(before_rows)
    act_flat = flatten(act)
    point_sum = matmul(mid.T, upstream_flat)
    conv_sum = jnp.stack(
        [
            matmul(act_flat.T, after_flat),
            matmul(act_flat.T, pre_grad),
            matmul(act_flat.T, before_flat),
        ]
    )
    act_grad = (
        matmul(after_flat, kernel[0].T)
        + matmul(pre_grad, kernel[1].T)
        + matmul(before_flat, kernel[2].T)
    )
    state_slope = gelu_parts(flatten(state).astype(jnp.float32))[1]
    state_grad = (upstream_flat.astype(jnp.float32) + act_grad * state_slope).astype(jnp.bfloat16)
    return (state_grad.reshape(state.shape), conv_sum, point_sum)


def reduce_weights(conv_sum, point_sum, scale):
    whole_conv, whole_point = lax.psum((conv_sum, point_sum), "seq")
    part_conv, part_point = (
        lax.psum_scatter(whole_conv, "dp", scatter_dimension=1, tiled=True),
        lax.psum_scatter(whole_point, "dp", scatter_dimension=1, tiled=True),
    )
    return (part_conv * scale, part_point * scale)


def shards(
    inputs,
    cotangent,
    first_dilated_kernel,
    first_pointwise_weight,
    second_dilated_kernel,
    second_pointwise_weight,
):
    resident_rows = inputs.shape[1]
    first_block_jumps = DILATION_ONE // resident_rows
    second_block_jumps = DILATION_TWO // resident_rows
    total_rows = inputs.shape[0] * lax.axis_size("dp") * resident_rows * lax.axis_size("seq")
    scale = 1.0 / math.sqrt(total_rows)
    hidden_block_state, first_block_activation, first_gelu_derivative, first_middle_value = (
        residual_block_forward(
            inputs, first_dilated_kernel, first_pointwise_weight, first_block_jumps, True
        )
    )
    ignored_placeholder, second_block_activation, second_gelu_derivative, second_middle_value = (
        residual_block_forward(
            hidden_block_state,
            second_dilated_kernel,
            second_pointwise_weight,
            second_block_jumps,
            False,
        )
    )
    second_block_gradient, second_kernel_value, second_pointwise_value = residual_block_backward(
        hidden_block_state,
        cotangent,
        second_dilated_kernel,
        second_pointwise_weight,
        second_block_jumps,
        second_block_activation,
        second_gelu_derivative,
        second_middle_value,
    )
    conv_second_grad, point_second_grad = reduce_weights(
        second_kernel_value, second_pointwise_value, scale
    )
    input_gradient, first_kernel_value, first_pointwise_value = residual_block_backward(
        inputs,
        second_block_gradient,
        first_dilated_kernel,
        first_pointwise_weight,
        first_block_jumps,
        first_block_activation,
        first_gelu_derivative,
        first_middle_value,
    )
    conv_first_grad, point_first_grad = reduce_weights(
        first_kernel_value, first_pointwise_value, scale
    )
    return (input_gradient, conv_first_grad, point_first_grad, conv_second_grad, point_second_grad)


def solution(mesh):
    return jax.shard_map(
        shards,
        mesh=mesh,
        in_specs=(P("dp", "seq", None), P("dp", "seq", None), P(), P(), P(), P()),
        out_specs=(
            P("dp", "seq", None),
            P(None, "dp", None),
            P(None, "dp"),
            P(None, "dp", None),
            P(None, "dp"),
        ),
        check_vma=False,
    )
```

profile of v0, /device:TPU:0, one launch (start us, length us, event | category | flops | bytes accessed | tf_op | source)
XLA Modules:
  0.0 278.4 jit_solution(17049231830426986339)
XLA Ops:
  7.2 1.8 fusion.29
  9.0 1.3 collective-permute-start.1
  10.3 5.6 %collective-permute-start = (bf16[1,1024,384]{2,1,0:T(8,128)(2,1)S(1)}, bf16[1,1024,384]{2,1,0:T(8,128)(2,1)S(1)}, u32[]{:S(2)}, u32[]{:S(2)}) collective-permute-start(bf16[1,1024,384]{2,1,0:T(8,128)(2,1)S(1)} %fusion.29), channel_id=1, source_target_pairs={{0,2},{1,3},{2,4},{3,5},{4,6},{5,7},{8,10},{9,11},{10,12},{11,13},... | collective-permute-start | bytes 2359304 | tf_op jit(solution)/shard_map/ppermute | solution.py:15
  15.9 0.4 fusion.58
  16.4 15.1 %collective-permute-done.1 = bf16[1,1024,384]{2,1,0:T(8,128)(2,1)S(1)} collective-permute-done((bf16[1,1024,384]{2,1,0:T(8,128)(2,1)S(1)}, bf16[1,1024,384]{2,1,0:T(8,128)(2,1)S(1)}, u32[]{:S(2)}, u32[]{:S(2)}) %collective-permute-start.1) | collective-permute-done | bytes 786464 | tf_op jit(solution)/shard_map/ppermute | solution.py:15
  31.5 0.4 fusion.53
  31.9 0.7 collective-permute-done
  32.6 0.4 fusion.36
  33.1 0.5 fusion.17
  33.7 0.6 fusion.119
  34.2 1.3 collective-permute-start.3
  35.5 5.7 %collective-permute-start.2 = (bf16[1,1024,384]{2,1,0:T(8,128)(2,1)S(1)}, bf16[1,1024,384]{2,1,0:T(8,128)(2,1)S(1)}, u32[]{:S(2)}, u32[]{:S(2)}) collective-permute-start(bf16[1,1024,384]{2,1,0:T(8,128)(2,1)S(1)} %fusion.119), channel_id=1, source_target_pairs={{0,4},{1,5},{2,6},{3,7},{8,12},{9,13},{10,14},{11,15},{16,20},{17,... | collective-permute-start | bytes 2359304 | tf_op jit(solution)/shard_map/ppermute | solution.py:15
  41.2 0.8 fusion.88
  42.0 30.5 %collective-permute-done.3 = bf16[1,1024,384]{2,1,0:T(8,128)(2,1)S(1)} collective-permute-done((bf16[1,1024,384]{2,1,0:T(8,128)(2,1)S(1)}, bf16[1,1024,384]{2,1,0:T(8,128)(2,1)S(1)}, u32[]{:S(2)}, u32[]{:S(2)}) %collective-permute-start.3) | collective-permute-done | bytes 786464 | tf_op jit(solution)/shard_map/ppermute | solution.py:15
  72.5 0.4 fusion.50
  73.0 0.4 fusion.37
  73.4 0.7 copy-done.16
  74.1 1.5 fusion.38
  75.6 2.2 collective-permute-start.5
  77.8 1.3 collective-permute-start.4
  79.1 1.5 fusion.86
  80.5 1.3 convolution_bitcast_fusion
  81.8 2.7 convolution_bitcast_fusion.3
  84.7 13.6 %collective-permute-done.4 = bf16[1,1024,192]{1,2,0:T(8,128)(2,1)S(1)} collective-permute-done((bf16[1,1024,192]{1,2,0:T(8,128)(2,1)}, bf16[1,1024,192]{1,2,0:T(8,128)(2,1)S(1)}, u32[]{:S(2)}, u32[]{:S(2)}) %collective-permute-start.4) | collective-permute-done | bytes 393248 | tf_op jit(solution)/shard_map/ppermute | solution.py:15
  98.3 0.5 fusion.78
  98.8 2.5 fusion.16
  101.3 0.9 copy-done.19
  102.2 1.3 convolution_bitcast_fusion.1
  103.5 0.2 reduce-scatter.17.cloned.1.call-start
  103.8 1.7 convolution_bitcast_fusion.2
  105.5 0.8 convolution_bitcast_fusion.4
  106.3 0.2 copy-done.13
  106.6 0.9 copy.19
  107.4 1.8 reshape.87
  109.3 2.1 fusion.39
  111.4 1.3 collective-permute-start.7
  112.7 1.3 collective-permute-start.6
  114.0 0.4 convolution_bitcast_fusion.6
  114.3 5.0 %collective-permute-done.7 = bf16[1,1024,192]{1,2,0:T(8,128)(2,1)S(1)} collective-permute-done((bf16[1,1024,192]{1,2,0:T(8,128)(2,1)S(1)}, bf16[1,1024,192]{1,2,0:T(8,128)(2,1)S(1)}, u32[]{:S(2)}, u32[]{:S(2)}) %collective-permute-start.7) | collective-permute-done | bytes 393248 | tf_op jit(solution)/shard_map/ppermute | solution.py:15
  119.3 0.4 convolution_bitcast_fusion.5
  119.7 3.8 %collective-permute-done.6 = bf16[1,1024,192]{1,2,0:T(8,128)(2,1)S(1)} collective-permute-done((bf16[1,1024,192]{1,2,0:T(8,128)(2,1)S(1)}, bf16[1,1024,192]{1,2,0:T(8,128)(2,1)S(1)}, u32[]{:S(2)}, u32[]{:S(2)}) %collective-permute-start.6) | collective-permute-done | bytes 393248 | tf_op jit(solution)/shard_map/ppermute | solution.py:15
  123.4 0.4 convolution_bitcast_fusion.7
  123.9 0.9 copy.15
  124.8 1.8 reshape.83
  126.6 0.5 fusion.94
  127.1 1.6 copy.22
  128.7 6.0 %reduce-scatter.15.cloned.1.call-done = f32[96,192]{1,0:T(8,128)} async-done(((f32[384,192]{1,0:T(8,128)}), f32[96,192]{1,0:T(8,128)}) %reduce-scatter.15.cloned.1.call-update) | async-done | bytes 73744
  134.8 1.6 copy.18
  136.4 25.5 %reduce-scatter.17.cloned.1.call-done = f32[96,576]{1,0:T(8,128)} async-done(((f32[384,576]{1,0:T(8,128)}), f32[96,576]{1,0:T(8,128)}) %reduce-scatter.17.cloned.1.call-update) | async-done | bytes 221200
  161.9 1.1 reshape.88
  163.0 0.9 copy.20
  163.9 25.1 %reduce-scatter.13.cloned.1.call-done = f32[96,576]{1,0:T(8,128)} async-done(((f32[384,576]{1,0:T(8,128)}), f32[96,576]{1,0:T(8,128)}) %reduce-scatter.13.cloned.1.call-update) | async-done | bytes 221200
  189.0 1.1 reshape.84
  190.2 0.9 copy.16
  191.1 0.5 fusion.70
  191.6 0.5 copy-done.12
  192.1 0.3 copy-done.5
  192.3 0.2 copy-done.20
  192.6 2.3 fusion.63
  194.9 73.5 %all-reduce.3.cloned.1.call-done = (f32[3,96,192]{1,2,0:T(8,128)}, f32[192,96]{1,0:T(8,128)}, f32[3,96,192]{1,2,0:T(8,128)}, f32[192,96]{1,0:T(8,128)}) async-done(((f32[3,96,192]{1,2,0:T(8,128)}, f32[192,96]{1,0:T(8,128)}, f32[3,96,192]{1,2,0:T(8,128)}, f32[192,96]{1,0:T(8,128)}), (f32[3,96,192]{1,2,0:T(8,128)}, f32[192,96]{1,0:T(8,128)}, f32[3,96,192]{1,2,0:T(8,128)}, ...) | async-done | bytes 589840 | tf_op jit(solution)/shard_map/psum | solution.py:97
  268.3 1.1 broadcast_multiply_fusion
  269.5 0.9 copy.14
  270.3 0.9 copy.13
  271.2 0.7 broadcast_multiply_fusion.2
  (50 shorter events, 0.5 us)
Async XLA Ops:
  7.2 25.9 %copy-start = (bf16[192,384]{1,0:T(8,128)(2,1)S(1)}, bf16[192,384]{1,0:T(8,128)(2,1)}, u32[]{:S(2)}) copy-start(bf16[192,384]{1,0:T(8,128)(2,1)} %param.9) | copy-start | bytes 442372
  7.2 8.7 %copy-start.1 = (bf16[3,384,192]{1,2,0:T(8,128)(2,1)S(1)}, bf16[3,384,192]{1,2,0:T(8,128)(2,1)}, u32[]{:S(2)}) copy-start(bf16[3,384,192]{1,2,0:T(8,128)(2,1)} %param.8) | copy-start | bytes 1327108
  7.2 119.9 %reduce-scatter.19.cloned.1.call-start = ((), (), s32[]{:S(2)}) async-start(), calls=%async_computation.7 | async-start | bytes 491520
  9.0 22.5 %collective-permute-start.1 = (bf16[1,1024,384]{2,1,0:T(8,128)(2,1)S(1)}, bf16[1,1024,384]{2,1,0:T(8,128)(2,1)S(1)}, u32[]{:S(2)}, u32[]{:S(2)}) collective-permute-start(bf16[1,1024,384]{2,1,0:T(8,128)(2,1)S(1)} %fusion.29), channel_id=1, source_target_pairs={{2,0},{3,1},{4,2},{5,3},{6,4},{7,5},{10,8},{11,9},{12,10},{13,11},... | collective-permute-start | bytes 2359304 | tf_op jit(solution)/shard_map/ppermute | solution.py:15
  10.3 22.3 %collective-permute-start = (bf16[1,1024,384]{2,1,0:T(8,128)(2,1)S(1)}, bf16[1,1024,384]{2,1,0:T(8,128)(2,1)S(1)}, u32[]{:S(2)}, u32[]{:S(2)}) collective-permute-start(bf16[1,1024,384]{2,1,0:T(8,128)(2,1)S(1)} %fusion.29), channel_id=1, source_target_pairs={{0,2},{1,3},{2,4},{3,5},{4,6},{5,7},{8,10},{9,11},{10,12},{11,13},... | collective-permute-start | bytes 2359304 | tf_op jit(solution)/shard_map/ppermute | solution.py:15
  31.9 1.2 copy-start.4
  33.1 39.9 %copy-start.9 = (f32[1024,192]{0,1:T(8,128)}, f32[1024,192]{0,1:T(8,128)S(1)}, u32[]{:S(2)}) copy-start(f32[1024,192]{0,1:T(8,128)S(1)} %fusion.36) | copy-start | bytes 2359300
  33.1 8.1 %copy-start.3 = (bf16[3,384,192]{1,2,0:T(8,128)(2,1)S(1)}, bf16[3,384,192]{1,2,0:T(8,128)(2,1)}, u32[]{:S(2)}) copy-start(bf16[3,384,192]{1,2,0:T(8,128)(2,1)} %param.10) | copy-start | bytes 1327108
  33.7 8.3 %copy-start.6 = (bf16[1024,384]{1,0:T(8,128)(2,1)}, bf16[1024,384]{1,0:T(8,128)(2,1)S(1)}, u32[]{:S(2)}) copy-start(bf16[1024,384]{1,0:T(8,128)(2,1)S(1)} %fusion.17) | copy-start | bytes 2359300
  34.2 38.3 %collective-permute-start.3 = (bf16[1,1024,384]{2,1,0:T(8,128)(2,1)S(1)}, bf16[1,1024,384]{2,1,0:T(8,128)(2,1)S(1)}, u32[]{:S(2)}, u32[]{:S(2)}) collective-permute-start(bf16[1,1024,384]{2,1,0:T(8,128)(2,1)S(1)} %fusion.119), channel_id=1, source_target_pairs={{4,0},{5,1},{6,2},{7,3},{12,8},{13,9},{14,10},{15,11},{20,16},{21,... | collective-permute-start | bytes 2359304 | tf_op jit(solution)/shard_map/ppermute | solution.py:15
  35.5 37.5 %collective-permute-start.2 = (bf16[1,1024,384]{2,1,0:T(8,128)(2,1)S(1)}, bf16[1,1024,384]{2,1,0:T(8,128)(2,1)S(1)}, u32[]{:S(2)}, u32[]{:S(2)}) collective-permute-start(bf16[1,1024,384]{2,1,0:T(8,128)(2,1)S(1)} %fusion.119), channel_id=1, source_target_pairs={{0,4},{1,5},{2,6},{3,7},{8,12},{9,13},{10,14},{11,15},{16,20},{17,... | collective-permute-start | bytes 2359304 | tf_op jit(solution)/shard_map/ppermute | solution.py:15
  73.0 1.1 copy-start.16
  73.0 1.1 copy-start.18
  75.6 23.2 %collective-permute-start.5 = (bf16[1,1024,192]{1,2,0:T(8,128)(2,1)}, bf16[1,1024,192]{1,2,0:T(8,128)(2,1)}, u32[]{:S(2)}, u32[]{:S(2)}) collective-permute-start(bf16[1,1024,192]{1,2,0:T(8,128)(2,1)} %bitcast.14), channel_id=1, source_target_pairs={{0,4},{1,5},{2,6},{3,7},{8,12},{9,13},{10,14},{11,15},{16,20},{17,... | collective-permute-start | bytes 1179656 | tf_op jit(solution)/shard_map/ppermute | solution.py:15
  77.8 20.5 %collective-permute-start.4 = (bf16[1,1024,192]{1,2,0:T(8,128)(2,1)}, bf16[1,1024,192]{1,2,0:T(8,128)(2,1)S(1)}, u32[]{:S(2)}, u32[]{:S(2)}) collective-permute-start(bf16[1,1024,192]{1,2,0:T(8,128)(2,1)} %bitcast.14), channel_id=1, source_target_pairs={{4,0},{5,1},{6,2},{7,3},{12,8},{13,9},{14,10},{15,11},{20,16},{21,... | collective-permute-start | bytes 1179656 | tf_op jit(solution)/shard_map/ppermute | solution.py:15
  84.6 50.2 %reduce-scatter.15.cloned.1.call-start = ((), (), s32[]{:S(2)}) async-start(), calls=%async_computation.5 | async-start | bytes 491520
  84.6 14.2 %copy-start.7 = (bf16[1024,384]{1,0:T(8,128)(2,1)S(1)}, bf16[1024,384]{1,0:T(8,128)(2,1)}, u32[]{:S(2)}) copy-start(bf16[1024,384]{1,0:T(8,128)(2,1)} %copy-done.6) | copy-start | bytes 2359300
  84.6 14.2 %copy-start.17 = (bf16[1,1024,384]{2,1,0:T(8,128)(2,1)S(1)}, bf16[1,1024,384]{2,1,0:T(8,128)(2,1)}, u32[]{:S(2)}) copy-start(bf16[1,1024,384]{2,1,0:T(8,128)(2,1)} %param.7) | copy-start | bytes 2359300
  98.8 3.4 %copy-start.10 = (f32[1024,192]{0,1:T(8,128)S(1)}, f32[1024,192]{0,1:T(8,128)}, u32[]{:S(2)}) copy-start(f32[1024,192]{0,1:T(8,128)} %copy-done.9) | copy-start | bytes 2359300
  101.3 0.9 copy-start.19
  102.2 1.6 copy-start.8
  103.5 58.4 %reduce-scatter.17.cloned.1.call-start = ((), (), s32[]{:S(2)}) async-start(), calls=%async_computation.6 | async-start | bytes 1228800
  105.5 1.0 copy-start.13
  109.2 79.8 %reduce-scatter.13.cloned.1.call-start = ((), (), s32[]{:S(2)}) async-start(), calls=%async_computation.4 | async-start | bytes 1228800
  111.4 7.9 %collective-permute-start.7 = (bf16[1,1024,192]{1,2,0:T(8,128)(2,1)S(1)}, bf16[1,1024,192]{1,2,0:T(8,128)(2,1)S(1)}, u32[]{:S(2)}, u32[]{:S(2)}) collective-permute-start(bf16[1,1024,192]{1,2,0:T(8,128)(2,1)S(1)} %bitcast.176), channel_id=1, source_target_pairs={{0,2},{1,3},{2,4},{3,5},{4,6},{5,7},{8,10},{9,11},{10,12},{11,13},... | collective-permute-start | bytes 1179656 | tf_op jit(solution)/shard_map/ppermute | solution.py:15
  112.7 10.8 %collective-permute-start.6 = (bf16[1,1024,192]{1,2,0:T(8,128)(2,1)S(1)}, bf16[1,1024,192]{1,2,0:T(8,128)(2,1)S(1)}, u32[]{:S(2)}, u32[]{:S(2)}) collective-permute-start(bf16[1,1024,192]{1,2,0:T(8,128)(2,1)S(1)} %bitcast.177), channel_id=1, source_target_pairs={{2,0},{3,1},{4,2},{5,3},{6,4},{7,5},{10,8},{11,9},{12,10},{13,11},... | collective-permute-start | bytes 1179656 | tf_op jit(solution)/shard_map/ppermute | solution.py:15
  119.3 4.1 %copy-start.11 = (bf16[1,1024,192]{1,2,0:T(8,128)(2,1)}, bf16[1,1024,192]{1,2,0:T(8,128)(2,1)S(1)}, u32[]{:S(2)}) copy-start(bf16[1,1024,192]{1,2,0:T(8,128)(2,1)S(1)} %collective-permute-done.7) | copy-start | bytes 1179652
  124.8 1.8 copy-start.2
  126.6 141.8 %all-reduce.3.cloned.1.call-start = ((), (), s32[]{:S(2)}) async-start(), calls=%async_computation.8 | async-start | bytes 1572864 | tf_op jit(solution)/shard_map/psum | solution.py:97
  191.1 1.0 copy-start.12
  191.1 1.2 copy-start.5
  191.1 1.5 copy-start.20
  268.3 2.9 %copy-start.14 = (f32[192,96]{1,0:T(8,128)S(1)}, f32[192,96]{1,0:T(8,128)}, u32[]{:S(2)}) copy-start(f32[192,96]{1,0:T(8,128)} %get-tuple-element.16) | copy-start | bytes 221188
  268.3 2.9 %copy-start.15 = (f32[192,96]{1,0:T(8,128)S(1)}, f32[192,96]{1,0:T(8,128)}, u32[]{:S(2)}) copy-start(f32[192,96]{1,0:T(8,128)} %get-tuple-element.18) | copy-start | bytes 221188
Sparse Core Ops, SparseCore 0:
  84.7 26.7 reduce-scatter.18
  113.9 20.7 reduce-scatter.14
  137.4 24.4 reduce-scatter.16
  164.5 24.4 reduce-scatter.12
  193.2 75.1 all-reduce.2
where the time goes:
time: 279 us; the launch traced here: 278 us
  waiting for transfers between devices  199 us (71%)
  matrix products  23.6 us (8%)
  starting transfers between devices  20.3 us (7%)
  local copies, waits for them, and re-layouts  17.1 us (6%)
  between operations  14.2 us (5%)
  other arithmetic  4.26 us (2%)
    psum x1, waiting for transfers between devices, reduce_weights(): whole_conv, whole_point = lax.psum((conv_sum, point_sum), 'seq')  73.5 us
    ppermute x8, waiting for transfers between devices, passed_along(): return lax.ppermute(block, axis, route)  68.7 us
    unnamed x9, waiting for transfers between devices  56.7 us
    dot_general x21, matrix products, matmul(): return jnp.dot(left, right, preferred_element_type=jnp.float32)  20.9 us
    ppermute x8, starting transfers between devices, passed_along(): return lax.ppermute(block, axis, route)  19.9 us
    unnamed x54, local copies, waits for them, and re-layouts  17.1 us
  transfers between devices with their start and end apart: 13, of which 10 were waited for; matrix products, arithmetic and copies ran while one was open for 11% of the time, Pallas kernels for 0%

commit v1 on v0

v1 whole, which is shorter than its diff:
```python
import functools
import math

import jax
import jax.numpy as jnp
from jax import lax
from jax.experimental import pallas as pl
from jax.experimental.pallas import tpu as pltpu
from jax.sharding import PartitionSpec as P

DILATION_ONE = 2048
DILATION_TWO = 4096
TILE = 256
CHUNK = 32
MAX_PERMUTES = 8
BF16 = jnp.bfloat16
F32 = jnp.float32


def gelu_parts(values):
    coeff = math.sqrt(2.0 / math.pi)
    square = values * values
    tanh_val = jnp.tanh(values * (coeff + (coeff * 0.044715) * square))
    half = 0.5 + 0.5 * tanh_val
    slope = half + half * (1.0 - tanh_val) * (values * (coeff + (3.0 * coeff * 0.044715) * square))
    return values * half, slope


def dot(left, right):
    return jnp.dot(left, right, preferred_element_type=F32)


def dot_nt(left, right):
    return lax.dot_general(left, right, (((1,), (1,)), ((), ())), preferred_element_type=F32)


def position(hop):
    return lax.axis_index("seq") // hop


def place(parts, rows_ref, hop):
    if len(parts) == 1:
        rows_ref[...] = parts[0][...]
        return
    count = len(parts)
    size = rows_ref.shape[0] // count
    me = position(hop)
    for k, part in enumerate(parts):
        at = lax.rem(me + (count - k), count)
        rows_ref[pl.ds(pl.multiple_of(at * size, size), size), :] = part[...]


def hand_out(rows_ref, parts, hop):
    if len(parts) == 1:
        parts[0][...] = rows_ref[...]
        return
    count = len(parts)
    size = rows_ref.shape[0] // count
    me = position(hop)
    for k, part in enumerate(parts):
        at = lax.rem(me + k, count)
        part[...] = rows_ref[pl.ds(pl.multiple_of(at * size, size), size), :]


def tap_sum(padded_ref, shift, start, weight_of, mm):
    total = mm(padded_ref[pl.ds(start + shift, TILE), :], weight_of(1))
    rows = padded_ref.shape[0] - 2 * shift
    if start + TILE > shift:
        total = total + mm(padded_ref[pl.ds(start, TILE), :], weight_of(0))
    if start < rows - shift:
        total = total + mm(padded_ref[pl.ds(start + 2 * shift, TILE), :], weight_of(2))
    return total


def clear_edges(padded_ref, shift):
    rows = padded_ref.shape[0]
    zeros = jnp.zeros((shift, padded_ref.shape[1]), padded_ref.dtype)
    padded_ref[pl.ds(0, shift), :] = zeros
    padded_ref[pl.ds(rows - shift, shift), :] = zeros


def forward_kernel(shifts, hop, count, *refs):
    parts = refs[:count]
    k1t, p1, k2t = refs[count : count + 3]
    outs = refs[count + 3 : count + 11]
    act1_t, mid1_t, s_x, s_p1, act2_t, mid2_t, s_h, s_p2 = outs
    x_rows, pad1, pad2, wide, narrow = refs[count + 11 :]
    rows = x_rows.shape[0]
    place(parts, x_rows, hop)

    def activate(source, source_start, pad, shift, start, slope_ref):
        def step(i, carry):
            at = pl.multiple_of(i * CHUNK, CHUNK)
            value, slope = gelu_parts(
                source[pl.ds(source_start + at, CHUNK), :].astype(F32)
            )
            pad[pl.ds(start + shift + at, CHUNK), :] = value.astype(BF16)
            slope_ref[pl.ds(start + at, CHUNK), :] = slope
            return carry

        lax.fori_loop(0, TILE // CHUNK, step, 0, unroll=2)

    def narrow_gelu(start, slope_ref):
        def step(i, carry):
            at = pl.multiple_of(i * CHUNK, CHUNK)
            value, slope = gelu_parts(narrow[pl.ds(at, CHUNK), :])
            narrow[pl.ds(at, CHUNK), :] = value
            slope_ref[pl.ds(start + at, CHUNK), :] = slope
            return carry

        lax.fori_loop(0, TILE // CHUNK, step, 0, unroll=2)

    clear_edges(pad1, shifts[0])
    clear_edges(pad2, shifts[1])
    for start in range(0, rows, TILE):
        activate(x_rows, start, pad1, shifts[0], start, s_x)
        act1_t[:, pl.ds(start, TILE)] = pad1[pl.ds(start + shifts[0], TILE), :].T
    for start in range(0, rows, TILE):
        narrow[...] = tap_sum(pad1, shifts[0], start, lambda k: k1t[k], dot_nt)
        narrow_gelu(start, s_p1)
        mid = narrow[...].astype(BF16)
        mid1_t[:, pl.ds(start, TILE)] = mid.T
        wide[...] = (x_rows[pl.ds(start, TILE), :].astype(F32) + dot(mid, p1[...])).astype(BF16)
        activate(wide, 0, pad2, shifts[1], start, s_h)
        act2_t[:, pl.ds(start, TILE)] = pad2[pl.ds(start + shifts[1], TILE), :].T
    for start in range(0, rows, TILE):
        narrow[...] = tap_sum(pad2, shifts[1], start, lambda k: k2t[k], dot_nt)
        narrow_gelu(start, s_p2)
        mid2_t[:, pl.ds(start, TILE)] = narrow[...].astype(BF16).T


def backward_kernel(shift, hop, n_in, n_out, *refs):
    parts = refs[:n_in]
    act_t, mid_t, s_state, s_pre, kt, point = refs[n_in : n_in + 6]
    outs = refs[n_in + 6 : n_in + 6 + n_out]
    keep, send = refs[n_in + 6 + n_out : n_in + 8 + n_out]
    g_rows, pad, grads, x_rows = refs[n_in + 8 + n_out :]
    rows = g_rows.shape[0]
    place(parts, g_rows, hop)
    clear_edges(pad, shift)
    for start in range(0, rows, TILE):
        mid_grad = dot_nt(g_rows[pl.ds(start, TILE), :], point[...])
        pad[pl.ds(start + shift, TILE), :] = (mid_grad * s_pre[pl.ds(start, TILE), :]).astype(BF16)
    for start in range(0, rows, TILE):
        act_grad = tap_sum(pad, shift, start, lambda k: kt[2 - k], dot)
        x_rows[pl.ds(start, TILE), :] = (
            g_rows[pl.ds(start, TILE), :].astype(F32) + act_grad * s_state[pl.ds(start, TILE), :]
        ).astype(BF16)
    hand_out(x_rows, outs, hop)
    act = act_t[...]
    grads[...] = jnp.concatenate(
        [
            dot(act, pad[pl.ds(2 * shift, rows), :]),
            dot(act, pad[pl.ds(shift, rows), :]),
            dot(act, pad[pl.ds(0, rows), :]),
            dot(mid_t[...], g_rows[...]).T,
        ],
        axis=1,
    )
    size = keep.shape[1]
    core = lax.rem(lax.axis_index("dp"), 2)
    for half in range(2):
        for target, parity in ((keep, core), (send, 1 - core)):
            at = pl.multiple_of((2 * half + parity) * size, size)
            target[half] = grads[pl.ds(at, size), :].astype(BF16)


def split_kernel(keep, received, *pieces):
    x_at = lax.axis_index("dp") // 2
    y_at = lax.rem(lax.axis_index("seq"), 2)
    size = pieces[0].shape[0]
    for k, piece in enumerate(pieces):
        x_to = lax.rem(x_at + k // 2, 2)
        rows = pl.ds(pl.multiple_of(lax.rem(y_at + k, 2) * size, size), size)
        piece[...] = (keep[x_to, rows, :].astype(F32) + received[x_to, rows, :].astype(F32)).astype(BF16)


def sum_kernel(*refs):
    total = refs[0][...].astype(F32)
    for ref in refs[1:-1]:
        total = total + ref[...].astype(F32)
    refs[-1][...] = total.astype(BF16)


def ordered_sum_kernel(hop, *refs):
    *parts, out, held = refs
    count = len(parts)
    me = position(hop)
    for k, part in enumerate(parts):
        held[lax.rem(me + (count - k), count)] = part[...]
    total = held[0].astype(F32)
    for k in range(1, count):
        total = total + held[k].astype(F32)
    out[...] = total.astype(BF16)


def finish_kernel(scale, own, other, conv, point, rows):
    y_at = lax.rem(lax.axis_index("seq"), 2)
    size = own.shape[0]
    rows[pl.ds(pl.multiple_of(y_at * size, size), size), :] = own[...].astype(F32) * scale
    rows[pl.ds(pl.multiple_of((1 - y_at) * size, size), size), :] = other[...].astype(F32) * scale
    width = conv.shape[2]
    whole = rows[...]
    for k in range(3):
        conv[k] = whole[:, k * width : (k + 1) * width]
    point[...] = whole[:, 3 * width :].T


def call(kernel, out_shapes, scratch, *args):
    vmem = pl.BlockSpec(memory_space=pltpu.VMEM)
    return pl.pallas_call(
        kernel,
        out_shape=[jax.ShapeDtypeStruct(s, d) for s, d in out_shapes],
        in_specs=[vmem] * len(args),
        out_specs=[vmem] * len(out_shapes),
        scratch_shapes=[pltpu.VMEM(s, d) for s, d in scratch],
        compiler_params=pltpu.CompilerParams(vmem_limit_bytes=48 << 20),
    )(*args)


def send_ahead(block, hop, k):
    size = lax.axis_size("seq")
    count = size // hop
    route = [(i, ((i // hop + k) % count) * hop + i % hop) for i in range(size)]
    return lax.ppermute(block, "seq", route)


def mirrored(block, dp_bits, seq_bits):
    n_dp, n_seq = lax.axis_size("dp"), lax.axis_size("seq")
    route = [
        (i * n_seq + j, (i ^ dp_bits) * n_seq + (j ^ seq_bits))
        for i in range(n_dp)
        for j in range(n_seq)
    ]
    return lax.ppermute(block, ("dp", "seq"), route)


def column_groups(hop):
    size = lax.axis_size("seq")
    return [list(range(first, size, hop)) for first in range(hop)]


def exchange_all(block, hop):
    count = lax.axis_size("seq") // hop
    cut = block.reshape(count, -1, block.shape[-1])
    swapped = lax.all_to_all(
        cut, "seq", 0, 0, axis_index_groups=column_groups(hop), tiled=True
    )
    return swapped.reshape(block.shape)


def to_columns(block, hop):
    count = lax.axis_size("seq") // hop
    if count > MAX_PERMUTES:
        return [exchange_all(block, hop)]
    size = block.shape[0] // count
    me = position(hop)
    pieces = [
        lax.dynamic_slice_in_dim(block, ((me + k) % count) * size, size, 0) for k in range(count)
    ]
    return [pieces[0]] + [send_ahead(pieces[k], hop, k) for k in range(1, count)]


def from_columns(parts, hop):
    if len(parts) == 1:
        return [exchange_all(parts[0], hop)]
    return [parts[0]] + [send_ahead(parts[k], hop, k) for k in range(1, len(parts))]


def collect_kernel(hop, *refs):
    place(refs[:-1], refs[-1], hop)


def reduce_weights(keep, send, hop, scale):
    half, rows, lanes = keep.shape
    width = lanes // 4
    received = mirrored(send, 1, 0)
    piece = ((rows // 2, lanes), BF16)
    pieces = call(split_kernel, [piece] * 4, [], keep, received)
    arrived = [pieces[0]] + [
        mirrored(pieces[k], 2 * (k // 2), k % 2) for k in range(1, 4)
    ]
    (plane,) = call(sum_kernel, [piece], [], *arrived)
    count = lax.axis_size("seq") // hop
    if count > MAX_PERMUTES:
        own = lax.psum(plane.astype(F32), "seq", axis_index_groups=column_groups(hop)).astype(BF16)
    else:
        column = [plane] + [send_ahead(plane, hop, k) for k in range(1, count)]
        (own,) = call(
            functools.partial(ordered_sum_kernel, hop),
            [piece],
            [((count, rows // 2, lanes), BF16)],
            *column,
        )
    other = mirrored(own, 0, 1)
    return call(
        functools.partial(finish_kernel, scale),
        [((3, rows, width), F32), ((width, rows), F32)],
        [((rows, lanes), F32)],
        own,
        other,
    )


def shards(
    inputs,
    cotangent,
    first_dilated_kernel,
    first_pointwise_weight,
    second_dilated_kernel,
    second_pointwise_weight,
):
    samples, rows, channels = inputs.shape
    width = first_pointwise_weight.shape[0]
    hop = DILATION_ONE // rows
    count = lax.axis_size("seq") // hop
    size = rows // count
    shifts = (size, size * (DILATION_TWO // DILATION_ONE))
    total_rows = samples * lax.axis_size("dp") * rows * lax.axis_size("seq")
    scale = 1.0 / math.sqrt(total_rows)
    k1t = jnp.swapaxes(first_dilated_kernel, 1, 2)
    k2t = jnp.swapaxes(second_dilated_kernel, 1, 2)

    x_parts = to_columns(inputs.reshape(rows, channels), hop)
    g_parts = to_columns(cotangent.reshape(rows, channels), hop)
    state = [
        ((channels, rows), BF16),
        ((width, rows), BF16),
        ((rows, channels), F32),
        ((rows, width), F32),
    ]
    saved = call(
        functools.partial(forward_kernel, shifts, hop, len(x_parts)),
        state * 2,
        [
            ((rows, channels), BF16),
            ((rows + 2 * shifts[0], channels), BF16),
            ((rows + 2 * shifts[1], channels), BF16),
            ((TILE, channels), BF16),
            ((TILE, width), F32),
        ],
        *x_parts,
        k1t,
        first_pointwise_weight,
        k2t,
    )
    part_shape = (x_parts[0].shape, BF16)
    whole_shape = ((rows, channels), BF16)

    def backward(g_in, saved, shift, kt, point, out_shapes):
        act_t, mid_t, s_state, s_pre = saved
        quarter = ((2, channels // 4, 4 * width), BF16)
        *outs, keep, send = call(
            functools.partial(backward_kernel, shift, hop, len(g_in), len(out_shapes)),
            out_shapes + [quarter, quarter],
            [
                whole_shape,
                ((rows + 2 * shift, width), BF16),
                ((channels, 4 * width), F32),
                whole_shape,
            ],
            *g_in,
            act_t,
            mid_t,
            s_state,
            s_pre,
            kt,
            point,
        )
        return outs, keep, send

    hidden_grad, keep2, send2 = backward(
        g_parts, saved[4:], shifts[1], k2t, second_pointwise_weight, [whole_shape]
    )
    conv2, point2 = reduce_weights(keep2, send2, hop, scale)
    x_grads, keep1, send1 = backward(
        hidden_grad, saved[:4], shifts[0], k1t, first_pointwise_weight, [part_shape] * len(x_parts)
    )
    conv1, point1 = reduce_weights(keep1, send1, hop, scale)
    back = from_columns(x_grads, hop)
    (input_grad,) = call(functools.partial(collect_kernel, hop), [whole_shape], [], *back)
    return input_grad.reshape(inputs.shape), conv1, point1, conv2, point2


def solution(mesh):
    return jax.shard_map(
        shards,
        mesh=mesh,
        in_specs=(P("dp", "seq", None), P("dp", "seq", None), P(), P(), P(), P()),
        out_specs=(
            P("dp", "seq", None),
            P(None, "dp", None),
            P(None, "dp"),
            P(None, "dp", None),
            P(None, "dp"),
        ),
        check_vma=False,
    )
```

time: 279 us -> 98.8 us (0.35)
  waiting for transfers between devices: 199 us -> 41.3 us
  matrix products: 23.6 us -> 0 us
  Pallas kernels: 0 us -> 21.4 us
  local copies, waits for them, and re-layouts: 17.1 us -> 2.73 us
  between operations: 14.2 us -> 0.86 us
  starting transfers between devices: 20.3 us -> 32.3 us
  other arithmetic: 4.26 us -> 0 us
    psum x1 -> x0, waiting for transfers between devices: 73.5 us -> none  [reduce_weights(): whole_conv, whole_point = lax.psum((conv_sum, point_sum), 'seq')]
    unnamed x9 -> x0, waiting for transfers between devices: 56.7 us -> none
    ppermute x8 -> x25, waiting for transfers between devices: 68.7 us -> 41.3 us  [the longest x15 37 us: send_ahead(): return lax.ppermute(block, 'seq', route)]
    pallas_call x0 -> x12, Pallas kernels: none -> 21.4 us  [call(): pl.pallas_call(kernel, out_shape=[jax.ShapeDtypeStruct(s, d) for s, d in...]
    dot_general x21 -> x0, matrix products: 20.9 us -> none  [matmul(): return jnp.dot(left, right, preferred_element_type=jnp.float32)]
    unnamed x54 -> x12, local copies, waits for them, and re-layouts: 17.1 us -> 1.25 us
    ppermute x8 -> x25, starting transfers between devices: 19.9 us -> 32.3 us  [the longest x15 22.6 us: send_ahead(): return lax.ppermute(block, 'seq', route)]
  transfers between devices with their start and end apart: 13 -> 25, of which waited for: 10 -> 10; matrix products, arithmetic and copies ran while one was open for 11% -> 0% of each run, Pallas kernels for 0% -> 13%
where the time goes in v1:
time: 98.8 us; the launch traced here: 98.6 us
  waiting for transfers between devices  41.3 us (42%)
  starting transfers between devices  32.3 us (33%)
  Pallas kernels  21.4 us (22%)
  local copies, waits for them, and re-layouts  2.73 us (3%)
    ppermute x15, waiting for transfers between devices, send_ahead(): return lax.ppermute(block, 'seq', route)  37 us
    ppermute x15, starting transfers between devices, send_ahead(): return lax.ppermute(block, 'seq', route)  22.6 us
    pallas_call x12, Pallas kernels, call(): pl.pallas_call(kernel, out_shape=[jax.ShapeDtypeStruct(s, d) for s, d in...  21.4 us
    ppermute x10, starting transfers between devices, mirrored(): return lax.ppermute(block, ('dp', 'seq'), route)  9.77 us
    ppermute x10, waiting for transfers between devices, mirrored(): return lax.ppermute(block, ('dp', 'seq'), route)  4.3 us
  transfers between devices with their start and end apart: 25, of which 10 were waited for; matrix products, arithmetic and copies ran while one was open for 0% of the time, Pallas kernels for 13%

profile of v1, /device:TPU:0, one launch (start us, length us, event | category | flops | bytes accessed | tf_op | source)
XLA Modules:
  0.0 98.6 jit_solution(17837627029386339432)
XLA Ops:
  0.8 1.4 %dynamic-slice_bitcast_fusion = (bf16[256,384]{1,0:T(8,128)(2,1)S(1)}, bf16[256,384]{1,0:T(8,128)(2,1)S(1)}, bf16[256,384]{1,0:T(8,128)(2,1)S(1)}, bf16[256,384]{1,0:T(8,128)(2,1)S(1)}) fusion(bf16[1,1024,384]{2,1,0:T(8,128)(2,1)} %param.6, s32[]{:T(128)S(6)} %select_n.56, s32[]{:T(128)S(6)} %select_n.52, s32[]{:T(128)S(6)} %select_n.50, s32[]{:T(128)S(6)} %select_n.54), kind=kLoop, calls=%fused_computation | loop fusion | bytes 1572880 | tf_op jit(solution)/shard_map/dynamic_slice | solution.py:259
  2.2 5.1 %collective-permute-start.5 = (bf16[256,384]{1,0:T(8,128)(2,1)S(1)}, bf16[256,384]{1,0:T(8,128)(2,1)S(1)}, u32[]{:S(2)}, u32[]{:S(2)}) collective-permute-start(bf16[256,384]{1,0:T(8,128)(2,1)S(1)} %get-tuple-element.63), channel_id=1, source_target_pairs={{0,6},{1,7},{2,0},{3,1},{4,2},{5,3},{6,4},{7,5},{8,14},{9,15},{10,... | collective-permute-start | bytes 589832 | tf_op jit(solution)/shard_map/ppermute | solution.py:225
  7.3 0.0 collective-permute-start.3
  7.3 1.0 %collective-permute-start.4 = (bf16[256,384]{1,0:T(8,128)(2,1)S(1)}, bf16[256,384]{1,0:T(8,128)(2,1)S(1)}, u32[]{:S(2)}, u32[]{:S(2)}) collective-permute-start(bf16[256,384]{1,0:T(8,128)(2,1)S(1)} %get-tuple-element.66), channel_id=1, source_target_pairs={{0,4},{1,5},{2,6},{3,7},{4,0},{5,1},{6,2},{7,3},{8,12},{9,13},{10,... | collective-permute-start | bytes 589832 | tf_op jit(solution)/shard_map/ppermute | solution.py:225
  8.3 0.1 dynamic-slice_bitcast_fusion.4
  8.4 2.9 %collective-permute-start.2 = (bf16[256,384]{1,0:T(8,128)(2,1)S(1)}, bf16[256,384]{1,0:T(8,128)(2,1)S(1)}, u32[]{:S(2)}, u32[]{:S(2)}) collective-permute-start(bf16[256,384]{1,0:T(8,128)(2,1)S(1)} %get-tuple-element.67), channel_id=1, source_target_pairs={{0,6},{1,7},{2,0},{3,1},{4,2},{5,3},{6,4},{7,5},{8,14},{9,15},{10,... | collective-permute-start | bytes 589832 | tf_op jit(solution)/shard_map/ppermute | solution.py:225
  11.3 0.6 collective-permute-start
  11.9 0.7 collective-permute-done.5.refs_3_
  12.6 1.4 %collective-permute-start.1 = (bf16[256,384]{1,0:T(8,128)(2,1)S(1)}, bf16[256,384]{1,0:T(8,128)(2,1)S(1)}, u32[]{:S(2)}, u32[]{:S(2)}) collective-permute-start(bf16[256,384]{1,0:T(8,128)(2,1)S(1)} %get-tuple-element.70), channel_id=1, source_target_pairs={{0,4},{1,5},{2,6},{3,7},{4,0},{5,1},{6,2},{7,3},{8,12},{9,13},{10,... | collective-permute-start | bytes 589832 | tf_op jit(solution)/shard_map/ppermute | solution.py:225
  14.0 3.7 %collective-permute-done.3.refs_1_ = bf16[256,384]{1,0:T(8,128)(2,1)S(1)} collective-permute-done((bf16[256,384]{1,0:T(8,128)(2,1)S(1)}, bf16[256,384]{1,0:T(8,128)(2,1)S(1)}, u32[]{:S(2)}, u32[]{:S(2)}) %collective-permute-start.3) | collective-permute-done | bytes 196640 | tf_op jit(solution)/shard_map/ppermute | solution.py:225
  17.7 8.1 %collective-permute-done.4.refs_2_ = bf16[256,384]{1,0:T(8,128)(2,1)S(1)} collective-permute-done((bf16[256,384]{1,0:T(8,128)(2,1)S(1)}, bf16[256,384]{1,0:T(8,128)(2,1)S(1)}, u32[]{:S(2)}, u32[]{:S(2)}) %collective-permute-start.4) | collective-permute-done | bytes 196640 | tf_op jit(solution)/shard_map/ppermute | solution.py:225
  25.8 0.0 copy-done.3
  25.8 10.5 %shard_map.101 = (bf16[384,1024]{1,0:T(8,128)(2,1)S(1)}, bf16[192,1024]{1,0:T(8,128)(2,1)S(1)}, f32[1024,384]{1,0:T(8,128)}, f32[1024,192]{1,0:T(8,128)S(1)}, bf...) custom-call(bf16[256,384]{1,0:T(8,128)(2,1)S(1)} %get-tuple-element.65.r, ...), custom_call_target="tpu_custom_call" | custom-call | tf_op jit(solution)/shard_map/pallas_call | solution.py:211
  36.4 0.0 collective-permute-done.2.refs_3_
  36.4 0.0 collective-permute-done.refs_1_
  36.4 4.4 %collective-permute-done.1.refs_2_ = bf16[256,384]{1,0:T(8,128)(2,1)S(1)} collective-permute-done((bf16[256,384]{1,0:T(8,128)(2,1)S(1)}, bf16[256,384]{1,0:T(8,128)(2,1)S(1)}, u32[]{:S(2)}, u32[]{:S(2)}) %collective-permute-start.1) | collective-permute-done | bytes 196640 | tf_op jit(solution)/shard_map/ppermute | solution.py:225
  40.8 1.2 %copy-done.2 = f32[1024,192]{1,0:T(8,128)S(1)} copy-done((f32[1024,192]{1,0:T(8,128)S(1)}, f32[1024,192]{1,0:T(8,128)}, u32[]{:S(2)}) %copy-start.2) | copy-done | bytes 786456
  42.1 3.8 %shard_map.102 = (bf16[1024,384]{1,0:T(8,128)(2,1)S(1)}, bf16[2,96,768]{2,1,0:T(8,128)(2,1)S(1)}, bf16[2,96,768]{2,1,0:T(8,128)(2,1)S(1)}) custom-call(bf16[256,384]{1,0:T(8,128)(2,1)S(1)} %get-tuple-element.69.refs_0_, bf16[256,384]{1,0:T(8,128)(2,1)S(1)} %collective-permute-done.refs_1_, bf16[256,384]{1,0:T(8,128)(2,1)S(1)} %collective-permute-done.1.refs_2_, ...), custom_call_target="tpu_custom_call" | custom-call | tf_op jit(solution)/shard_map/pallas_call | solution.py:211
  45.8 3.9 %shard_map.103 = (bf16[256,384]{1,0:T(8,128)(2,1)S(1)}, bf16[256,384]{1,0:T(8,128)(2,1)S(1)}, bf16[256,384]{1,0:T(8,128)(2,1)S(1)}, bf16[256,384]{1,0:T(8,128)(2...) custom-call(bf16[1024,384]{1,0:T(8,128)(2,1)S(1)} %get-tuple-element.38.refs_0_, ...), custom_call_target="tpu_custom_call" | custom-call | tf_op jit(solution)/shard_map/pallas_call | solution.py:211
  49.7 0.1 collective-permute-start.9
  49.8 0.5 collective-permute-start.17
  50.3 1.1 %collective-permute-done.9.received = bf16[2,96,768]{2,1,0:T(8,128)(2,1)S(1)} collective-permute-done((bf16[2,96,768]{2,1,0:T(8,128)(2,1)S(1)}, bf16[2,96,768]{2,1,0:T(8,128)(2,1)S(1)}, u32[]{:S(2)}, u32[]{:S(2)}) %collective-permute-start.9) | collective-permute-done | bytes 294944 | tf_op jit(solution)/shard_map/ppermute | solution.py:235
  51.3 0.1 shard_map.105
  51.4 1.6 %collective-permute-start.10 = (bf16[48,768]{1,0:T(8,128)(2,1)S(1)}, bf16[48,768]{1,0:T(8,128)(2,1)S(1)}, u32[]{:S(2)}, u32[]{:S(2)}) collective-permute-start(bf16[48,768]{1,0:T(8,128)(2,1)S(1)} %get-tuple-element.50), channel_id=1, source_target_pairs={{0,1},{1,0},{2,3},{3,2},{4,5},{5,4},{6,7},{7,6},{8,9},{9,8},{10,11... | collective-permute-start | bytes 221192 | tf_op jit(solution)/shard_map/ppermute | solution.py:235
  53.0 1.5 %collective-permute-start.11 = (bf16[48,768]{1,0:T(8,128)(2,1)S(1)}, bf16[48,768]{1,0:T(8,128)(2,1)S(1)}, u32[]{:S(2)}, u32[]{:S(2)}) collective-permute-start(bf16[48,768]{1,0:T(8,128)(2,1)S(1)} %get-tuple-element.51), channel_id=1, source_target_pairs={{0,16},{1,17},{2,18},{3,19},{4,20},{5,21},{6,22},{7,23},{8,24},{9,... | collective-permute-start | bytes 221192 | tf_op jit(solution)/shard_map/ppermute | solution.py:235
  54.5 0.5 collective-permute-start.12
  55.0 0.0 collective-permute-done.17.received
  55.0 0.1 shard_map.109
  55.0 1.6 %collective-permute-start.18 = (bf16[48,768]{1,0:T(8,128)(2,1)S(1)}, bf16[48,768]{1,0:T(8,128)(2,1)S(1)}, u32[]{:S(2)}, u32[]{:S(2)}) collective-permute-start(bf16[48,768]{1,0:T(8,128)(2,1)S(1)} %get-tuple-element.58), channel_id=1, source_target_pairs={{0,1},{1,0},{2,3},{3,2},{4,5},{5,4},{6,7},{7,6},{8,9},{9,8},{10,11... | collective-permute-start | bytes 221192 | tf_op jit(solution)/shard_map/ppermute | solution.py:235
  56.6 1.5 %collective-permute-start.19 = (bf16[48,768]{1,0:T(8,128)(2,1)S(1)}, bf16[48,768]{1,0:T(8,128)(2,1)S(1)}, u32[]{:S(2)}, u32[]{:S(2)}) collective-permute-start(bf16[48,768]{1,0:T(8,128)(2,1)S(1)} %get-tuple-element.59), channel_id=1, source_target_pairs={{0,16},{1,17},{2,18},{3,19},{4,20},{5,21},{6,22},{7,23},{8,24},{9,... | collective-permute-start | bytes 221192 | tf_op jit(solution)/shard_map/ppermute | solution.py:235
  58.1 0.0 collective-permute-done.10.refs_1_
  58.1 0.5 collective-permute-start.20
  58.6 0.0 collective-permute-done.11.refs_2_
  58.6 1.4 %collective-permute-done.12.refs_3_ = bf16[48,768]{1,0:T(8,128)(2,1)S(1)} collective-permute-done((bf16[48,768]{1,0:T(8,128)(2,1)S(1)}, bf16[48,768]{1,0:T(8,128)(2,1)S(1)}, u32[]{:S(2)}, u32[]{:S(2)}) %collective-permute-start.12) | collective-permute-done | bytes 73760 | tf_op jit(solution)/shard_map/ppermute | solution.py:235
  60.1 2.9 %collective-permute-start.15 = (bf16[48,768]{1,0:T(8,128)(2,1)S(1)}, bf16[48,768]{1,0:T(8,128)(2,1)S(1)}, u32[]{:S(2)}, u32[]{:S(2)}) collective-permute-start(bf16[48,768]{1,0:T(8,128)(2,1)S(1)} %shard_map.106.refs_0_), channel_id=1, source_target_pairs={{0,6},{1,7},{2,0},{3,1},{4,2},{5,3},{6,4},{7,5},{8,14},{9,15},{10,... | collective-permute-start | bytes 221192 | tf_op jit(solution)/shard_map/ppermute | solution.py:225
  62.9 0.0 collective-permute-start.14
  62.9 0.0 collective-permute-done.18.refs_1_
  62.9 0.6 collective-permute-start.13
  63.6 0.0 collective-permute-done.19.refs_2_
  63.6 0.0 collective-permute-done.20.refs_3_
  63.6 3.2 %collective-permute-start.23 = (bf16[48,768]{1,0:T(8,128)(2,1)S(1)}, bf16[48,768]{1,0:T(8,128)(2,1)S(1)}, u32[]{:S(2)}, u32[]{:S(2)}) collective-permute-start(bf16[48,768]{1,0:T(8,128)(2,1)S(1)} %shard_map.110.refs_0_), channel_id=1, source_target_pairs={{0,6},{1,7},{2,0},{3,1},{4,2},{5,3},{6,4},{7,5},{8,14},{9,15},{10,... | collective-permute-start | bytes 221192 | tf_op jit(solution)/shard_map/ppermute | solution.py:225
  66.9 0.0 collective-permute-start.6
  66.9 0.0 collective-permute-done.15.refs_3_
  66.9 1.1 %collective-permute-start.7 = (bf16[256,384]{1,0:T(8,128)(2,1)S(1)}, bf16[256,384]{1,0:T(8,128)(2,1)S(1)}, u32[]{:S(2)}, u32[]{:S(2)}) collective-permute-start(bf16[256,384]{1,0:T(8,128)(2,1)S(1)} %get-tuple-element.45), channel_id=1, source_target_pairs={{0,4},{1,5},{2,6},{3,7},{4,0},{5,1},{6,2},{7,3},{8,12},{9,13},{10,... | collective-permute-start | bytes 589832 | tf_op jit(solution)/shard_map/ppermute | solution.py:225
  68.0 8.0 %collective-permute-done.14.refs_2_ = bf16[48,768]{1,0:T(8,128)(2,1)S(1)} collective-permute-done((bf16[48,768]{1,0:T(8,128)(2,1)S(1)}, bf16[48,768]{1,0:T(8,128)(2,1)S(1)}, u32[]{:S(2)}, u32[]{:S(2)}) %collective-permute-start.14) | collective-permute-done | bytes 73760 | tf_op jit(solution)/shard_map/ppermute | solution.py:225
  76.1 0.0 collective-permute-start.8
  76.1 0.0 collective-permute-done.13.refs_1_
  76.1 0.0 collective-permute-start.22
  76.1 0.0 collective-permute-done.23.refs_3_
  76.1 3.7 %collective-permute-start.21 = (bf16[48,768]{1,0:T(8,128)(2,1)S(1)}, bf16[48,768]{1,0:T(8,128)(2,1)S(1)}, u32[]{:S(2)}, u32[]{:S(2)}) collective-permute-start(bf16[48,768]{1,0:T(8,128)(2,1)S(1)} %shard_map.110.refs_0_), channel_id=1, source_target_pairs={{0,2},{1,3},{2,4},{3,5},{4,6},{5,7},{6,0},{7,1},{8,10},{9,11},{10,... | collective-permute-start | bytes 221192 | tf_op jit(solution)/shard_map/ppermute | solution.py:225
  79.8 0.1 shard_map.107.own
  79.9 11.9 %collective-permute-done.22.refs_2_ = bf16[48,768]{1,0:T(8,128)(2,1)S(1)} collective-permute-done((bf16[48,768]{1,0:T(8,128)(2,1)S(1)}, bf16[48,768]{1,0:T(8,128)(2,1)S(1)}, u32[]{:S(2)}, u32[]{:S(2)}) %collective-permute-start.22) | collective-permute-done | bytes 73760 | tf_op jit(solution)/shard_map/ppermute | solution.py:225
  91.7 1.4 %collective-permute-start.16 = (bf16[48,768]{1,0:T(8,128)(2,1)S(1)}, bf16[48,768]{1,0:T(8,128)(2,1)S(1)}, u32[]{:S(2)}, u32[]{:S(2)}) collective-permute-start(bf16[48,768]{1,0:T(8,128)(2,1)S(1)} %shard_map.107.own), channel_id=1, source_target_pairs={{0,1},{1,0},{2,3},{3,2},{4,5},{5,4},{6,7},{7,6},{8,9},{9,8},{10,11... | collective-permute-start | bytes 221192 | tf_op jit(solution)/shard_map/ppermute | solution.py:235
  93.1 0.0 collective-permute-done.21.refs_1_
  93.1 0.1 shard_map.111.own
  93.2 0.7 collective-permute-start.24
  93.9 0.0 collective-permute-done.6.refs_1_
  93.9 0.0 collective-permute-done.7.refs_2_
  93.9 0.0 collective-permute-done.8.refs_3_
  93.9 1.0 shard_map.104
  94.9 1.2 %collective-permute-done.16.other = bf16[48,768]{1,0:T(8,128)(2,1)S(1)} collective-permute-done((bf16[48,768]{1,0:T(8,128)(2,1)S(1)}, bf16[48,768]{1,0:T(8,128)(2,1)S(1)}, u32[]{:S(2)}, u32[]{:S(2)}) %collective-permute-start.16) | collective-permute-done | bytes 73760 | tf_op jit(solution)/shard_map/ppermute | solution.py:235
  96.1 0.9 shard_map.108
  97.0 0.6 collective-permute-done.24.other
  97.6 0.9 shard_map.112
  (12 shorter events, 0.1 us)
Async XLA Ops:
  0.6 7.7 %copy-start.5 = (bf16[1,1024,384]{2,1,0:T(8,128)(2,1)S(1)}, bf16[1,1024,384]{2,1,0:T(8,128)(2,1)}, u32[]{:S(2)}) copy-start(bf16[1,1024,384]{2,1,0:T(8,128)(2,1)} %param.7) | copy-start | bytes 2359300
  0.7 25.1 %copy-start = (bf16[3,384,192]{1,2,0:T(8,128)(2,1)S(1)}, bf16[3,384,192]{1,2,0:T(8,128)(2,1)}, u32[]{:S(2)}) copy-start(bf16[3,384,192]{1,2,0:T(8,128)(2,1)} %param.10) | copy-start | bytes 1327108
  0.7 25.1 %copy-start.1 = (bf16[3,384,192]{1,2,0:T(8,128)(2,1)S(1)}, bf16[3,384,192]{1,2,0:T(8,128)(2,1)}, u32[]{:S(2)}) copy-start(bf16[3,384,192]{1,2,0:T(8,128)(2,1)} %param.8) | copy-start | bytes 1327108
  0.8 25.1 %copy-start.3 = (bf16[192,384]{1,0:T(8,128)(2,1)S(1)}, bf16[192,384]{1,0:T(8,128)(2,1)}, u32[]{:S(2)}) copy-start(bf16[192,384]{1,0:T(8,128)(2,1)} %refs_6_.1) | copy-start | bytes 442372
  2.2 10.4 %collective-permute-start.5 = (bf16[256,384]{1,0:T(8,128)(2,1)S(1)}, bf16[256,384]{1,0:T(8,128)(2,1)S(1)}, u32[]{:S(2)}, u32[]{:S(2)}) collective-permute-start(bf16[256,384]{1,0:T(8,128)(2,1)S(1)} %get-tuple-element.63), channel_id=1, source_target_pairs={{0,6},{1,7},{2,0},{3,1},{4,2},{5,3},{6,4},{7,5},{8,14},{9,15},{10,... | collective-permute-start | bytes 589832 | tf_op jit(solution)/shard_map/ppermute | solution.py:225
  7.3 10.4 %collective-permute-start.3 = (bf16[256,384]{1,0:T(8,128)(2,1)S(1)}, bf16[256,384]{1,0:T(8,128)(2,1)S(1)}, u32[]{:S(2)}, u32[]{:S(2)}) collective-permute-start(bf16[256,384]{1,0:T(8,128)(2,1)S(1)} %get-tuple-element.64), channel_id=1, source_target_pairs={{0,2},{1,3},{2,4},{3,5},{4,6},{5,7},{6,0},{7,1},{8,10},{9,11},{10,... | collective-permute-start | bytes 589832 | tf_op jit(solution)/shard_map/ppermute | solution.py:225
  7.3 33.5 %copy-start.4 = (bf16[192,384]{1,0:T(8,128)(2,1)S(1)}, bf16[192,384]{1,0:T(8,128)(2,1)}, u32[]{:S(2)}) copy-start(bf16[192,384]{1,0:T(8,128)(2,1)} %refs_9_.1) | copy-start | bytes 442372
  7.3 18.5 %collective-permute-start.4 = (bf16[256,384]{1,0:T(8,128)(2,1)S(1)}, bf16[256,384]{1,0:T(8,128)(2,1)S(1)}, u32[]{:S(2)}, u32[]{:S(2)}) collective-permute-start(bf16[256,384]{1,0:T(8,128)(2,1)S(1)} %get-tuple-element.66), channel_id=1, source_target_pairs={{0,4},{1,5},{2,6},{3,7},{4,0},{5,1},{6,2},{7,3},{8,12},{9,13},{10,... | collective-permute-start | bytes 589832 | tf_op jit(solution)/shard_map/ppermute | solution.py:225
  8.4 28.0 %collective-permute-start.2 = (bf16[256,384]{1,0:T(8,128)(2,1)S(1)}, bf16[256,384]{1,0:T(8,128)(2,1)S(1)}, u32[]{:S(2)}, u32[]{:S(2)}) collective-permute-start(bf16[256,384]{1,0:T(8,128)(2,1)S(1)} %get-tuple-element.67), channel_id=1, source_target_pairs={{0,6},{1,7},{2,0},{3,1},{4,2},{5,3},{6,4},{7,5},{8,14},{9,15},{10,... | collective-permute-start | bytes 589832 | tf_op jit(solution)/shard_map/ppermute | solution.py:225
  11.3 25.1 %collective-permute-start = (bf16[256,384]{1,0:T(8,128)(2,1)S(1)}, bf16[256,384]{1,0:T(8,128)(2,1)S(1)}, u32[]{:S(2)}, u32[]{:S(2)}) collective-permute-start(bf16[256,384]{1,0:T(8,128)(2,1)S(1)} %get-tuple-element.68), channel_id=1, source_target_pairs={{0,2},{1,3},{2,4},{3,5},{4,6},{5,7},{6,0},{7,1},{8,10},{9,11},{10,... | collective-permute-start | bytes 589832 | tf_op jit(solution)/shard_map/ppermute | solution.py:225
  12.6 28.2 %collective-permute-start.1 = (bf16[256,384]{1,0:T(8,128)(2,1)S(1)}, bf16[256,384]{1,0:T(8,128)(2,1)S(1)}, u32[]{:S(2)}, u32[]{:S(2)}) collective-permute-start(bf16[256,384]{1,0:T(8,128)(2,1)S(1)} %get-tuple-element.70), channel_id=1, source_target_pairs={{0,4},{1,5},{2,6},{3,7},{4,0},{5,1},{6,2},{7,3},{8,12},{9,13},{10,... | collective-permute-start | bytes 589832 | tf_op jit(solution)/shard_map/ppermute | solution.py:225
  40.8 1.2 %copy-start.2 = (f32[1024,192]{1,0:T(8,128)S(1)}, f32[1024,192]{1,0:T(8,128)}, u32[]{:S(2)}) copy-start(f32[1024,192]{1,0:T(8,128)} %get-tuple-element.37.refs_7_) | copy-start | bytes 2359300
  49.7 1.6 %collective-permute-start.9 = (bf16[2,96,768]{2,1,0:T(8,128)(2,1)S(1)}, bf16[2,96,768]{2,1,0:T(8,128)(2,1)S(1)}, u32[]{:S(2)}, u32[]{:S(2)}) collective-permute-start(bf16[2,96,768]{2,1,0:T(8,128)(2,1)S(1)} %get-tuple-element.48), channel_id=1, source_target_pairs={{0,8},{1,9},{2,10},{3,11},{4,12},{5,13},{6,14},{7,15},{8,0},{9,1},... | collective-permute-start | bytes 884744 | tf_op jit(solution)/shard_map/ppermute | solution.py:235
  49.8 5.2 %collective-permute-start.17 = (bf16[2,96,768]{2,1,0:T(8,128)(2,1)S(1)}, bf16[2,96,768]{2,1,0:T(8,128)(2,1)S(1)}, u32[]{:S(2)}, u32[]{:S(2)}) collective-permute-start(bf16[2,96,768]{2,1,0:T(8,128)(2,1)S(1)} %get-tuple-element.56), channel_id=1, source_target_pairs={{0,8},{1,9},{2,10},{3,11},{4,12},{5,13},{6,14},{7,15},{8,0},{9,1},... | collective-permute-start | bytes 884744 | tf_op jit(solution)/shard_map/ppermute | solution.py:235
  51.4 6.7 %collective-permute-start.10 = (bf16[48,768]{1,0:T(8,128)(2,1)S(1)}, bf16[48,768]{1,0:T(8,128)(2,1)S(1)}, u32[]{:S(2)}, u32[]{:S(2)}) collective-permute-start(bf16[48,768]{1,0:T(8,128)(2,1)S(1)} %get-tuple-element.50), channel_id=1, source_target_pairs={{0,1},{1,0},{2,3},{3,2},{4,5},{5,4},{6,7},{7,6},{8,9},{9,8},{10,11... | collective-permute-start | bytes 221192 | tf_op jit(solution)/shard_map/ppermute | solution.py:235
  53.0 5.6 %collective-permute-start.11 = (bf16[48,768]{1,0:T(8,128)(2,1)S(1)}, bf16[48,768]{1,0:T(8,128)(2,1)S(1)}, u32[]{:S(2)}, u32[]{:S(2)}) collective-permute-start(bf16[48,768]{1,0:T(8,128)(2,1)S(1)} %get-tuple-element.51), channel_id=1, source_target_pairs={{0,16},{1,17},{2,18},{3,19},{4,20},{5,21},{6,22},{7,23},{8,24},{9,... | collective-permute-start | bytes 221192 | tf_op jit(solution)/shard_map/ppermute | solution.py:235
  54.5 5.5 %collective-permute-start.12 = (bf16[48,768]{1,0:T(8,128)(2,1)S(1)}, bf16[48,768]{1,0:T(8,128)(2,1)S(1)}, u32[]{:S(2)}, u32[]{:S(2)}) collective-permute-start(bf16[48,768]{1,0:T(8,128)(2,1)S(1)} %get-tuple-element.52), channel_id=1, source_target_pairs={{0,17},{1,16},{2,19},{3,18},{4,21},{5,20},{6,23},{7,22},{8,25},{9,... | collective-permute-start | bytes 221192 | tf_op jit(solution)/shard_map/ppermute | solution.py:235
  55.0 7.9 %collective-permute-start.18 = (bf16[48,768]{1,0:T(8,128)(2,1)S(1)}, bf16[48,768]{1,0:T(8,128)(2,1)S(1)}, u32[]{:S(2)}, u32[]{:S(2)}) collective-permute-start(bf16[48,768]{1,0:T(8,128)(2,1)S(1)} %get-tuple-element.58), channel_id=1, source_target_pairs={{0,1},{1,0},{2,3},{3,2},{4,5},{5,4},{6,7},{7,6},{8,9},{9,8},{10,11... | collective-permute-start | bytes 221192 | tf_op jit(solution)/shard_map/ppermute | solution.py:235
  56.6 7.0 %collective-permute-start.19 = (bf16[48,768]{1,0:T(8,128)(2,1)S(1)}, bf16[48,768]{1,0:T(8,128)(2,1)S(1)}, u32[]{:S(2)}, u32[]{:S(2)}) collective-permute-start(bf16[48,768]{1,0:T(8,128)(2,1)S(1)} %get-tuple-element.59), channel_id=1, source_target_pairs={{0,16},{1,17},{2,18},{3,19},{4,20},{5,21},{6,22},{7,23},{8,24},{9,... | collective-permute-start | bytes 221192 | tf_op jit(solution)/shard_map/ppermute | solution.py:235
  58.1 5.5 %collective-permute-start.20 = (bf16[48,768]{1,0:T(8,128)(2,1)S(1)}, bf16[48,768]{1,0:T(8,128)(2,1)S(1)}, u32[]{:S(2)}, u32[]{:S(2)}) collective-permute-start(bf16[48,768]{1,0:T(8,128)(2,1)S(1)} %get-tuple-element.60), channel_id=1, source_target_pairs={{0,17},{1,16},{2,19},{3,18},{4,21},{5,20},{6,23},{7,22},{8,25},{9,... | collective-permute-start | bytes 221192 | tf_op jit(solution)/shard_map/ppermute | solution.py:235
  60.1 6.8 %collective-permute-start.15 = (bf16[48,768]{1,0:T(8,128)(2,1)S(1)}, bf16[48,768]{1,0:T(8,128)(2,1)S(1)}, u32[]{:S(2)}, u32[]{:S(2)}) collective-permute-start(bf16[48,768]{1,0:T(8,128)(2,1)S(1)} %shard_map.106.refs_0_), channel_id=1, source_target_pairs={{0,6},{1,7},{2,0},{3,1},{4,2},{5,3},{6,4},{7,5},{8,14},{9,15},{10,... | collective-permute-start | bytes 221192 | tf_op jit(solution)/shard_map/ppermute | solution.py:225
  62.9 13.1 %collective-permute-start.14 = (bf16[48,768]{1,0:T(8,128)(2,1)S(1)}, bf16[48,768]{1,0:T(8,128)(2,1)S(1)}, u32[]{:S(2)}, u32[]{:S(2)}) collective-permute-start(bf16[48,768]{1,0:T(8,128)(2,1)S(1)} %shard_map.106.refs_0_), channel_id=1, source_target_pairs={{0,4},{1,5},{2,6},{3,7},{4,0},{5,1},{6,2},{7,3},{8,12},{9,13},{10,... | collective-permute-start | bytes 221192 | tf_op jit(solution)/shard_map/ppermute | solution.py:225
  62.9 13.1 %collective-permute-start.13 = (bf16[48,768]{1,0:T(8,128)(2,1)S(1)}, bf16[48,768]{1,0:T(8,128)(2,1)S(1)}, u32[]{:S(2)}, u32[]{:S(2)}) collective-permute-start(bf16[48,768]{1,0:T(8,128)(2,1)S(1)} %shard_map.106.refs_0_), channel_id=1, source_target_pairs={{0,2},{1,3},{2,4},{3,5},{4,6},{5,7},{6,0},{7,1},{8,10},{9,11},{10,... | collective-permute-start | bytes 221192 | tf_op jit(solution)/shard_map/ppermute | solution.py:225
  63.6 12.4 %collective-permute-start.23 = (bf16[48,768]{1,0:T(8,128)(2,1)S(1)}, bf16[48,768]{1,0:T(8,128)(2,1)S(1)}, u32[]{:S(2)}, u32[]{:S(2)}) collective-permute-start(bf16[48,768]{1,0:T(8,128)(2,1)S(1)} %shard_map.110.refs_0_), channel_id=1, source_target_pairs={{0,6},{1,7},{2,0},{3,1},{4,2},{5,3},{6,4},{7,5},{8,14},{9,15},{10,... | collective-permute-start | bytes 221192 | tf_op jit(solution)/shard_map/ppermute | solution.py:225
  66.9 27.0 %collective-permute-start.6 = (bf16[256,384]{1,0:T(8,128)(2,1)S(1)}, bf16[256,384]{1,0:T(8,128)(2,1)S(1)}, u32[]{:S(2)}, u32[]{:S(2)}) collective-permute-start(bf16[256,384]{1,0:T(8,128)(2,1)S(1)} %get-tuple-element.44), channel_id=1, source_target_pairs={{0,2},{1,3},{2,4},{3,5},{4,6},{5,7},{6,0},{7,1},{8,10},{9,11},{10,... | collective-permute-start | bytes 589832 | tf_op jit(solution)/shard_map/ppermute | solution.py:225
  66.9 27.0 %collective-permute-start.7 = (bf16[256,384]{1,0:T(8,128)(2,1)S(1)}, bf16[256,384]{1,0:T(8,128)(2,1)S(1)}, u32[]{:S(2)}, u32[]{:S(2)}) collective-permute-start(bf16[256,384]{1,0:T(8,128)(2,1)S(1)} %get-tuple-element.45), channel_id=1, source_target_pairs={{0,4},{1,5},{2,6},{3,7},{4,0},{5,1},{6,2},{7,3},{8,12},{9,13},{10,... | collective-permute-start | bytes 589832 | tf_op jit(solution)/shard_map/ppermute | solution.py:225
  76.1 17.9 %collective-permute-start.8 = (bf16[256,384]{1,0:T(8,128)(2,1)S(1)}, bf16[256,384]{1,0:T(8,128)(2,1)S(1)}, u32[]{:S(2)}, u32[]{:S(2)}) collective-permute-start(bf16[256,384]{1,0:T(8,128)(2,1)S(1)} %get-tuple-element.46), channel_id=1, source_target_pairs={{0,6},{1,7},{2,0},{3,1},{4,2},{5,3},{6,4},{7,5},{8,14},{9,15},{10,... | collective-permute-start | bytes 589832 | tf_op jit(solution)/shard_map/ppermute | solution.py:225
  76.1 15.7 %collective-permute-start.22 = (bf16[48,768]{1,0:T(8,128)(2,1)S(1)}, bf16[48,768]{1,0:T(8,128)(2,1)S(1)}, u32[]{:S(2)}, u32[]{:S(2)}) collective-permute-start(bf16[48,768]{1,0:T(8,128)(2,1)S(1)} %shard_map.110.refs_0_), channel_id=1, source_target_pairs={{0,4},{1,5},{2,6},{3,7},{4,0},{5,1},{6,2},{7,3},{8,12},{9,13},{10,... | collective-permute-start | bytes 221192 | tf_op jit(solution)/shard_map/ppermute | solution.py:225
  76.1 17.0 %collective-permute-start.21 = (bf16[48,768]{1,0:T(8,128)(2,1)S(1)}, bf16[48,768]{1,0:T(8,128)(2,1)S(1)}, u32[]{:S(2)}, u32[]{:S(2)}) collective-permute-start(bf16[48,768]{1,0:T(8,128)(2,1)S(1)} %shard_map.110.refs_0_), channel_id=1, source_target_pairs={{0,2},{1,3},{2,4},{3,5},{4,6},{5,7},{6,0},{7,1},{8,10},{9,11},{10,... | collective-permute-start | bytes 221192 | tf_op jit(solution)/shard_map/ppermute | solution.py:225
  91.7 4.4 %collective-permute-start.16 = (bf16[48,768]{1,0:T(8,128)(2,1)S(1)}, bf16[48,768]{1,0:T(8,128)(2,1)S(1)}, u32[]{:S(2)}, u32[]{:S(2)}) collective-permute-start(bf16[48,768]{1,0:T(8,128)(2,1)S(1)} %shard_map.107.own), channel_id=1, source_target_pairs={{0,1},{1,0},{2,3},{3,2},{4,5},{5,4},{6,7},{7,6},{8,9},{9,8},{10,11... | collective-permute-start | bytes 221192 | tf_op jit(solution)/shard_map/ppermute | solution.py:235
  93.2 4.4 %collective-permute-start.24 = (bf16[48,768]{1,0:T(8,128)(2,1)S(1)}, bf16[48,768]{1,0:T(8,128)(2,1)S(1)}, u32[]{:S(2)}, u32[]{:S(2)}) collective-permute-start(bf16[48,768]{1,0:T(8,128)(2,1)S(1)} %shard_map.111.own), channel_id=1, source_target_pairs={{0,1},{1,0},{2,3},{3,2},{4,5},{5,4},{6,7},{7,6},{8,9},{9,8},{10,11... | collective-permute-start | bytes 221192 | tf_op jit(solution)/shard_map/ppermute | solution.py:235

commit v2 on v1

v2 whole, which is shorter than its diff:
```python
import functools
import math

import jax
import jax.numpy as jnp
from jax import lax
from jax.experimental import pallas as pl
from jax.experimental.pallas import tpu as pltpu
from jax.sharding import PartitionSpec as P

DILATION_ONE = 2048
DILATION_TWO = 4096
TILE = 256
CHUNK = 32
MAX_PERMUTES = 8
MERGED = True
AFTER = ((),(),(),1,)
BF16 = jnp.bfloat16
F32 = jnp.float32
VMEM = pl.BlockSpec(memory_space=pltpu.VMEM)
ANY = pl.BlockSpec(memory_space=pl.ANY)


def gelu_parts(values):
    coeff = math.sqrt(2.0 / math.pi)
    square = values * values
    tanh_val = jnp.tanh(values * (coeff + (coeff * 0.044715) * square))
    half = 0.5 + 0.5 * tanh_val
    slope = half + half * (1.0 - tanh_val) * (values * (coeff + (3.0 * coeff * 0.044715) * square))
    return values * half, slope


def dot(left, right):
    return jnp.dot(left, right, preferred_element_type=F32)


def dot_nt(left, right):
    return lax.dot_general(left, right, (((1,), (1,)), ((), ())), preferred_element_type=F32)


def position(hop):
    return lax.axis_index("seq") // hop


def behind(me, k, count):
    return lax.rem(me + (count - k), count)


def ahead(me, k, count):
    return lax.rem(me + k, count)


def call(kernel, out_shapes, scratch, args, after=(), mib=8):
    n_args, n_after = len(args), len(after)

    def body(*refs):
        kernel(*refs[:n_args], *refs[n_args + n_after :])

    return pl.pallas_call(
        body,
        out_shape=[jax.ShapeDtypeStruct(s, d) for s, d in out_shapes],
        in_specs=[VMEM] * n_args + [ANY] * n_after,
        out_specs=[VMEM] * len(out_shapes),
        scratch_shapes=[pltpu.VMEM(s, d) for s, d in scratch],
        compiler_params=pltpu.CompilerParams(vmem_limit_bytes=mib << 20),
    )(*args, *after)


def cut_kernel(hop, halves, block, *pieces):
    count = len(pieces) // halves
    step = pieces[0].shape[0]
    me = position(hop)
    for i, piece in enumerate(pieces):
        at = ahead(me, i % count, count) * (step * halves) + i // count * step
        piece[...] = block[pl.ds(pl.multiple_of(at, step), step), :]


def place(parts, rows_ref, hop, half=0):
    if len(parts) == 1:
        rows_ref[...] = parts[0][...]
        return
    count = len(parts)
    size = rows_ref.shape[0] // count
    me = position(hop)
    for k, part in enumerate(parts):
        at = pl.multiple_of(behind(me, k, count) * size, size)
        rows_ref[pl.ds(at, size), :] = part[pl.ds(half * size, size), :]


def hand_out(rows_ref, parts, hop):
    if len(parts) == 1:
        parts[0][...] = rows_ref[...]
        return
    count = len(parts)
    size = rows_ref.shape[0] // count
    me = position(hop)
    for k, part in enumerate(parts):
        at = pl.multiple_of(ahead(me, k, count) * size, size)
        part[...] = rows_ref[pl.ds(at, size), :]


def tap_sum(padded_ref, shift, start, tile, weight_of, mm):
    total = mm(padded_ref[pl.ds(start + shift, tile), :], weight_of(1))
    rows = padded_ref.shape[0] - 2 * shift
    if start + tile > shift:
        total = total + mm(padded_ref[pl.ds(start, tile), :], weight_of(0))
    if start < rows - shift:
        total = total + mm(padded_ref[pl.ds(start + 2 * shift, tile), :], weight_of(2))
    return total


def clear_edges(padded_ref, shift):
    rows = padded_ref.shape[0]
    zeros = jnp.zeros((shift, padded_ref.shape[1]), padded_ref.dtype)
    padded_ref[pl.ds(0, shift), :] = zeros
    padded_ref[pl.ds(rows - shift, shift), :] = zeros


def forward_kernel(shifts, hop, count, halves, *refs):
    parts = refs[:count]
    weights = refs[count : count + 3]
    outs = refs[count + 3 : count + 11]
    scratch = refs[count + 11 :]
    for half in range(halves):
        place(parts, scratch[0], hop, half)
        forward_half(shifts, weights, [out.at[half] for out in outs], scratch)


def forward_half(shifts, weights, outs, scratch):
    k1t, p1, k2t = weights
    act1_t, mid1_t, s_x, s_p1, act2_t, mid2_t, s_h, s_p2 = outs
    x_rows, pad1, pad2, wide, narrow = scratch
    rows = x_rows.shape[0]

    def activate(source, source_start, pad, shift, start, slope_ref):
        def step(i, carry):
            at = pl.multiple_of(i * CHUNK, CHUNK)
            value, slope = gelu_parts(source[pl.ds(source_start + at, CHUNK), :].astype(F32))
            pad[pl.ds(start + shift + at, CHUNK), :] = value.astype(BF16)
            slope_ref[pl.ds(start + at, CHUNK), :] = slope.astype(BF16)
            return carry

        lax.fori_loop(0, TILE // CHUNK, step, 0, unroll=2)

    def narrow_gelu(start, slope_ref):
        def step(i, carry):
            at = pl.multiple_of(i * CHUNK, CHUNK)
            value, slope = gelu_parts(narrow[pl.ds(at, CHUNK), :])
            narrow[pl.ds(at, CHUNK), :] = value
            slope_ref[pl.ds(start + at, CHUNK), :] = slope.astype(BF16)
            return carry

        lax.fori_loop(0, TILE // CHUNK, step, 0, unroll=2)

    clear_edges(pad1, shifts[0])
    clear_edges(pad2, shifts[1])
    for start in range(0, rows, TILE):
        activate(x_rows, start, pad1, shifts[0], start, s_x)
        act1_t[:, pl.ds(start, TILE)] = pad1[pl.ds(start + shifts[0], TILE), :].T
    for start in range(0, rows, TILE):
        narrow[...] = tap_sum(pad1, shifts[0], start, TILE, lambda k: k1t[k], dot_nt)
        narrow_gelu(start, s_p1)
        mid = narrow[...].astype(BF16)
        mid1_t[:, pl.ds(start, TILE)] = mid.T
        wide[...] = (x_rows[pl.ds(start, TILE), :].astype(F32) + dot(mid, p1[...])).astype(BF16)
        activate(wide, 0, pad2, shifts[1], start, s_h)
        act2_t[:, pl.ds(start, TILE)] = pad2[pl.ds(start + shifts[1], TILE), :].T
    for start in range(0, rows, TILE):
        narrow[...] = tap_sum(pad2, shifts[1], start, TILE, lambda k: k2t[k], dot_nt)
        narrow_gelu(start, s_p2)
        mid2_t[:, pl.ds(start, TILE)] = narrow[...].astype(BF16).T


def backward_kernel(shift, hop, half, n_in, n_out, first, last, *refs):
    parts = refs[:n_in]
    act_t, mid_t, s_state, s_pre = (ref.at[half] for ref in refs[n_in : n_in + 4])
    kt, point = refs[n_in + 4 : n_in + 6]
    at = n_in + 6
    if not first:
        so_far = refs[at]
        at += 1
    outs = refs[at : at + n_out]
    at += n_out
    if last:
        keep, send = refs[at : at + 2]
        at += 2
        g_rows, pad, x_rows, grads = refs[at:]
    else:
        grads = refs[at]
        g_rows, pad, x_rows = refs[at + 1 :]
    rows = g_rows.shape[0]
    place(parts, g_rows, hop)
    clear_edges(pad, shift)
    for start in range(0, rows, TILE):
        mid_grad = dot_nt(g_rows[pl.ds(start, TILE), :], point[...])
        pad[pl.ds(start + shift, TILE), :] = (
            mid_grad * s_pre[pl.ds(start, TILE), :].astype(F32)
        ).astype(BF16)
    for start in range(0, rows, TILE):
        act_grad = tap_sum(pad, shift, start, TILE, lambda k: kt[2 - k], dot)
        x_rows[pl.ds(start, TILE), :] = (
            g_rows[pl.ds(start, TILE), :].astype(F32)
            + act_grad * s_state[pl.ds(start, TILE), :].astype(F32)
        ).astype(BF16)
    hand_out(x_rows, outs, hop)
    act = act_t[...]
    total = jnp.concatenate(
        [
            dot(act, pad[pl.ds(2 * shift, rows), :]),
            dot(act, pad[pl.ds(shift, rows), :]),
            dot(act, pad[pl.ds(0, rows), :]),
            dot(mid_t[...], g_rows[...]).T,
        ],
        axis=1,
    )
    if not first:
        total = total + so_far[...]
    grads[...] = total
    if last:
        size = keep.shape[1]
        core = lax.rem(lax.axis_index("dp"), 2)
        for x_to in range(2):
            for target, parity in ((keep, core), (send, 1 - core)):
                rows_at = pl.multiple_of((2 * x_to + parity) * size, size)
                target[x_to] = grads[pl.ds(rows_at, size), :].astype(BF16)


def split_kernel(*refs):
    pieces = refs[-4:]
    pairs = list(zip(refs[0:-4:2], refs[1:-4:2]))
    x_at = lax.axis_index("dp") // 2
    y_at = lax.rem(lax.axis_index("seq"), 2)
    size = pieces[0].shape[1]
    for k, piece in enumerate(pieces):
        x_to = lax.rem(x_at + k // 2, 2)
        rows = pl.ds(pl.multiple_of(lax.rem(y_at + k, 2) * size, size), size)
        for i, (keep, received) in enumerate(pairs):
            total = keep[x_to, rows, :].astype(F32) + received[x_to, rows, :].astype(F32)
            piece[i] = total.astype(piece.dtype)


def sum_of(refs):
    total = refs[0][...].astype(F32)
    for ref in refs[1:]:
        total = total + ref[...].astype(F32)
    return total


def sum_kernel(*refs):
    refs[-1][...] = sum_of(refs[:-1]).astype(refs[-1].dtype)


def halve_kernel(hop, *refs):
    *parts, keep, send, total = refs
    total[...] = sum_of(parts)
    size = keep.shape[1]
    mine = lax.rem(position(hop), 2)
    for target, half in ((keep, mine), (send, 1 - mine)):
        target[...] = total[:, pl.ds(pl.multiple_of(half * size, size), size), :].astype(target.dtype)


def finish_kernel(scale, hop, n_blocks, *refs):
    parts, outs, rows = refs[: -2 * n_blocks - 1], refs[-2 * n_blocks - 1 : -1], refs[-1]
    z_at = lax.rem(position(hop), 2)
    y_at = lax.rem(lax.axis_index("seq"), 2)
    size = parts[0].shape[1]
    per_y = rows.shape[1] // 2
    for k, part in enumerate(parts):
        at = lax.rem(y_at + k, 2) * per_y
        if len(parts) > 2:
            at = at + lax.rem(z_at + k // 2, 2) * size
        rows[:, pl.ds(pl.multiple_of(at, size), size), :] = part[...].astype(F32) * scale
    for i in range(n_blocks):
        conv, point = outs[2 * i : 2 * i + 2]
        width = conv.shape[2]
        whole = rows[i]
        for k in range(3):
            conv[k] = whole[:, k * width : (k + 1) * width]
        point[...] = whole[:, 3 * width :].T


def collect_kernel(hop, halves, *refs):
    *parts, out = refs
    count = len(parts) // halves
    size = out.shape[0] // count
    step = size // halves
    me = position(hop)
    for h in range(halves):
        for k in range(count):
            at = pl.multiple_of(behind(me, k, count) * size + h * step, step)
            out[pl.ds(at, step), :] = parts[h * count + k][...]


def send_ahead(block, hop, k):
    size = lax.axis_size("seq")
    count = size // hop
    route = [(i, ((i // hop + k) % count) * hop + i % hop) for i in range(size)]
    return lax.ppermute(block, "seq", route)


def mirrored(block, dp_bits, seq_bits):
    n_dp, n_seq = lax.axis_size("dp"), lax.axis_size("seq")
    route = [
        (i * n_seq + j, (i ^ dp_bits) * n_seq + (j ^ seq_bits))
        for i in range(n_dp)
        for j in range(n_seq)
    ]
    return lax.ppermute(block, ("dp", "seq"), route)


def column_groups(hop):
    size = lax.axis_size("seq")
    return [list(range(first, size, hop)) for first in range(hop)]


def exchange_all(block, hop):
    count = lax.axis_size("seq") // hop
    cut = block.reshape(count, -1, block.shape[-1])
    swapped = lax.all_to_all(cut, "seq", 0, 0, axis_index_groups=column_groups(hop), tiled=True)
    return swapped.reshape(block.shape)


def to_columns(block, hop, halves, after=()):
    count = lax.axis_size("seq") // hop
    rows, channels = block.shape
    if count > MAX_PERMUTES:
        return [[exchange_all(block, hop)]]
    n_pieces = count * halves
    pieces = call(
        functools.partial(cut_kernel, hop, halves),
        [((rows // n_pieces, channels), BF16)] * n_pieces,
        [],
        [block],
        after,
        mib=2,
    )
    return [forward_pieces(pieces[h * count : (h + 1) * count], hop) for h in range(halves)]


def forward_pieces(pieces, hop):
    return [pieces[0]] + [send_ahead(pieces[k], hop, k) for k in range(1, len(pieces))]


def reduce_weights(blocks, hop, scale, after=()):
    n_blocks = len(blocks)
    _, rows, lanes = blocks[0][0].shape
    width = lanes // 4
    count = lax.axis_size("seq") // hop
    pairs = []
    for keep, send in blocks:
        pairs += [keep, mirrored(send, 1, 0)]
    half = (n_blocks, rows // 2, lanes)
    fourth = (n_blocks, rows // 4, lanes)
    pieces = call(split_kernel, [(half, F32)] + [(half, BF16)] * 3, [], pairs, AFTER[0] and after)
    arrived = [pieces[0]] + [mirrored(pieces[k], 2 * (k // 2), k % 2) for k in range(1, 4)]
    if count == 4:
        keep, send = call(
            functools.partial(halve_kernel, hop), [(fourth, F32), (fourth, BF16)], [(half, F32)], arrived, AFTER[1] and after
        )
        (pair,) = call(sum_kernel, [(fourth, BF16)], [], [keep, mirrored(send, 0, hop)], AFTER[2] and after)
        (own,) = call(sum_kernel, [(fourth, BF16)], [], [pair, mirrored(pair, 0, 2 * hop)], AFTER[3] and after)
        parts = [own] + [mirrored(own, 0, hop * (k // 2) + k % 2) for k in range(1, 4)]
    else:
        (plane,) = call(sum_kernel, [(half, F32)], [], arrived)
        own = lax.psum(plane, "seq", axis_index_groups=column_groups(hop)).astype(BF16)
        parts = [own, mirrored(own, 0, 1)]
    outs = call(
        functools.partial(finish_kernel, scale, hop, n_blocks),
        [((3, rows, width), F32), ((width, rows), F32)] * n_blocks,
        [((n_blocks, rows, lanes), F32)],
        parts,
    )
    return [outs[2 * i : 2 * i + 2] for i in range(n_blocks)]


def shards(
    inputs,
    cotangent,
    first_dilated_kernel,
    first_pointwise_weight,
    second_dilated_kernel,
    second_pointwise_weight,
):
    samples, rows, channels = inputs.shape
    width = first_pointwise_weight.shape[0]
    hop = DILATION_ONE // rows
    count = lax.axis_size("seq") // hop
    size = rows // count
    halves = 1
    step = size // halves
    part = rows // halves
    shifts = (step, step * (DILATION_TWO // DILATION_ONE))
    total_rows = samples * lax.axis_size("dp") * rows * lax.axis_size("seq")
    scale = 1.0 / math.sqrt(total_rows)
    k1t = jnp.swapaxes(first_dilated_kernel, 1, 2)
    k2t = jnp.swapaxes(second_dilated_kernel, 1, 2)

    (x_parts,) = to_columns(inputs.reshape(rows, channels), hop, 1)
    g_parts = to_columns(cotangent.reshape(rows, channels), hop, halves, x_parts[1:3])
    n_parts = len(x_parts)
    state = [
        ((halves, channels, part), BF16),
        ((halves, width, part), BF16),
        ((halves, part, channels), BF16),
        ((halves, part, width), BF16),
    ]
    saved = call(
        functools.partial(forward_kernel, shifts, hop, n_parts, halves),
        state * 2,
        [
            ((part, channels), BF16),
            ((part + 2 * shifts[0], channels), BF16),
            ((part + 2 * shifts[1], channels), BF16),
            ((TILE, channels), BF16),
            ((TILE, width), F32),
        ],
        list(x_parts) + [k1t, first_pointwise_weight, k2t],
        mib=16,
    )
    piece_shape = (g_parts[0][0].shape, BF16)
    part_shape = ((part, channels), BF16)
    grads_shape = ((channels, 4 * width), F32)
    quarter = ((2, channels // 4, 4 * width), BF16)

    def backward(half, g_in, saved, shift, kt, point, out_shapes, so_far, after=()):
        first, last = half == 0, half == halves - 1
        scratch = [part_shape, ((part + 2 * shift, width), BF16), part_shape]
        results = call(
            functools.partial(
                backward_kernel, shift, hop, half, len(g_in), len(out_shapes), first, last
            ),
            out_shapes + ([quarter, quarter] if last else [grads_shape]),
            scratch + ([grads_shape] if last else []),
            list(g_in) + list(saved) + [kt, point] + ([] if first else [so_far]),
            after,
            mib=16,
        )
        n = len(out_shapes)
        return results[:n], results[n:]

    grads2, grads1 = (None,), (None,)
    x_grads = []
    for half in range(halves):
        hidden_grad, grads2 = backward(
            half, g_parts[half], saved[4:], shifts[1], k2t, second_pointwise_weight,
            [part_shape], grads2[0],
        )
        outs, grads1 = backward(
            half, hidden_grad, saved[:4], shifts[0], k1t, first_pointwise_weight,
            [piece_shape] * n_parts, grads1[0],
        )
        x_grads.append(outs)
    back = []
    for outs in x_grads:
        if n_parts == 1:
            back.append(exchange_all(outs[0], hop))
        else:
            back += forward_pieces(outs, hop)
    if n_parts == 1:
        (input_grad,) = back
    else:
        (input_grad,) = call(
            functools.partial(collect_kernel, hop, halves), [((rows, channels), BF16)], [], back
        )
    if MERGED:
        (conv2, point2), (conv1, point1) = reduce_weights([grads2, grads1], hop, scale, back[1:])
    else:
        ((conv2, point2),) = reduce_weights([grads2], hop, scale, back[1:])
        ((conv1, point1),) = reduce_weights([grads1], hop, scale, back[1:])
    return input_grad.reshape(inputs.shape), conv1, point1, conv2, point2


def solution(mesh):
    return jax.shard_map(
        shards,
        mesh=mesh,
        in_specs=(P("dp", "seq", None), P("dp", "seq", None), P(), P(), P(), P()),
        out_specs=(
            P("dp", "seq", None),
            P(None, "dp", None),
            P(None, "dp"),
            P(None, "dp", None),
            P(None, "dp"),
        ),
        check_vma=False,
    )
```

time: 98.8 us -> 82.2 us (0.83)
  waiting for transfers between devices: 41.3 us -> 30.4 us
  Pallas kernels: 21.4 us -> 15.9 us
  local copies, waits for them, and re-layouts: 2.73 us -> 1.15 us
  starting transfers between devices: 32.3 us -> 33.8 us
    ppermute x15 -> x9, waiting for transfers between devices: 37 us -> 14.4 us  [send_ahead(): return lax.ppermute(block, 'seq', route)]
    ppermute x10, waiting for transfers between devices: 4.3 us -> 16 us  [mirrored(): return lax.ppermute(block, ('dp', 'seq'), route)]
    pallas_call x12 -> x11, Pallas kernels: 21.4 us -> 15.9 us  [call(): pl.pallas_call(body, out_shape=[jax.ShapeDtypeStruct(s, d) for s, d in ou...]
    ppermute x10, starting transfers between devices: 9.77 us -> 13 us  [mirrored(): return lax.ppermute(block, ('dp', 'seq'), route)]
    ppermute x15 -> x9, starting transfers between devices: 22.6 us -> 20.8 us  [send_ahead(): return lax.ppermute(block, 'seq', route)]
    dynamic_slice x2 -> x0, local copies, waits for them, and re-layouts: 1.49 us -> none  [to_columns(): lax.dynamic_slice_in_dim(block, (me + k) % count * size, size, 0)]
  transfers between devices with their start and end apart: 25 -> 19, of which waited for: 10 -> 9; matrix products, arithmetic and copies ran while one was open for 0% -> 0% of each run, Pallas kernels for 13% -> 12%
where the time goes in v2:
time: 82.2 us; the launch traced here: 82.1 us
  starting transfers between devices  33.8 us (41%)
  waiting for transfers between devices  30.4 us (37%)
  Pallas kernels  15.9 us (19%)
  local copies, waits for them, and re-layouts  1.15 us (1%)
    ppermute x9, starting transfers between devices, send_ahead(): return lax.ppermute(block, 'seq', route)  20.8 us
    ppermute x10, waiting for transfers between devices, mirrored(): return lax.ppermute(block, ('dp', 'seq'), route)  16 us
    pallas_call x11, Pallas kernels, call(): pl.pallas_call(body, out_shape=[jax.ShapeDtypeStruct(s, d) for s, d in ou...  15.9 us
    ppermute x9, waiting for transfers between devices, send_ahead(): return lax.ppermute(block, 'seq', route)  14.4 us
    ppermute x10, starting transfers between devices, mirrored(): return lax.ppermute(block, ('dp', 'seq'), route)  13 us
  transfers between devices with their start and end apart: 19, of which 9 were waited for; matrix products, arithmetic and copies ran while one was open for 0% of the time, Pallas kernels for 12%

profile of v2, /device:TPU:0, one launch (start us, length us, event | category | flops | bytes accessed | tf_op | source)
XLA Modules:
  0.0 82.1 jit_solution(11830517851531883570)
XLA Ops:
  0.6 0.0 copy-start.2
  0.6 1.1 %copy-done.2 = bf16[1,1024,384]{2,1,0:T(8,128)(2,1)S(1)} copy-done((bf16[1,1024,384]{2,1,0:T(8,128)(2,1)S(1)}, bf16[1,1024,384]{2,1,0:T(8,128)(2,1)}, u32[]{:S(2)}) %copy-start.2) | copy-done | bytes 786456
  1.8 0.0 copy-start.3
  1.8 0.1 shard_map.101
  1.8 3.1 %collective-permute-start = (bf16[256,384]{1,0:T(8,128)(2,1)S(1)}, bf16[256,384]{1,0:T(8,128)(2,1)S(1)}, u32[]{:S(2)}, u32[]{:S(2)}) collective-permute-start(bf16[256,384]{1,0:T(8,128)(2,1)S(1)} %get-tuple-element.40), channel_id=1, source_target_pairs={{0,2},{1,3},{2,4},{3,5},{4,6},{5,7},{6,0},{7,1},{8,10},{9,11},{10,... | collective-permute-start | bytes 589832 | tf_op jit(solution)/shard_map/ppermute | solution.py:298
  4.9 2.6 %collective-permute-start.1 = (bf16[256,384]{1,0:T(8,128)(2,1)S(1)}, bf16[256,384]{1,0:T(8,128)(2,1)S(1)}, u32[]{:S(2)}, u32[]{:S(2)}) collective-permute-start(bf16[256,384]{1,0:T(8,128)(2,1)S(1)} %get-tuple-element.41), channel_id=1, source_target_pairs={{0,4},{1,5},{2,6},{3,7},{4,0},{5,1},{6,2},{7,3},{8,12},{9,13},{10,... | collective-permute-start | bytes 589832 | tf_op jit(solution)/shard_map/ppermute | solution.py:298
  7.5 1.3 %collective-permute-start.5 = (bf16[256,384]{1,0:T(8,128)(2,1)S(1)}, bf16[256,384]{1,0:T(8,128)(2,1)S(1)}, u32[]{:S(2)}, u32[]{:S(2)}) collective-permute-start(bf16[256,384]{1,0:T(8,128)(2,1)S(1)} %get-tuple-element.47), channel_id=1, source_target_pairs={{0,6},{1,7},{2,0},{3,1},{4,2},{5,3},{6,4},{7,5},{8,14},{9,15},{10,... | collective-permute-start | bytes 589832 | tf_op jit(solution)/shard_map/ppermute | solution.py:298
  8.9 3.9 %collective-permute-done.refs_1_ = bf16[256,384]{1,0:T(8,128)(2,1)S(1)} collective-permute-done((bf16[256,384]{1,0:T(8,128)(2,1)S(1)}, bf16[256,384]{1,0:T(8,128)(2,1)S(1)}, u32[]{:S(2)}, u32[]{:S(2)}) %collective-permute-start) | collective-permute-done | bytes 196640 | tf_op jit(solution)/shard_map/ppermute | solution.py:298
  12.8 7.6 %collective-permute-done.1.refs_2_ = bf16[256,384]{1,0:T(8,128)(2,1)S(1)} collective-permute-done((bf16[256,384]{1,0:T(8,128)(2,1)S(1)}, bf16[256,384]{1,0:T(8,128)(2,1)S(1)}, u32[]{:S(2)}, u32[]{:S(2)}) %collective-permute-start.1) | collective-permute-done | bytes 196640 | tf_op jit(solution)/shard_map/ppermute | solution.py:298
  20.4 0.0 copy-done.3
  20.4 0.0 copy-start
  20.4 0.0 copy-start.1
  20.4 0.0 copy-start.4
  20.4 0.1 shard_map.102
  20.5 3.4 %collective-permute-start.2 = (bf16[256,384]{1,0:T(8,128)(2,1)S(1)}, bf16[256,384]{1,0:T(8,128)(2,1)S(1)}, u32[]{:S(2)}, u32[]{:S(2)}) collective-permute-start(bf16[256,384]{1,0:T(8,128)(2,1)S(1)} %get-tuple-element.43), channel_id=1, source_target_pairs={{0,2},{1,3},{2,4},{3,5},{4,6},{5,7},{6,0},{7,1},{8,10},{9,11},{10,... | collective-permute-start | bytes 589832 | tf_op jit(solution)/shard_map/ppermute | solution.py:298
  23.9 3.4 %collective-permute-start.3 = (bf16[256,384]{1,0:T(8,128)(2,1)S(1)}, bf16[256,384]{1,0:T(8,128)(2,1)S(1)}, u32[]{:S(2)}, u32[]{:S(2)}) collective-permute-start(bf16[256,384]{1,0:T(8,128)(2,1)S(1)} %get-tuple-element.44), channel_id=1, source_target_pairs={{0,4},{1,5},{2,6},{3,7},{4,0},{5,1},{6,2},{7,3},{8,12},{9,13},{10,... | collective-permute-start | bytes 589832 | tf_op jit(solution)/shard_map/ppermute | solution.py:298
  27.2 0.0 collective-permute-start.4
  27.2 0.0 collective-permute-done.5.refs_3_
  27.3 0.0 copy-done
  27.3 0.0 copy-done.1
  27.3 0.0 copy-done.4
  27.3 0.0 copy-start.5
  27.3 8.7 %shard_map.103 = (bf16[1,384,1024]{2,1,0:T(8,128)(2,1)S(1)}, bf16[1,192,1024]{2,1,0:T(8,128)(2,1)S(1)}, bf16[1,1024,384]{2,1,0:T(8,128)(2,1)S(1)}, bf16[1,1024,1...) custom-call(bf16[256,384]{1,0:T(8,128)(2,1)S(1)} %get-tuple-element., ...), custom_call_target="tpu_custom_call" | custom-call | tf_op jit(solution)/shard_map/pallas_call | solution.py:59
  36.0 0.0 collective-permute-done.2.refs_1_
  36.0 2.9 %collective-permute-done.3.refs_2_ = bf16[256,384]{1,0:T(8,128)(2,1)S(1)} collective-permute-done((bf16[256,384]{1,0:T(8,128)(2,1)S(1)}, bf16[256,384]{1,0:T(8,128)(2,1)S(1)}, u32[]{:S(2)}, u32[]{:S(2)}) %collective-permute-start.3) | collective-permute-done | bytes 196640 | tf_op jit(solution)/shard_map/ppermute | solution.py:298
  38.8 0.0 collective-permute-done.4.refs_3_
  38.8 0.0 copy-done.5
  38.8 2.4 %shard_map.104 = (bf16[1024,384]{1,0:T(8,128)(2,1)S(1)}, bf16[2,96,768]{2,1,0:T(8,128)(2,1)S(1)}, bf16[2,96,768]{2,1,0:T(8,128)(2,1)S(1)}) custom-call(bf16[256,384]{1,0:T(8,128)(2,1)S(1)} %get-tuple-element.42.refs_0_, bf16[256,384]{1,0:T(8,128)(2,1)S(1)} %collective-permute-done.2.refs_1_, bf16[256,384]{1,0:T(8,128)(2,1)S(1)} %collective-permute-done.3.refs_2_, ...), custom_call_target="tpu_custom_call" | custom-call | tf_op jit(solution)/shard_map/pallas_call | solution.py:59
  41.2 2.4 %shard_map.105 = (bf16[256,384]{1,0:T(8,128)(2,1)S(1)}, bf16[256,384]{1,0:T(8,128)(2,1)S(1)}, bf16[256,384]{1,0:T(8,128)(2,1)S(1)}, bf16[256,384]{1,0:T(8,128)(2...) custom-call(bf16[1024,384]{1,0:T(8,128)(2,1)S(1)} %get-tuple-element.52.refs_0_, ...), custom_call_target="tpu_custom_call" | custom-call | tf_op jit(solution)/shard_map/pallas_call | solution.py:59
  43.6 0.1 collective-permute-start.10
  43.7 0.5 collective-permute-start.9
  44.2 1.1 %collective-permute-done.10.refs_3_ = bf16[2,96,768]{2,1,0:T(8,128)(2,1)S(1)} collective-permute-done((bf16[2,96,768]{2,1,0:T(8,128)(2,1)S(1)}, bf16[2,96,768]{2,1,0:T(8,128)(2,1)S(1)}, u32[]{:S(2)}, u32[]{:S(2)}) %collective-permute-start.10) | collective-permute-done | bytes 294944 | tf_op jit(solution)/shard_map/ppermute | solution.py:308
  45.3 0.4 collective-permute-done.9.refs_1_
  45.7 0.1 shard_map.107
  45.8 1.6 %collective-permute-start.11 = (bf16[2,48,768]{2,1,0:T(8,128)(2,1)S(1)}, bf16[2,48,768]{2,1,0:T(8,128)(2,1)S(1)}, u32[]{:S(2)}, u32[]{:S(2)}) collective-permute-start(bf16[2,48,768]{2,1,0:T(8,128)(2,1)S(1)} %get-tuple-element.66), channel_id=1, source_target_pairs={{0,1},{1,0},{2,3},{3,2},{4,5},{5,4},{6,7},{7,6},{8,9},{9,8},{10,11... | collective-permute-start | bytes 442376 | tf_op jit(solution)/shard_map/ppermute | solution.py:308
  47.4 1.5 %collective-permute-start.12 = (bf16[2,48,768]{2,1,0:T(8,128)(2,1)S(1)}, bf16[2,48,768]{2,1,0:T(8,128)(2,1)S(1)}, u32[]{:S(2)}, u32[]{:S(2)}) collective-permute-start(bf16[2,48,768]{2,1,0:T(8,128)(2,1)S(1)} %get-tuple-element.67), channel_id=1, source_target_pairs={{0,16},{1,17},{2,18},{3,19},{4,20},{5,21},{6,22},{7,23},{8,24},{9,... | collective-permute-start | bytes 442376 | tf_op jit(solution)/shard_map/ppermute | solution.py:308
  48.9 0.5 collective-permute-start.13
  49.4 4.7 %collective-permute-start.6 = (bf16[256,384]{1,0:T(8,128)(2,1)S(1)}, bf16[256,384]{1,0:T(8,128)(2,1)S(1)}, u32[]{:S(2)}, u32[]{:S(2)}) collective-permute-start(bf16[256,384]{1,0:T(8,128)(2,1)S(1)} %get-tuple-element.58), channel_id=1, source_target_pairs={{0,2},{1,3},{2,4},{3,5},{4,6},{5,7},{6,0},{7,1},{8,10},{9,11},{10,... | collective-permute-start | bytes 589832 | tf_op jit(solution)/shard_map/ppermute | solution.py:298
  54.1 0.0 collective-permute-start.7
  54.1 0.0 collective-permute-done.11.refs_1_
  54.1 2.3 %collective-permute-start.8 = (bf16[256,384]{1,0:T(8,128)(2,1)S(1)}, bf16[256,384]{1,0:T(8,128)(2,1)S(1)}, u32[]{:S(2)}, u32[]{:S(2)}) collective-permute-start(bf16[256,384]{1,0:T(8,128)(2,1)S(1)} %get-tuple-element.60), channel_id=1, source_target_pairs={{0,6},{1,7},{2,0},{3,1},{4,2},{5,3},{6,4},{7,5},{8,14},{9,15},{10,... | collective-permute-start | bytes 589832 | tf_op jit(solution)/shard_map/ppermute | solution.py:298
  56.4 0.0 collective-permute-done.12.refs_2_
  56.4 0.0 collective-permute-done.13.refs_3_
  56.4 0.1 shard_map.108
  56.6 4.4 %collective-permute-start.14 = (bf16[2,24,768]{2,1,0:T(8,128)(2,1)S(1)}, bf16[2,24,768]{2,1,0:T(8,128)(2,1)S(1)}, u32[]{:S(2)}, u32[]{:S(2)}) collective-permute-start(bf16[2,24,768]{2,1,0:T(8,128)(2,1)S(1)} %get-tuple-element.70), channel_id=1, source_target_pairs={{0,2},{1,3},{2,0},{3,1},{4,6},{5,7},{6,4},{7,5},{8,10},{9,11},{10,... | collective-permute-start | bytes 221192 | tf_op jit(solution)/shard_map/ppermute | solution.py:308
  61.0 7.0 %collective-permute-done.14.refs_1_ = bf16[2,24,768]{2,1,0:T(8,128)(2,1)S(1)} collective-permute-done((bf16[2,24,768]{2,1,0:T(8,128)(2,1)S(1)}, bf16[2,24,768]{2,1,0:T(8,128)(2,1)S(1)}, u32[]{:S(2)}, u32[]{:S(2)}) %collective-permute-start.14) | collective-permute-done | bytes 73760 | tf_op jit(solution)/shard_map/ppermute | solution.py:308
  68.0 0.6 collective-permute-start.15
  68.6 0.0 collective-permute-done.6.refs_1_.refs_2_
  68.6 0.0 collective-permute-done.7.refs_2_.refs_3_
  68.6 0.0 collective-permute-done.8.refs_3_.refs_4_
  68.6 4.8 %collective-permute-done.15.refs_1_ = bf16[2,24,768]{2,1,0:T(8,128)(2,1)S(1)} collective-permute-done((bf16[2,24,768]{2,1,0:T(8,128)(2,1)S(1)}, bf16[2,24,768]{2,1,0:T(8,128)(2,1)S(1)}, u32[]{:S(2)}, u32[]{:S(2)}) %collective-permute-start.15) | collective-permute-done | bytes 73760 | tf_op jit(solution)/shard_map/ppermute | solution.py:308
  73.4 3.2 %collective-permute-start.18 = (bf16[2,24,768]{2,1,0:T(8,128)(2,1)S(1)}, bf16[2,24,768]{2,1,0:T(8,128)(2,1)S(1)}, u32[]{:S(2)}, u32[]{:S(2)}) collective-permute-start(bf16[2,24,768]{2,1,0:T(8,128)(2,1)S(1)} %shard_map.110.refs_0_), channel_id=1, source_target_pairs={{0,3},{1,2},{2,1},{3,0},{4,7},{5,6},{6,5},{7,4},{8,11},{9,10},{10,... | collective-permute-start | bytes 221192 | tf_op jit(solution)/shard_map/ppermute | solution.py:308
  76.6 0.0 collective-permute-start.17
  76.6 0.6 collective-permute-start.16
  77.3 1.0 %shard_map.106 = bf16[1024,384]{1,0:T(8,128)(2,1)} custom-call(bf16[256,384]{1,0:T(8,128)(2,1)S(1)} %get-tuple-element.57.refs_0_, bf16[256,384]{1,0:T(8,128)(2,1)S(1)} %collective-permute-done.6.refs_1_.refs_2_, bf16[256,384]{1,0:T(8,128)(2,1)S(1)} %collective-permute-done.7.refs_2_.refs_3_, bf16[256,384]{1,0:T(8,128)(2,1)S(1)} %collective-permute-done.8.refs_3_.refs_4_), custom_call_target="tpu_custom_call" | custom-call | tf_op jit(solution)/shard_map/pallas_call | solution.py:59
  78.2 0.8 %collective-permute-done.18.refs_3_ = bf16[2,24,768]{2,1,0:T(8,128)(2,1)S(1)} collective-permute-done((bf16[2,24,768]{2,1,0:T(8,128)(2,1)S(1)}, bf16[2,24,768]{2,1,0:T(8,128)(2,1)S(1)}, u32[]{:S(2)}, u32[]{:S(2)}) %collective-permute-start.18) | collective-permute-done | bytes 73760 | tf_op jit(solution)/shard_map/ppermute | solution.py:308
  79.1 1.9 %collective-permute-done.17.refs_2_ = bf16[2,24,768]{2,1,0:T(8,128)(2,1)S(1)} collective-permute-done((bf16[2,24,768]{2,1,0:T(8,128)(2,1)S(1)}, bf16[2,24,768]{2,1,0:T(8,128)(2,1)S(1)}, u32[]{:S(2)}, u32[]{:S(2)}) %collective-permute-start.17) | collective-permute-done | bytes 73760 | tf_op jit(solution)/shard_map/ppermute | solution.py:308
  81.0 0.0 collective-permute-done.16.refs_1_
  81.0 1.1 %shard_map.111 = (f32[3,96,192]{2,1,0:T(8,128)}, f32[192,96]{1,0:T(8,128)}, f32[3,96,192]{2,1,0:T(8,128)}, f32[192,96]{1,0:T(8,128)}) custom-call(bf16[2,24,768]{2,1,0:T(8,128)(2,1)S(1)} %shard_map.110.refs_0_, bf16[2,24,768]{2,1,0:T(8,128)(2,1)S(1)} %collective-permute-done.16.refs_1_, bf16[2,24,768]{2,1,0:T(8,128)(2,1)S(1)} %collective-permute-done.17.refs_2_, ...), custom_call_target="tpu_custom_call" | custom-call | tf_op jit(solution)/shard_map/pallas_call | solution.py:59
  (2 shorter events, 0.0 us)
Async XLA Ops:
  0.6 1.1 %copy-start.2 = (bf16[1,1024,384]{2,1,0:T(8,128)(2,1)S(1)}, bf16[1,1024,384]{2,1,0:T(8,128)(2,1)}, u32[]{:S(2)}) copy-start(bf16[1,1024,384]{2,1,0:T(8,128)(2,1)} %param.6) | copy-start | bytes 2359300
  1.8 18.6 %copy-start.3 = (bf16[1,1024,384]{2,1,0:T(8,128)(2,1)S(1)}, bf16[1,1024,384]{2,1,0:T(8,128)(2,1)}, u32[]{:S(2)}) copy-start(bf16[1,1024,384]{2,1,0:T(8,128)(2,1)} %param.7) | copy-start | bytes 2359300
  1.8 11.0 %collective-permute-start = (bf16[256,384]{1,0:T(8,128)(2,1)S(1)}, bf16[256,384]{1,0:T(8,128)(2,1)S(1)}, u32[]{:S(2)}, u32[]{:S(2)}) collective-permute-start(bf16[256,384]{1,0:T(8,128)(2,1)S(1)} %get-tuple-element.40), channel_id=1, source_target_pairs={{0,2},{1,3},{2,4},{3,5},{4,6},{5,7},{6,0},{7,1},{8,10},{9,11},{10,... | collective-permute-start | bytes 589832 | tf_op jit(solution)/shard_map/ppermute | solution.py:298
  4.9 15.5 %collective-permute-start.1 = (bf16[256,384]{1,0:T(8,128)(2,1)S(1)}, bf16[256,384]{1,0:T(8,128)(2,1)S(1)}, u32[]{:S(2)}, u32[]{:S(2)}) collective-permute-start(bf16[256,384]{1,0:T(8,128)(2,1)S(1)} %get-tuple-element.41), channel_id=1, source_target_pairs={{0,4},{1,5},{2,6},{3,7},{4,0},{5,1},{6,2},{7,3},{8,12},{9,13},{10,... | collective-permute-start | bytes 589832 | tf_op jit(solution)/shard_map/ppermute | solution.py:298
  7.5 19.7 %collective-permute-start.5 = (bf16[256,384]{1,0:T(8,128)(2,1)S(1)}, bf16[256,384]{1,0:T(8,128)(2,1)S(1)}, u32[]{:S(2)}, u32[]{:S(2)}) collective-permute-start(bf16[256,384]{1,0:T(8,128)(2,1)S(1)} %get-tuple-element.47), channel_id=1, source_target_pairs={{0,6},{1,7},{2,0},{3,1},{4,2},{5,3},{6,4},{7,5},{8,14},{9,15},{10,... | collective-permute-start | bytes 589832 | tf_op jit(solution)/shard_map/ppermute | solution.py:298
  20.4 6.9 %copy-start = (bf16[3,384,192]{1,2,0:T(8,128)(2,1)S(1)}, bf16[3,384,192]{1,2,0:T(8,128)(2,1)}, u32[]{:S(2)}) copy-start(bf16[3,384,192]{1,2,0:T(8,128)(2,1)} %param.10) | copy-start | bytes 1327108
  20.4 6.9 %copy-start.1 = (bf16[3,384,192]{1,2,0:T(8,128)(2,1)S(1)}, bf16[3,384,192]{1,2,0:T(8,128)(2,1)}, u32[]{:S(2)}) copy-start(bf16[3,384,192]{1,2,0:T(8,128)(2,1)} %param.8) | copy-start | bytes 1327108
  20.4 6.9 %copy-start.4 = (bf16[192,384]{1,0:T(8,128)(2,1)S(1)}, bf16[192,384]{1,0:T(8,128)(2,1)}, u32[]{:S(2)}) copy-start(bf16[192,384]{1,0:T(8,128)(2,1)} %refs_6_.1) | copy-start | bytes 442372
  20.5 15.5 %collective-permute-start.2 = (bf16[256,384]{1,0:T(8,128)(2,1)S(1)}, bf16[256,384]{1,0:T(8,128)(2,1)S(1)}, u32[]{:S(2)}, u32[]{:S(2)}) collective-permute-start(bf16[256,384]{1,0:T(8,128)(2,1)S(1)} %get-tuple-element.43), channel_id=1, source_target_pairs={{0,2},{1,3},{2,4},{3,5},{4,6},{5,7},{6,0},{7,1},{8,10},{9,11},{10,... | collective-permute-start | bytes 589832 | tf_op jit(solution)/shard_map/ppermute | solution.py:298
  23.9 15.0 %collective-permute-start.3 = (bf16[256,384]{1,0:T(8,128)(2,1)S(1)}, bf16[256,384]{1,0:T(8,128)(2,1)S(1)}, u32[]{:S(2)}, u32[]{:S(2)}) collective-permute-start(bf16[256,384]{1,0:T(8,128)(2,1)S(1)} %get-tuple-element.44), channel_id=1, source_target_pairs={{0,4},{1,5},{2,6},{3,7},{4,0},{5,1},{6,2},{7,3},{8,12},{9,13},{10,... | collective-permute-start | bytes 589832 | tf_op jit(solution)/shard_map/ppermute | solution.py:298
  27.2 11.6 %collective-permute-start.4 = (bf16[256,384]{1,0:T(8,128)(2,1)S(1)}, bf16[256,384]{1,0:T(8,128)(2,1)S(1)}, u32[]{:S(2)}, u32[]{:S(2)}) collective-permute-start(bf16[256,384]{1,0:T(8,128)(2,1)S(1)} %get-tuple-element.45), channel_id=1, source_target_pairs={{0,6},{1,7},{2,0},{3,1},{4,2},{5,3},{6,4},{7,5},{8,14},{9,15},{10,... | collective-permute-start | bytes 589832 | tf_op jit(solution)/shard_map/ppermute | solution.py:298
  27.3 11.6 %copy-start.5 = (bf16[192,384]{1,0:T(8,128)(2,1)S(1)}, bf16[192,384]{1,0:T(8,128)(2,1)}, u32[]{:S(2)}) copy-start(bf16[192,384]{1,0:T(8,128)(2,1)} %refs_9_.1) | copy-start | bytes 442372
  43.6 1.6 %collective-permute-start.10 = (bf16[2,96,768]{2,1,0:T(8,128)(2,1)S(1)}, bf16[2,96,768]{2,1,0:T(8,128)(2,1)S(1)}, u32[]{:S(2)}, u32[]{:S(2)}) collective-permute-start(bf16[2,96,768]{2,1,0:T(8,128)(2,1)S(1)} %get-tuple-element.64), channel_id=1, source_target_pairs={{0,8},{1,9},{2,10},{3,11},{4,12},{5,13},{6,14},{7,15},{8,0},{9,1},... | collective-permute-start | bytes 884744 | tf_op jit(solution)/shard_map/ppermute | solution.py:308
  43.7 2.0 %collective-permute-start.9 = (bf16[2,96,768]{2,1,0:T(8,128)(2,1)S(1)}, bf16[2,96,768]{2,1,0:T(8,128)(2,1)S(1)}, u32[]{:S(2)}, u32[]{:S(2)}) collective-permute-start(bf16[2,96,768]{2,1,0:T(8,128)(2,1)S(1)} %get-tuple-element.62), channel_id=1, source_target_pairs={{0,8},{1,9},{2,10},{3,11},{4,12},{5,13},{6,14},{7,15},{8,0},{9,1},... | collective-permute-start | bytes 884744 | tf_op jit(solution)/shard_map/ppermute | solution.py:308
  45.8 8.3 %collective-permute-start.11 = (bf16[2,48,768]{2,1,0:T(8,128)(2,1)S(1)}, bf16[2,48,768]{2,1,0:T(8,128)(2,1)S(1)}, u32[]{:S(2)}, u32[]{:S(2)}) collective-permute-start(bf16[2,48,768]{2,1,0:T(8,128)(2,1)S(1)} %get-tuple-element.66), channel_id=1, source_target_pairs={{0,1},{1,0},{2,3},{3,2},{4,5},{5,4},{6,7},{7,6},{8,9},{9,8},{10,11... | collective-permute-start | bytes 442376 | tf_op jit(solution)/shard_map/ppermute | solution.py:308
  47.4 9.0 %collective-permute-start.12 = (bf16[2,48,768]{2,1,0:T(8,128)(2,1)S(1)}, bf16[2,48,768]{2,1,0:T(8,128)(2,1)S(1)}, u32[]{:S(2)}, u32[]{:S(2)}) collective-permute-start(bf16[2,48,768]{2,1,0:T(8,128)(2,1)S(1)} %get-tuple-element.67), channel_id=1, source_target_pairs={{0,16},{1,17},{2,18},{3,19},{4,20},{5,21},{6,22},{7,23},{8,24},{9,... | collective-permute-start | bytes 442376 | tf_op jit(solution)/shard_map/ppermute | solution.py:308
  48.9 7.5 %collective-permute-start.13 = (bf16[2,48,768]{2,1,0:T(8,128)(2,1)S(1)}, bf16[2,48,768]{2,1,0:T(8,128)(2,1)S(1)}, u32[]{:S(2)}, u32[]{:S(2)}) collective-permute-start(bf16[2,48,768]{2,1,0:T(8,128)(2,1)S(1)} %get-tuple-element.68), channel_id=1, source_target_pairs={{0,17},{1,16},{2,19},{3,18},{4,21},{5,20},{6,23},{7,22},{8,25},{9,... | collective-permute-start | bytes 442376 | tf_op jit(solution)/shard_map/ppermute | solution.py:308
  49.4 19.2 %collective-permute-start.6 = (bf16[256,384]{1,0:T(8,128)(2,1)S(1)}, bf16[256,384]{1,0:T(8,128)(2,1)S(1)}, u32[]{:S(2)}, u32[]{:S(2)}) collective-permute-start(bf16[256,384]{1,0:T(8,128)(2,1)S(1)} %get-tuple-element.58), channel_id=1, source_target_pairs={{0,2},{1,3},{2,4},{3,5},{4,6},{5,7},{6,0},{7,1},{8,10},{9,11},{10,... | collective-permute-start | bytes 589832 | tf_op jit(solution)/shard_map/ppermute | solution.py:298
  54.1 14.5 %collective-permute-start.7 = (bf16[256,384]{1,0:T(8,128)(2,1)S(1)}, bf16[256,384]{1,0:T(8,128)(2,1)S(1)}, u32[]{:S(2)}, u32[]{:S(2)}) collective-permute-start(bf16[256,384]{1,0:T(8,128)(2,1)S(1)} %get-tuple-element.59), channel_id=1, source_target_pairs={{0,4},{1,5},{2,6},{3,7},{4,0},{5,1},{6,2},{7,3},{8,12},{9,13},{10,... | collective-permute-start | bytes 589832 | tf_op jit(solution)/shard_map/ppermute | solution.py:298
  54.1 14.5 %collective-permute-start.8 = (bf16[256,384]{1,0:T(8,128)(2,1)S(1)}, bf16[256,384]{1,0:T(8,128)(2,1)S(1)}, u32[]{:S(2)}, u32[]{:S(2)}) collective-permute-start(bf16[256,384]{1,0:T(8,128)(2,1)S(1)} %get-tuple-element.60), channel_id=1, source_target_pairs={{0,6},{1,7},{2,0},{3,1},{4,2},{5,3},{6,4},{7,5},{8,14},{9,15},{10,... | collective-permute-start | bytes 589832 | tf_op jit(solution)/shard_map/ppermute | solution.py:298
  56.6 11.4 %collective-permute-start.14 = (bf16[2,24,768]{2,1,0:T(8,128)(2,1)S(1)}, bf16[2,24,768]{2,1,0:T(8,128)(2,1)S(1)}, u32[]{:S(2)}, u32[]{:S(2)}) collective-permute-start(bf16[2,24,768]{2,1,0:T(8,128)(2,1)S(1)} %get-tuple-element.70), channel_id=1, source_target_pairs={{0,2},{1,3},{2,0},{3,1},{4,6},{5,7},{6,4},{7,5},{8,10},{9,11},{10,... | collective-permute-start | bytes 221192 | tf_op jit(solution)/shard_map/ppermute | solution.py:308
  68.0 5.4 %collective-permute-start.15 = (bf16[2,24,768]{2,1,0:T(8,128)(2,1)S(1)}, bf16[2,24,768]{2,1,0:T(8,128)(2,1)S(1)}, u32[]{:S(2)}, u32[]{:S(2)}) collective-permute-start(bf16[2,24,768]{2,1,0:T(8,128)(2,1)S(1)} %shard_map.109.refs_0_), channel_id=1, source_target_pairs={{0,4},{1,5},{2,6},{3,7},{4,0},{5,1},{6,2},{7,3},{8,12},{9,13},{10,... | collective-permute-start | bytes 221192 | tf_op jit(solution)/shard_map/ppermute | solution.py:308
  73.4 5.7 %collective-permute-start.18 = (bf16[2,24,768]{2,1,0:T(8,128)(2,1)S(1)}, bf16[2,24,768]{2,1,0:T(8,128)(2,1)S(1)}, u32[]{:S(2)}, u32[]{:S(2)}) collective-permute-start(bf16[2,24,768]{2,1,0:T(8,128)(2,1)S(1)} %shard_map.110.refs_0_), channel_id=1, source_target_pairs={{0,3},{1,2},{2,1},{3,0},{4,7},{5,6},{6,5},{7,4},{8,11},{9,10},{10,... | collective-permute-start | bytes 221192 | tf_op jit(solution)/shard_map/ppermute | solution.py:308
  76.6 4.4 %collective-permute-start.17 = (bf16[2,24,768]{2,1,0:T(8,128)(2,1)S(1)}, bf16[2,24,768]{2,1,0:T(8,128)(2,1)S(1)}, u32[]{:S(2)}, u32[]{:S(2)}) collective-permute-start(bf16[2,24,768]{2,1,0:T(8,128)(2,1)S(1)} %shard_map.110.refs_0_), channel_id=1, source_target_pairs={{0,2},{1,3},{2,0},{3,1},{4,6},{5,7},{6,4},{7,5},{8,10},{9,11},{10,... | collective-permute-start | bytes 221192 | tf_op jit(solution)/shard_map/ppermute | solution.py:308
  76.6 4.4 %collective-permute-start.16 = (bf16[2,24,768]{2,1,0:T(8,128)(2,1)S(1)}, bf16[2,24,768]{2,1,0:T(8,128)(2,1)S(1)}, u32[]{:S(2)}, u32[]{:S(2)}) collective-permute-start(bf16[2,24,768]{2,1,0:T(8,128)(2,1)S(1)} %shard_map.110.refs_0_), channel_id=1, source_target_pairs={{0,1},{1,0},{2,3},{3,2},{4,5},{5,4},{6,7},{7,6},{8,9},{9,8},{10,11... | collective-permute-start | bytes 221192 | tf_op jit(solution)/shard_map/ppermute | solution.py:308

commit v3 on v2

v3 whole, which is shorter than its diff:
```python
import functools
import math

import jax
import jax.numpy as jnp
from jax import lax
from jax.experimental import pallas as pl
from jax.experimental.pallas import tpu as pltpu
from jax.sharding import PartitionSpec as P

DILATION_ONE = 2048
DILATION_TWO = 4096
TILE = 256
CHUNK = 32
MAX_PERMUTES = 8
NEED = ((1,), (2,), (3,))
GATE = (1, 2,)
BF16 = jnp.bfloat16
F32 = jnp.float32
VMEM = pl.BlockSpec(memory_space=pltpu.VMEM)
ANY = pl.BlockSpec(memory_space=pl.ANY)


def gelu_parts(values):
    coeff = math.sqrt(2.0 / math.pi)
    square = values * values
    tanh_val = jnp.tanh(values * (coeff + (coeff * 0.044715) * square))
    half = 0.5 + 0.5 * tanh_val
    slope = half + half * (1.0 - tanh_val) * (values * (coeff + (3.0 * coeff * 0.044715) * square))
    return values * half, slope


def dot(left, right):
    return jnp.dot(left, right, preferred_element_type=F32)


def dot_nt(left, right):
    return lax.dot_general(left, right, (((1,), (1,)), ((), ())), preferred_element_type=F32)


def position(hop):
    return lax.axis_index("seq") // hop


def behind(me, k, count):
    return lax.rem(me + (count - k), count)


def ahead(me, k, count):
    return lax.rem(me + k, count)


def call(kernel, out_shapes, scratch, args, after=(), mib=8):
    n_args, n_after = len(args), len(after)

    def body(*refs):
        kernel(*refs[:n_args], *refs[n_args + n_after :])

    return pl.pallas_call(
        body,
        out_shape=[jax.ShapeDtypeStruct(s, d) for s, d in out_shapes],
        in_specs=[VMEM] * n_args + [ANY] * n_after,
        out_specs=[VMEM] * len(out_shapes),
        scratch_shapes=[pltpu.VMEM(s, d) for s, d in scratch],
        compiler_params=pltpu.CompilerParams(vmem_limit_bytes=mib << 20),
    )(*args, *after)


def cut_kernel(hop, block, *pieces):
    count = len(pieces)
    size = pieces[0].shape[0]
    me = position(hop)
    for k, piece in enumerate(pieces):
        at = pl.multiple_of(ahead(me, k, count) * size, size)
        piece[...] = block[pl.ds(at, size), :]


def place(parts, rows_ref, hop):
    if len(parts) == 1:
        rows_ref[...] = parts[0][...]
        return
    count = len(parts)
    size = rows_ref.shape[0] // count
    me = position(hop)
    for k, part in enumerate(parts):
        at = pl.multiple_of(behind(me, k, count) * size, size)
        rows_ref[pl.ds(at, size), :] = part[...]


def hand_out(rows_ref, parts, hop):
    if len(parts) == 1:
        parts[0][...] = rows_ref[...]
        return
    count = len(parts)
    size = rows_ref.shape[0] // count
    me = position(hop)
    for k, part in enumerate(parts):
        at = pl.multiple_of(ahead(me, k, count) * size, size)
        part[...] = rows_ref[pl.ds(at, size), :]


def tap_sum(padded_ref, shift, start, tile, weight_of, mm):
    total = mm(padded_ref[pl.ds(start + shift, tile), :], weight_of(1))
    rows = padded_ref.shape[0] - 2 * shift
    if start + tile > shift:
        total = total + mm(padded_ref[pl.ds(start, tile), :], weight_of(0))
    if start < rows - shift:
        total = total + mm(padded_ref[pl.ds(start + 2 * shift, tile), :], weight_of(2))
    return total


def clear_edges(padded_ref, shift):
    rows = padded_ref.shape[0]
    zeros = jnp.zeros((shift, padded_ref.shape[1]), padded_ref.dtype)
    padded_ref[pl.ds(0, shift), :] = zeros
    padded_ref[pl.ds(rows - shift, shift), :] = zeros


def forward_kernel(shifts, hop, count, *refs):
    parts = refs[:count]
    weights = refs[count : count + 3]
    outs = refs[count + 3 : count + 11]
    scratch = refs[count + 11 :]
    place(parts, scratch[0], hop)
    forward_rows(shifts, weights, outs, scratch)


def forward_rows(shifts, weights, outs, scratch):
    k1t, p1, k2t = weights
    act1_t, mid1_t, s_x, s_p1, act2_t, mid2_t, s_h, s_p2 = outs
    x_rows, pad1, pad2, wide, narrow = scratch
    rows = x_rows.shape[0]

    def activate(source, source_start, pad, shift, start, slope_ref):
        def step(i, carry):
            at = pl.multiple_of(i * CHUNK, CHUNK)
            value, slope = gelu_parts(source[pl.ds(source_start + at, CHUNK), :].astype(F32))
            pad[pl.ds(start + shift + at, CHUNK), :] = value.astype(BF16)
            slope_ref[pl.ds(start + at, CHUNK), :] = slope
            return carry

        lax.fori_loop(0, TILE // CHUNK, step, 0, unroll=2)

    def narrow_gelu(start, slope_ref):
        def step(i, carry):
            at = pl.multiple_of(i * CHUNK, CHUNK)
            value, slope = gelu_parts(narrow[pl.ds(at, CHUNK), :])
            narrow[pl.ds(at, CHUNK), :] = value
            slope_ref[pl.ds(start + at, CHUNK), :] = slope
            return carry

        lax.fori_loop(0, TILE // CHUNK, step, 0, unroll=2)

    clear_edges(pad1, shifts[0])
    clear_edges(pad2, shifts[1])
    for start in range(0, rows, TILE):
        activate(x_rows, start, pad1, shifts[0], start, s_x)
        act1_t[:, pl.ds(start, TILE)] = pad1[pl.ds(start + shifts[0], TILE), :].T
    for start in range(0, rows, TILE):
        narrow[...] = tap_sum(pad1, shifts[0], start, TILE, lambda k: k1t[k], dot_nt)
        narrow_gelu(start, s_p1)
        mid = narrow[...].astype(BF16)
        mid1_t[:, pl.ds(start, TILE)] = mid.T
        wide[...] = (x_rows[pl.ds(start, TILE), :].astype(F32) + dot(mid, p1[...])).astype(BF16)
        activate(wide, 0, pad2, shifts[1], start, s_h)
        act2_t[:, pl.ds(start, TILE)] = pad2[pl.ds(start + shifts[1], TILE), :].T
    for start in range(0, rows, TILE):
        narrow[...] = tap_sum(pad2, shifts[1], start, TILE, lambda k: k2t[k], dot_nt)
        narrow_gelu(start, s_p2)
        mid2_t[:, pl.ds(start, TILE)] = narrow[...].astype(BF16).T


def chain_kernel(shifts, hop, n_in, n_out, *refs):
    parts = refs[:n_in]
    s_x, s_p1, s_h, s_p2, k1t, p1, k2t, p2 = refs[n_in : n_in + 8]
    outs = refs[n_in + 8 : n_in + 8 + n_out]
    g2_rows, pad2, g1_rows, pad1, x_rows = refs[n_in + 8 + n_out :]
    place(parts, g2_rows, hop)
    backward_rows(shifts[1], g2_rows, pad2, s_p2, s_h, k2t, p2, g1_rows)
    backward_rows(shifts[0], g1_rows, pad1, s_p1, s_x, k1t, p1, x_rows)
    hand_out(x_rows, outs, hop)


def backward_rows(shift, g_rows, pad, s_pre, s_state, kt, point, x_rows):
    rows = g_rows.shape[0]
    clear_edges(pad, shift)
    for start in range(0, rows, TILE):
        mid_grad = dot_nt(g_rows[pl.ds(start, TILE), :], point[...])
        pad[pl.ds(start + shift, TILE), :] = (mid_grad * s_pre[pl.ds(start, TILE), :]).astype(BF16)
    for start in range(0, rows, TILE):
        act_grad = tap_sum(pad, shift, start, TILE, lambda k: kt[2 - k], dot)
        x_rows[pl.ds(start, TILE), :] = (
            g_rows[pl.ds(start, TILE), :].astype(F32) + act_grad * s_state[pl.ds(start, TILE), :]
        ).astype(BF16)


def weights_kernel(shifts, *refs):
    keep, send, grads = refs[-3:]
    size = keep.shape[2]
    core = lax.rem(lax.axis_index("dp"), 2)
    for i, shift in enumerate(shifts):
        act_t, mid_t, pad, g_rows = refs[4 * i : 4 * i + 4]
        rows = g_rows.shape[0]
        act = act_t[...]
        grads[...] = jnp.concatenate(
            [
                dot(act, pad[pl.ds(2 * shift, rows), :]),
                dot(act, pad[pl.ds(shift, rows), :]),
                dot(act, pad[pl.ds(0, rows), :]),
                dot(mid_t[...], g_rows[...]).T,
            ],
            axis=1,
        )
        for x_to in range(2):
            for target, parity in ((keep, core), (send, 1 - core)):
                rows_at = pl.multiple_of((2 * x_to + parity) * size, size)
                target[i, x_to] = grads[pl.ds(rows_at, size), :].astype(target.dtype)


def split_kernel(keep, received, *pieces):
    x_at = lax.axis_index("dp") // 2
    y_at = lax.rem(lax.axis_index("seq"), 2)
    size = pieces[0].shape[1]
    for k, piece in enumerate(pieces):
        x_to = lax.rem(x_at + k // 2, 2)
        rows = pl.ds(pl.multiple_of(lax.rem(y_at + k, 2) * size, size), size)
        for i in range(keep.shape[0]):
            total = keep[i, x_to, rows, :].astype(F32) + received[i, x_to, rows, :].astype(F32)
            piece[i] = total.astype(piece.dtype)


def sum_of(refs):
    total = refs[0][...].astype(F32)
    for ref in refs[1:]:
        total = total + ref[...].astype(F32)
    return total


def sum_kernel(*refs):
    refs[-1][...] = sum_of(refs[:-1]).astype(refs[-1].dtype)


def halve_kernel(hop, *refs):
    *parts, keep, send, total = refs
    total[...] = sum_of(parts)
    size = keep.shape[1]
    mine = lax.rem(position(hop), 2)
    for target, half in ((keep, mine), (send, 1 - mine)):
        target[...] = total[:, pl.ds(pl.multiple_of(half * size, size), size), :].astype(target.dtype)


def finish_kernel(scale, hop, n_blocks, *refs):
    parts, outs, rows = refs[: -2 * n_blocks - 1], refs[-2 * n_blocks - 1 : -1], refs[-1]
    z_at = lax.rem(position(hop), 2)
    y_at = lax.rem(lax.axis_index("seq"), 2)
    size = parts[0].shape[1]
    per_y = rows.shape[1] // 2
    for k, part in enumerate(parts):
        at = lax.rem(y_at + k, 2) * per_y
        if len(parts) > 2:
            at = at + lax.rem(z_at + k // 2, 2) * size
        rows[:, pl.ds(pl.multiple_of(at, size), size), :] = part[...].astype(F32) * scale
    for i in range(n_blocks):
        conv, point = outs[2 * i : 2 * i + 2]
        width = conv.shape[2]
        whole = rows[i]
        for k in range(3):
            conv[k] = whole[:, k * width : (k + 1) * width]
        point[...] = whole[:, 3 * width :].T


def collect_kernel(hop, *refs):
    place(refs[:-1], refs[-1], hop)


def send_ahead(block, hop, k):
    size = lax.axis_size("seq")
    count = size // hop
    route = [(i, ((i // hop + k) % count) * hop + i % hop) for i in range(size)]
    return lax.ppermute(block, "seq", route)


def mirrored(block, dp_bits, seq_bits):
    n_dp, n_seq = lax.axis_size("dp"), lax.axis_size("seq")
    route = [
        (i * n_seq + j, (i ^ dp_bits) * n_seq + (j ^ seq_bits))
        for i in range(n_dp)
        for j in range(n_seq)
    ]
    return lax.ppermute(block, ("dp", "seq"), route)


def column_groups(hop):
    size = lax.axis_size("seq")
    return [list(range(first, size, hop)) for first in range(hop)]


def exchange_all(block, hop):
    count = lax.axis_size("seq") // hop
    cut = block.reshape(count, -1, block.shape[-1])
    swapped = lax.all_to_all(cut, "seq", 0, 0, axis_index_groups=column_groups(hop), tiled=True)
    return swapped.reshape(block.shape)


def to_columns(block, hop, after=()):
    count = lax.axis_size("seq") // hop
    rows, channels = block.shape
    if count > MAX_PERMUTES:
        return [exchange_all(block, hop)]
    pieces = call(
        functools.partial(cut_kernel, hop), [((rows // count, channels), BF16)] * count, [], [block], mib=2
    )
    if after:
        pieces, _ = lax.optimization_barrier((pieces, list(after)))
    return forward_pieces(pieces, hop)


def forward_pieces(pieces, hop):
    return [pieces[0]] + [send_ahead(pieces[k], hop, k) for k in range(1, len(pieces))]


def once(block, after):
    return lax.optimization_barrier((block, after))[0]


def reduce_weights(keep, send, grads, hop, scale):
    n_blocks, _, rows, lanes = keep.shape
    width = lanes // 4
    count = lax.axis_size("seq") // hop
    half = (n_blocks, rows // 2, lanes)
    fourth = (n_blocks, rows // 4, lanes)
    received = mirrored(send, 1, 0)
    back = dict.fromkeys(range(count))

    def send_home(ks, after=None):
        for k in ks:
            back[k] = send_ahead(grads[k] if after is None else once(grads[k], after), hop, k)
        return [back[k] for k in ks]

    if count == 4:
        back[0] = grads[0]
        send_home((1, 2, 3))
    pieces = call(split_kernel, [(half, F32)] + [(half, BF16)] * 3, [], [keep, received])
    arrived = [pieces[0]] + [mirrored(pieces[k], 2 * (k // 2), k % 2) for k in range(1, 4)]
    if count == 4:
        keep, send = call(
            functools.partial(halve_kernel, hop), [(fourth, F32), (fourth, BF16)], [(half, F32)], arrived,
            [back[k] for k in NEED[0]],
        )
        (pair,) = call(sum_kernel, [(fourth, BF16)], [], [keep, mirrored(send, 0, hop)], [back[k] for k in NEED[1]])
        (own,) = call(sum_kernel, [(fourth, BF16)], [], [pair, mirrored(pair, 0, 2 * hop)], [back[k] for k in NEED[2]])
        parts = [own] + [mirrored(own, 0, hop * (k // 2) + k % 2) for k in range(1, 4)]
        back = [back[k] for k in range(count)]
    else:
        (plane,) = call(sum_kernel, [(half, F32)], [], arrived)
        own = lax.psum(plane, "seq", axis_index_groups=column_groups(hop)).astype(BF16)
        parts = [own, mirrored(own, 0, 1)]
        back = [exchange_all(grads[0], hop)] if len(grads) == 1 else forward_pieces(grads, hop)
    outs = call(
        functools.partial(finish_kernel, scale, hop, n_blocks),
        [((3, rows, width), F32), ((width, rows), F32)] * n_blocks,
        [((n_blocks, rows, lanes), F32)],
        parts,
    )
    return back, [outs[2 * i : 2 * i + 2] for i in range(n_blocks)]


def shards(
    inputs,
    cotangent,
    first_dilated_kernel,
    first_pointwise_weight,
    second_dilated_kernel,
    second_pointwise_weight,
):
    samples, rows, channels = inputs.shape
    width = first_pointwise_weight.shape[0]
    hop = DILATION_ONE // rows
    size = rows // (lax.axis_size("seq") // hop)
    shifts = (size, size * (DILATION_TWO // DILATION_ONE))
    total_rows = samples * lax.axis_size("dp") * rows * lax.axis_size("seq")
    scale = 1.0 / math.sqrt(total_rows)
    k1t = jnp.swapaxes(first_dilated_kernel, 1, 2)
    k2t = jnp.swapaxes(second_dilated_kernel, 1, 2)
    p1, p2 = first_pointwise_weight, second_pointwise_weight

    x_parts = to_columns(inputs.reshape(rows, channels), hop)
    g_parts = to_columns(cotangent.reshape(rows, channels), hop, [x_parts[k] for k in GATE if k < len(x_parts)])
    n_parts = len(x_parts)
    whole = ((rows, channels), BF16)
    pads = [((rows + 2 * shift, width), BF16) for shift in shifts]
    state = [((channels, rows), BF16), ((width, rows), BF16), ((rows, channels), F32), ((rows, width), F32)]
    act1_t, mid1_t, s_x, s_p1, act2_t, mid2_t, s_h, s_p2 = call(
        functools.partial(forward_kernel, shifts, hop, n_parts),
        state * 2,
        [
            whole,
            ((rows + 2 * shifts[0], channels), BF16),
            ((rows + 2 * shifts[1], channels), BF16),
            ((TILE, channels), BF16),
            ((TILE, width), F32),
        ],
        list(x_parts) + [k1t, p1, k2t],
        mib=16,
    )
    *x_grads, g2_rows, pad2, g1_rows, pad1 = call(
        functools.partial(chain_kernel, shifts, hop, n_parts, n_parts),
        [(x_parts[0].shape, BF16)] * n_parts + [whole, pads[1], whole, pads[0]],
        [whole],
        list(g_parts) + [s_x, s_p1, s_h, s_p2, k1t, p1, k2t, p2],
        mib=16,
    )
    quarters = ((2, 2, channels // 4, 4 * width), BF16)
    keep, send = call(
        functools.partial(weights_kernel, (shifts[1], shifts[0])),
        [quarters, quarters],
        [((channels, 4 * width), F32)],
        [act2_t, mid2_t, pad2, g2_rows, act1_t, mid1_t, pad1, g1_rows],
        mib=16,
    )
    back, ((conv2, point2), (conv1, point1)) = reduce_weights(keep, send, x_grads, hop, scale)
    if n_parts == 1:
        (input_grad,) = back
    else:
        (input_grad,) = call(functools.partial(collect_kernel, hop), [whole], [], back)
    return input_grad.reshape(inputs.shape), conv1, point1, conv2, point2


def solution(mesh):
    return jax.shard_map(
        shards,
        mesh=mesh,
        in_specs=(P("dp", "seq", None), P("dp", "seq", None), P(), P(), P(), P()),
        out_specs=(
            P("dp", "seq", None),
            P(None, "dp", None),
            P(None, "dp"),
            P(None, "dp", None),
            P(None, "dp"),
        ),
        check_vma=False,
    )
```

time: 82.2 us -> 79.9 us (0.972)
  waiting for transfers between devices: 30.4 us -> 24.3 us
  local copies, waits for them, and re-layouts: 1.15 us -> 3.25 us
  starting transfers between devices: 33.8 us -> 35.7 us
    ppermute x10 -> x9, waiting for transfers between devices: 16 us -> 7.63 us  [mirrored(): return lax.ppermute(block, ('dp', 'seq'), route)]
    ppermute x9, waiting for transfers between devices: 14.4 us -> 16.7 us  [send_ahead(): return lax.ppermute(block, 'seq', route)]
    unnamed x12, local copies, waits for them, and re-layouts: 1.15 us -> 3.25 us
    ppermute x9, starting transfers between devices: 20.8 us -> 22.3 us  [send_ahead(): return lax.ppermute(block, 'seq', route)]
    ppermute x10 -> x9, starting transfers between devices: 13 us -> 13.4 us  [mirrored(): return lax.ppermute(block, ('dp', 'seq'), route)]
  transfers between devices with their start and end apart: 19 -> 18, of which waited for: 9 -> 11; matrix products, arithmetic and copies ran while one was open for 0% -> 0% of each run, Pallas kernels for 12% -> 12%
where the time goes in v3:
time: 79.9 us; the launch traced here: 79.7 us
  starting transfers between devices  35.7 us (45%)
  waiting for transfers between devices  24.3 us (30%)
  Pallas kernels  15.6 us (20%)
  local copies, waits for them, and re-layouts  3.25 us (4%)
    ppermute x9, starting transfers between devices, send_ahead(): return lax.ppermute(block, 'seq', route)  22.3 us
    ppermute x9, waiting for transfers between devices, send_ahead(): return lax.ppermute(block, 'seq', route)  16.7 us
    pallas_call x11, Pallas kernels, call(): pl.pallas_call(body, out_shape=[jax.ShapeDtypeStruct(s, d) for s, d in ou...  15.6 us
    ppermute x9, starting transfers between devices, mirrored(): return lax.ppermute(block, ('dp', 'seq'), route)  13.4 us
    ppermute x9, waiting for transfers between devices, mirrored(): return lax.ppermute(block, ('dp', 'seq'), route)  7.63 us
    unnamed x12, local copies, waits for them, and re-layouts  3.25 us
  transfers between devices with their start and end apart: 18, of which 11 were waited for; matrix products, arithmetic and copies ran while one was open for 0% of the time, Pallas kernels for 12%

profile of v3, /device:TPU:0, one launch (start us, length us, event | category | flops | bytes accessed | tf_op | source)
XLA Modules:
  0.0 79.7 jit_solution(17717028394107481710)
XLA Ops:
  0.6 0.0 copy-start.1
  0.6 0.0 copy-start
  0.7 0.0 copy-start.2
  0.7 1.2 %copy-done.2 = bf16[1,1024,384]{2,1,0:T(8,128)(2,1)S(1)} copy-done((bf16[1,1024,384]{2,1,0:T(8,128)(2,1)S(1)}, bf16[1,1024,384]{2,1,0:T(8,128)(2,1)}, u32[]{:S(2)}) %copy-start.2) | copy-done | bytes 786456
  1.9 0.1 shard_map.102
  1.9 3.1 %collective-permute-start = (bf16[256,384]{1,0:T(8,128)(2,1)S(1)}, bf16[256,384]{1,0:T(8,128)(2,1)S(1)}, u32[]{:S(2)}, u32[]{:S(2)}) collective-permute-start(bf16[256,384]{1,0:T(8,128)(2,1)S(1)} %get-tuple-element.49), channel_id=1, source_target_pairs={{0,2},{1,3},{2,4},{3,5},{4,6},{5,7},{6,0},{7,1},{8,10},{9,11},{10,... | collective-permute-start | bytes 589832 | tf_op jit(solution)/shard_map/ppermute | solution.py:280
  5.0 2.6 %collective-permute-start.1 = (bf16[256,384]{1,0:T(8,128)(2,1)S(1)}, bf16[256,384]{1,0:T(8,128)(2,1)S(1)}, u32[]{:S(2)}, u32[]{:S(2)}) collective-permute-start(bf16[256,384]{1,0:T(8,128)(2,1)S(1)} %get-tuple-element.50), channel_id=1, source_target_pairs={{0,4},{1,5},{2,6},{3,7},{4,0},{5,1},{6,2},{7,3},{8,12},{9,13},{10,... | collective-permute-start | bytes 589832 | tf_op jit(solution)/shard_map/ppermute | solution.py:280
  7.6 1.3 %collective-permute-start.5 = (bf16[256,384]{1,0:T(8,128)(2,1)S(1)}, bf16[256,384]{1,0:T(8,128)(2,1)S(1)}, u32[]{:S(2)}, u32[]{:S(2)}) collective-permute-start(bf16[256,384]{1,0:T(8,128)(2,1)S(1)} %get-tuple-element.56), channel_id=1, source_target_pairs={{0,6},{1,7},{2,0},{3,1},{4,2},{5,3},{6,4},{7,5},{8,14},{9,15},{10,... | collective-permute-start | bytes 589832 | tf_op jit(solution)/shard_map/ppermute | solution.py:280
  8.9 0.0 copy-start.3
  9.0 1.1 %copy-done.3 = bf16[1,1024,384]{2,1,0:T(8,128)(2,1)S(1)} copy-done((bf16[1,1024,384]{2,1,0:T(8,128)(2,1)S(1)}, bf16[1,1024,384]{2,1,0:T(8,128)(2,1)}, u32[]{:S(2)}) %copy-start.3) | copy-done | bytes 786456
  10.1 0.0 copy-start.5
  10.1 0.1 shard_map.101
  10.2 2.7 %collective-permute-done.refs_1_ = bf16[256,384]{1,0:T(8,128)(2,1)S(1)} collective-permute-done((bf16[256,384]{1,0:T(8,128)(2,1)S(1)}, bf16[256,384]{1,0:T(8,128)(2,1)S(1)}, u32[]{:S(2)}, u32[]{:S(2)}) %collective-permute-start) | collective-permute-done | bytes 196640 | tf_op jit(solution)/shard_map/ppermute | solution.py:280
  12.9 7.6 %collective-permute-done.1.refs_2_ = bf16[256,384]{1,0:T(8,128)(2,1)S(1)} collective-permute-done((bf16[256,384]{1,0:T(8,128)(2,1)S(1)}, bf16[256,384]{1,0:T(8,128)(2,1)S(1)}, u32[]{:S(2)}, u32[]{:S(2)}) %collective-permute-start.1) | collective-permute-done | bytes 196640 | tf_op jit(solution)/shard_map/ppermute | solution.py:280
  20.5 3.5 %collective-permute-start.2 = (bf16[256,384]{1,0:T(8,128)(2,1)S(1)}, bf16[256,384]{1,0:T(8,128)(2,1)S(1)}, u32[]{:S(2)}, u32[]{:S(2)}) collective-permute-start(bf16[256,384]{1,0:T(8,128)(2,1)S(1)} %get-tuple-element.52), channel_id=1, source_target_pairs={{0,2},{1,3},{2,4},{3,5},{4,6},{5,7},{6,0},{7,1},{8,10},{9,11},{10,... | collective-permute-start | bytes 589832 | tf_op jit(solution)/shard_map/ppermute | solution.py:280
  24.0 3.4 %collective-permute-start.3 = (bf16[256,384]{1,0:T(8,128)(2,1)S(1)}, bf16[256,384]{1,0:T(8,128)(2,1)S(1)}, u32[]{:S(2)}, u32[]{:S(2)}) collective-permute-start(bf16[256,384]{1,0:T(8,128)(2,1)S(1)} %get-tuple-element.53), channel_id=1, source_target_pairs={{0,4},{1,5},{2,6},{3,7},{4,0},{5,1},{6,2},{7,3},{8,12},{9,13},{10,... | collective-permute-start | bytes 589832 | tf_op jit(solution)/shard_map/ppermute | solution.py:280
  27.3 0.0 collective-permute-start.4
  27.3 0.0 collective-permute-done.5.refs_3_
  27.3 0.0 copy-done.1
  27.4 0.0 copy-done
  27.4 0.0 copy-start.4
  27.4 0.9 %copy-done.4 = bf16[192,384]{1,0:T(8,128)(2,1)S(1)} copy-done((bf16[192,384]{1,0:T(8,128)(2,1)S(1)}, bf16[192,384]{1,0:T(8,128)(2,1)}, u32[]{:S(2)}) %copy-start.4) | copy-done | bytes 147480
  28.3 8.6 %shard_map.103 = (bf16[384,1024]{1,0:T(8,128)(2,1)S(1)}, bf16[192,1024]{1,0:T(8,128)(2,1)S(1)}, f32[1024,384]{1,0:T(8,128)S(1)}, f32[1024,192]{1,0:T(8,128)S(1)}...) custom-call(bf16[256,384]{1,0:T(8,128)(2,1)S(1)} %get-tuple-element., ...), custom_call_target="tpu_custom_call" | custom-call | tf_op jit(solution)/shard_map/pallas_call | solution.py:59
  36.9 0.0 collective-permute-done.2.refs_1_
  36.9 1.8 %collective-permute-done.3.refs_2_ = bf16[256,384]{1,0:T(8,128)(2,1)S(1)} collective-permute-done((bf16[256,384]{1,0:T(8,128)(2,1)S(1)}, bf16[256,384]{1,0:T(8,128)(2,1)S(1)}, u32[]{:S(2)}, u32[]{:S(2)}) %collective-permute-start.3) | collective-permute-done | bytes 196640 | tf_op jit(solution)/shard_map/ppermute | solution.py:280
  38.8 0.0 collective-permute-done.4.refs_3_
  38.8 0.0 copy-done.5
  38.8 2.3 %shard_map.104 = (bf16[256,384]{1,0:T(8,128)(2,1)S(1)}, bf16[256,384]{1,0:T(8,128)(2,1)S(1)}, bf16[256,384]{1,0:T(8,128)(2,1)S(1)}, bf16[256,384]{1,0:T(8,128)(2...) custom-call(bf16[256,384]{1,0:T(8,128)(2,1)S(1)} %get-tuple-element., ...), custom_call_target="tpu_custom_call" | custom-call | tf_op jit(solution)/shard_map/pallas_call | solution.py:59
  41.0 2.3 %shard_map.106 = (bf16[2,2,96,768]{3,2,1,0:T(8,128)(2,1)S(1)}, bf16[2,2,96,768]{3,2,1,0:T(8,128)(2,1)S(1)}) custom-call(bf16[384,1024]{1,0:T(8,128)(2,1)S(1)} %get-tuple-element.65.refs_0_, bf16[192,1024]{1,0:T(8,128)(2,1)S(1)} %get-tuple-element.66.refs_1_, bf16[2048,192]{1,0:T(8,128)(2,1)S(1)} %get-tuple-element.67.refs_2_, ...), custom_call_target="tpu_custom_call" | custom-call | tf_op jit(solution)/shard_map/pallas_call | solution.py:59
  43.3 0.1 collective-permute-start.9
  43.4 4.7 %collective-permute-start.6 = (bf16[256,384]{1,0:T(8,128)(2,1)S(1)}, bf16[256,384]{1,0:T(8,128)(2,1)S(1)}, u32[]{:S(2)}, u32[]{:S(2)}) collective-permute-start(bf16[256,384]{1,0:T(8,128)(2,1)S(1)} %get-tuple-element.62), channel_id=1, source_target_pairs={{0,2},{1,3},{2,4},{3,5},{4,6},{5,7},{6,0},{7,1},{8,10},{9,11},{10,... | collective-permute-start | bytes 589832 | tf_op jit(solution)/shard_map/ppermute | solution.py:280
  48.1 0.0 collective-permute-done.9.refs_1_
  48.1 0.1 shard_map.107
  48.3 1.6 %collective-permute-start.10 = (bf16[2,48,768]{2,1,0:T(8,128)(2,1)S(1)}, bf16[2,48,768]{2,1,0:T(8,128)(2,1)S(1)}, u32[]{:S(2)}, u32[]{:S(2)}) collective-permute-start(bf16[2,48,768]{2,1,0:T(8,128)(2,1)S(1)} %get-tuple-element.76), channel_id=1, source_target_pairs={{0,1},{1,0},{2,3},{3,2},{4,5},{5,4},{6,7},{7,6},{8,9},{9,8},{10,11... | collective-permute-start | bytes 442376 | tf_op jit(solution)/shard_map/ppermute | solution.py:290
  49.9 1.5 %collective-permute-start.11 = (bf16[2,48,768]{2,1,0:T(8,128)(2,1)S(1)}, bf16[2,48,768]{2,1,0:T(8,128)(2,1)S(1)}, u32[]{:S(2)}, u32[]{:S(2)}) collective-permute-start(bf16[2,48,768]{2,1,0:T(8,128)(2,1)S(1)} %get-tuple-element.77), channel_id=1, source_target_pairs={{0,16},{1,17},{2,18},{3,19},{4,20},{5,21},{6,22},{7,23},{8,24},{9,... | collective-permute-start | bytes 442376 | tf_op jit(solution)/shard_map/ppermute | solution.py:290
  51.3 0.5 collective-permute-start.12
  51.8 0.9 %collective-permute-start.7 = (bf16[256,384]{1,0:T(8,128)(2,1)S(1)}, bf16[256,384]{1,0:T(8,128)(2,1)S(1)}, u32[]{:S(2)}, u32[]{:S(2)}) collective-permute-start(bf16[256,384]{1,0:T(8,128)(2,1)S(1)} %get-tuple-element.63), channel_id=1, source_target_pairs={{0,4},{1,5},{2,6},{3,7},{4,0},{5,1},{6,2},{7,3},{8,12},{9,13},{10,... | collective-permute-start | bytes 589832 | tf_op jit(solution)/shard_map/ppermute | solution.py:280
  52.7 0.6 collective-permute-done.6.refs_1_.refs_4_
  53.3 2.8 %collective-permute-start.8 = (bf16[256,384]{1,0:T(8,128)(2,1)S(1)}, bf16[256,384]{1,0:T(8,128)(2,1)S(1)}, u32[]{:S(2)}, u32[]{:S(2)}) collective-permute-start(bf16[256,384]{1,0:T(8,128)(2,1)S(1)} %get-tuple-element.64), channel_id=1, source_target_pairs={{0,6},{1,7},{2,0},{3,1},{4,2},{5,3},{6,4},{7,5},{8,14},{9,15},{10,... | collective-permute-start | bytes 589832 | tf_op jit(solution)/shard_map/ppermute | solution.py:280
  56.1 0.0 collective-permute-done.10.refs_1_
  56.1 0.5 collective-permute-done.11.refs_2_
  56.6 2.0 %collective-permute-done.12.refs_3_ = bf16[2,48,768]{2,1,0:T(8,128)(2,1)S(1)} collective-permute-done((bf16[2,48,768]{2,1,0:T(8,128)(2,1)S(1)}, bf16[2,48,768]{2,1,0:T(8,128)(2,1)S(1)}, u32[]{:S(2)}, u32[]{:S(2)}) %collective-permute-start.12) | collective-permute-done | bytes 147488 | tf_op jit(solution)/shard_map/ppermute | solution.py:290
  58.6 0.1 shard_map.108
  58.7 2.0 %collective-permute-start.13 = (bf16[2,24,768]{2,1,0:T(8,128)(2,1)S(1)}, bf16[2,24,768]{2,1,0:T(8,128)(2,1)S(1)}, u32[]{:S(2)}, u32[]{:S(2)}) collective-permute-start(bf16[2,24,768]{2,1,0:T(8,128)(2,1)S(1)} %get-tuple-element.80), channel_id=1, source_target_pairs={{0,2},{1,3},{2,0},{3,1},{4,6},{5,7},{6,4},{7,5},{8,10},{9,11},{10,... | collective-permute-start | bytes 221192 | tf_op jit(solution)/shard_map/ppermute | solution.py:290
  60.7 3.9 %collective-permute-done.7.refs_2_ = bf16[256,384]{1,0:T(8,128)(2,1)S(1)} collective-permute-done((bf16[256,384]{1,0:T(8,128)(2,1)S(1)}, bf16[256,384]{1,0:T(8,128)(2,1)S(1)}, u32[]{:S(2)}, u32[]{:S(2)}) %collective-permute-start.7) | collective-permute-done | bytes 196640 | tf_op jit(solution)/shard_map/ppermute | solution.py:280
  64.6 0.1 collective-permute-done.13.refs_1_
  64.7 3.8 %collective-permute-start.14 = (bf16[2,24,768]{2,1,0:T(8,128)(2,1)S(1)}, bf16[2,24,768]{2,1,0:T(8,128)(2,1)S(1)}, u32[]{:S(2)}, u32[]{:S(2)}) collective-permute-start(bf16[2,24,768]{2,1,0:T(8,128)(2,1)S(1)} %shard_map.109.refs_0_), channel_id=1, source_target_pairs={{0,4},{1,5},{2,6},{3,7},{4,0},{5,1},{6,2},{7,3},{8,12},{9,13},{10,... | collective-permute-start | bytes 221192 | tf_op jit(solution)/shard_map/ppermute | solution.py:290
  68.4 0.0 collective-permute-done.8.refs_3_.refs_2_
  68.4 2.3 %collective-permute-done.14.refs_1_ = bf16[2,24,768]{2,1,0:T(8,128)(2,1)S(1)} collective-permute-done((bf16[2,24,768]{2,1,0:T(8,128)(2,1)S(1)}, bf16[2,24,768]{2,1,0:T(8,128)(2,1)S(1)}, u32[]{:S(2)}, u32[]{:S(2)}) %collective-permute-start.14) | collective-permute-done | bytes 73760 | tf_op jit(solution)/shard_map/ppermute | solution.py:290
  70.8 3.4 %collective-permute-start.17 = (bf16[2,24,768]{2,1,0:T(8,128)(2,1)S(1)}, bf16[2,24,768]{2,1,0:T(8,128)(2,1)S(1)}, u32[]{:S(2)}, u32[]{:S(2)}) collective-permute-start(bf16[2,24,768]{2,1,0:T(8,128)(2,1)S(1)} %shard_map.110.refs_0_), channel_id=1, source_target_pairs={{0,3},{1,2},{2,1},{3,0},{4,7},{5,6},{6,5},{7,4},{8,11},{9,10},{10,... | collective-permute-start | bytes 221192 | tf_op jit(solution)/shard_map/ppermute | solution.py:290
  74.2 0.0 collective-permute-start.16
  74.2 0.6 collective-permute-start.15
  74.9 1.0 %shard_map.105 = bf16[1024,384]{1,0:T(8,128)(2,1)} custom-call(bf16[256,384]{1,0:T(8,128)(2,1)S(1)} %get-tuple-element.61.refs_0_, bf16[256,384]{1,0:T(8,128)(2,1)S(1)} %collective-permute-done.6.refs_1_.refs_4_, bf16[256,384]{1,0:T(8,128)(2,1)S(1)} %collective-permute-done.7.refs_2_, bf16[256,384]{1,0:T(8,128)(2,1)S(1)} %collective-permute-done.8.refs_3_.refs_2_), custom_call_target="tpu_custom_call" | custom-call | tf_op jit(solution)/shard_map/pallas_call | solution.py:59
  75.8 1.2 %collective-permute-done.17.refs_3_ = bf16[2,24,768]{2,1,0:T(8,128)(2,1)S(1)} collective-permute-done((bf16[2,24,768]{2,1,0:T(8,128)(2,1)S(1)}, bf16[2,24,768]{2,1,0:T(8,128)(2,1)S(1)}, u32[]{:S(2)}, u32[]{:S(2)}) %collective-permute-start.17) | collective-permute-done | bytes 73760 | tf_op jit(solution)/shard_map/ppermute | solution.py:290
  77.0 1.6 %collective-permute-done.16.refs_2_ = bf16[2,24,768]{2,1,0:T(8,128)(2,1)S(1)} collective-permute-done((bf16[2,24,768]{2,1,0:T(8,128)(2,1)S(1)}, bf16[2,24,768]{2,1,0:T(8,128)(2,1)S(1)}, u32[]{:S(2)}, u32[]{:S(2)}) %collective-permute-start.16) | collective-permute-done | bytes 73760 | tf_op jit(solution)/shard_map/ppermute | solution.py:290
  78.6 0.0 collective-permute-done.15.refs_1_
  78.6 1.1 %shard_map.111 = (f32[3,96,192]{2,1,0:T(8,128)}, f32[192,96]{1,0:T(8,128)}, f32[3,96,192]{2,1,0:T(8,128)}, f32[192,96]{1,0:T(8,128)}) custom-call(bf16[2,24,768]{2,1,0:T(8,128)(2,1)S(1)} %shard_map.110.refs_0_, bf16[2,24,768]{2,1,0:T(8,128)(2,1)S(1)} %collective-permute-done.15.refs_1_, bf16[2,24,768]{2,1,0:T(8,128)(2,1)S(1)} %collective-permute-done.16.refs_2_, ...), custom_call_target="tpu_custom_call" | custom-call | tf_op jit(solution)/shard_map/pallas_call | solution.py:59
  (2 shorter events, 0.0 us)
Async XLA Ops:
  0.6 26.7 %copy-start.1 = (bf16[3,384,192]{1,2,0:T(8,128)(2,1)S(1)}, bf16[3,384,192]{1,2,0:T(8,128)(2,1)}, u32[]{:S(2)}) copy-start(bf16[3,384,192]{1,2,0:T(8,128)(2,1)} %param.10) | copy-start | bytes 1327108
  0.6 26.7 %copy-start = (bf16[3,384,192]{1,2,0:T(8,128)(2,1)S(1)}, bf16[3,384,192]{1,2,0:T(8,128)(2,1)}, u32[]{:S(2)}) copy-start(bf16[3,384,192]{1,2,0:T(8,128)(2,1)} %param.8) | copy-start | bytes 1327108
  0.7 1.2 %copy-start.2 = (bf16[1,1024,384]{2,1,0:T(8,128)(2,1)S(1)}, bf16[1,1024,384]{2,1,0:T(8,128)(2,1)}, u32[]{:S(2)}) copy-start(bf16[1,1024,384]{2,1,0:T(8,128)(2,1)} %param.6) | copy-start | bytes 2359300
  1.9 11.0 %collective-permute-start = (bf16[256,384]{1,0:T(8,128)(2,1)S(1)}, bf16[256,384]{1,0:T(8,128)(2,1)S(1)}, u32[]{:S(2)}, u32[]{:S(2)}) collective-permute-start(bf16[256,384]{1,0:T(8,128)(2,1)S(1)} %get-tuple-element.49), channel_id=1, source_target_pairs={{0,2},{1,3},{2,4},{3,5},{4,6},{5,7},{6,0},{7,1},{8,10},{9,11},{10,... | collective-permute-start | bytes 589832 | tf_op jit(solution)/shard_map/ppermute | solution.py:280
  5.0 15.5 %collective-permute-start.1 = (bf16[256,384]{1,0:T(8,128)(2,1)S(1)}, bf16[256,384]{1,0:T(8,128)(2,1)S(1)}, u32[]{:S(2)}, u32[]{:S(2)}) collective-permute-start(bf16[256,384]{1,0:T(8,128)(2,1)S(1)} %get-tuple-element.50), channel_id=1, source_target_pairs={{0,4},{1,5},{2,6},{3,7},{4,0},{5,1},{6,2},{7,3},{8,12},{9,13},{10,... | collective-permute-start | bytes 589832 | tf_op jit(solution)/shard_map/ppermute | solution.py:280
  7.6 19.7 %collective-permute-start.5 = (bf16[256,384]{1,0:T(8,128)(2,1)S(1)}, bf16[256,384]{1,0:T(8,128)(2,1)S(1)}, u32[]{:S(2)}, u32[]{:S(2)}) collective-permute-start(bf16[256,384]{1,0:T(8,128)(2,1)S(1)} %get-tuple-element.56), channel_id=1, source_target_pairs={{0,6},{1,7},{2,0},{3,1},{4,2},{5,3},{6,4},{7,5},{8,14},{9,15},{10,... | collective-permute-start | bytes 589832 | tf_op jit(solution)/shard_map/ppermute | solution.py:280
  8.9 1.1 %copy-start.3 = (bf16[1,1024,384]{2,1,0:T(8,128)(2,1)S(1)}, bf16[1,1024,384]{2,1,0:T(8,128)(2,1)}, u32[]{:S(2)}) copy-start(bf16[1,1024,384]{2,1,0:T(8,128)(2,1)} %param.7) | copy-start | bytes 2359300
  10.1 28.7 %copy-start.5 = (bf16[192,384]{1,0:T(8,128)(2,1)S(1)}, bf16[192,384]{1,0:T(8,128)(2,1)}, u32[]{:S(2)}) copy-start(bf16[192,384]{1,0:T(8,128)(2,1)} %refs_11_.1) | copy-start | bytes 442372
  20.5 16.4 %collective-permute-start.2 = (bf16[256,384]{1,0:T(8,128)(2,1)S(1)}, bf16[256,384]{1,0:T(8,128)(2,1)S(1)}, u32[]{:S(2)}, u32[]{:S(2)}) collective-permute-start(bf16[256,384]{1,0:T(8,128)(2,1)S(1)} %get-tuple-element.52), channel_id=1, source_target_pairs={{0,2},{1,3},{2,4},{3,5},{4,6},{5,7},{6,0},{7,1},{8,10},{9,11},{10,... | collective-permute-start | bytes 589832 | tf_op jit(solution)/shard_map/ppermute | solution.py:280
  24.0 14.8 %collective-permute-start.3 = (bf16[256,384]{1,0:T(8,128)(2,1)S(1)}, bf16[256,384]{1,0:T(8,128)(2,1)S(1)}, u32[]{:S(2)}, u32[]{:S(2)}) collective-permute-start(bf16[256,384]{1,0:T(8,128)(2,1)S(1)} %get-tuple-element.53), channel_id=1, source_target_pairs={{0,4},{1,5},{2,6},{3,7},{4,0},{5,1},{6,2},{7,3},{8,12},{9,13},{10,... | collective-permute-start | bytes 589832 | tf_op jit(solution)/shard_map/ppermute | solution.py:280
  27.3 11.4 %collective-permute-start.4 = (bf16[256,384]{1,0:T(8,128)(2,1)S(1)}, bf16[256,384]{1,0:T(8,128)(2,1)S(1)}, u32[]{:S(2)}, u32[]{:S(2)}) collective-permute-start(bf16[256,384]{1,0:T(8,128)(2,1)S(1)} %get-tuple-element.54), channel_id=1, source_target_pairs={{0,6},{1,7},{2,0},{3,1},{4,2},{5,3},{6,4},{7,5},{8,14},{9,15},{10,... | collective-permute-start | bytes 589832 | tf_op jit(solution)/shard_map/ppermute | solution.py:280
  27.4 0.9 %copy-start.4 = (bf16[192,384]{1,0:T(8,128)(2,1)S(1)}, bf16[192,384]{1,0:T(8,128)(2,1)}, u32[]{:S(2)}) copy-start(bf16[192,384]{1,0:T(8,128)(2,1)} %refs_9_.1) | copy-start | bytes 442372
  43.3 4.8 %collective-permute-start.9 = (bf16[2,2,96,768]{3,2,1,0:T(8,128)(2,1)S(1)}, bf16[2,2,96,768]{3,2,1,0:T(8,128)(2,1)S(1)}, u32[]{:S(2)}, u32[]{:S(2)}) collective-permute-start(bf16[2,2,96,768]{3,2,1,0:T(8,128)(2,1)S(1)} %get-tuple-element.74), channel_id=1, source_target_pairs={{0,8},{1,9},{2,10},{3,11},{4,12},{5,13},{6,14},{7,15},{8,0},{9,1},... | collective-permute-start | bytes 1769480 | tf_op jit(solution)/shard_map/ppermute | solution.py:290
  43.4 10.0 %collective-permute-start.6 = (bf16[256,384]{1,0:T(8,128)(2,1)S(1)}, bf16[256,384]{1,0:T(8,128)(2,1)S(1)}, u32[]{:S(2)}, u32[]{:S(2)}) collective-permute-start(bf16[256,384]{1,0:T(8,128)(2,1)S(1)} %get-tuple-element.62), channel_id=1, source_target_pairs={{0,2},{1,3},{2,4},{3,5},{4,6},{5,7},{6,0},{7,1},{8,10},{9,11},{10,... | collective-permute-start | bytes 589832 | tf_op jit(solution)/shard_map/ppermute | solution.py:280
  48.3 7.9 %collective-permute-start.10 = (bf16[2,48,768]{2,1,0:T(8,128)(2,1)S(1)}, bf16[2,48,768]{2,1,0:T(8,128)(2,1)S(1)}, u32[]{:S(2)}, u32[]{:S(2)}) collective-permute-start(bf16[2,48,768]{2,1,0:T(8,128)(2,1)S(1)} %get-tuple-element.76), channel_id=1, source_target_pairs={{0,1},{1,0},{2,3},{3,2},{4,5},{5,4},{6,7},{7,6},{8,9},{9,8},{10,11... | collective-permute-start | bytes 442376 | tf_op jit(solution)/shard_map/ppermute | solution.py:290
  49.9 6.7 %collective-permute-start.11 = (bf16[2,48,768]{2,1,0:T(8,128)(2,1)S(1)}, bf16[2,48,768]{2,1,0:T(8,128)(2,1)S(1)}, u32[]{:S(2)}, u32[]{:S(2)}) collective-permute-start(bf16[2,48,768]{2,1,0:T(8,128)(2,1)S(1)} %get-tuple-element.77), channel_id=1, source_target_pairs={{0,16},{1,17},{2,18},{3,19},{4,20},{5,21},{6,22},{7,23},{8,24},{9,... | collective-permute-start | bytes 442376 | tf_op jit(solution)/shard_map/ppermute | solution.py:290
  51.3 7.2 %collective-permute-start.12 = (bf16[2,48,768]{2,1,0:T(8,128)(2,1)S(1)}, bf16[2,48,768]{2,1,0:T(8,128)(2,1)S(1)}, u32[]{:S(2)}, u32[]{:S(2)}) collective-permute-start(bf16[2,48,768]{2,1,0:T(8,128)(2,1)S(1)} %get-tuple-element.78), channel_id=1, source_target_pairs={{0,17},{1,16},{2,19},{3,18},{4,21},{5,20},{6,23},{7,22},{8,25},{9,... | collective-permute-start | bytes 442376 | tf_op jit(solution)/shard_map/ppermute | solution.py:290
  51.8 12.7 %collective-permute-start.7 = (bf16[256,384]{1,0:T(8,128)(2,1)S(1)}, bf16[256,384]{1,0:T(8,128)(2,1)S(1)}, u32[]{:S(2)}, u32[]{:S(2)}) collective-permute-start(bf16[256,384]{1,0:T(8,128)(2,1)S(1)} %get-tuple-element.63), channel_id=1, source_target_pairs={{0,4},{1,5},{2,6},{3,7},{4,0},{5,1},{6,2},{7,3},{8,12},{9,13},{10,... | collective-permute-start | bytes 589832 | tf_op jit(solution)/shard_map/ppermute | solution.py:280
  53.3 15.1 %collective-permute-start.8 = (bf16[256,384]{1,0:T(8,128)(2,1)S(1)}, bf16[256,384]{1,0:T(8,128)(2,1)S(1)}, u32[]{:S(2)}, u32[]{:S(2)}) collective-permute-start(bf16[256,384]{1,0:T(8,128)(2,1)S(1)} %get-tuple-element.64), channel_id=1, source_target_pairs={{0,6},{1,7},{2,0},{3,1},{4,2},{5,3},{6,4},{7,5},{8,14},{9,15},{10,... | collective-permute-start | bytes 589832 | tf_op jit(solution)/shard_map/ppermute | solution.py:280
  58.7 5.9 %collective-permute-start.13 = (bf16[2,24,768]{2,1,0:T(8,128)(2,1)S(1)}, bf16[2,24,768]{2,1,0:T(8,128)(2,1)S(1)}, u32[]{:S(2)}, u32[]{:S(2)}) collective-permute-start(bf16[2,24,768]{2,1,0:T(8,128)(2,1)S(1)} %get-tuple-element.80), channel_id=1, source_target_pairs={{0,2},{1,3},{2,0},{3,1},{4,6},{5,7},{6,4},{7,5},{8,10},{9,11},{10,... | collective-permute-start | bytes 221192 | tf_op jit(solution)/shard_map/ppermute | solution.py:290
  64.7 6.1 %collective-permute-start.14 = (bf16[2,24,768]{2,1,0:T(8,128)(2,1)S(1)}, bf16[2,24,768]{2,1,0:T(8,128)(2,1)S(1)}, u32[]{:S(2)}, u32[]{:S(2)}) collective-permute-start(bf16[2,24,768]{2,1,0:T(8,128)(2,1)S(1)} %shard_map.109.refs_0_), channel_id=1, source_target_pairs={{0,4},{1,5},{2,6},{3,7},{4,0},{5,1},{6,2},{7,3},{8,12},{9,13},{10,... | collective-permute-start | bytes 221192 | tf_op jit(solution)/shard_map/ppermute | solution.py:290
  70.8 6.2 %collective-permute-start.17 = (bf16[2,24,768]{2,1,0:T(8,128)(2,1)S(1)}, bf16[2,24,768]{2,1,0:T(8,128)(2,1)S(1)}, u32[]{:S(2)}, u32[]{:S(2)}) collective-permute-start(bf16[2,24,768]{2,1,0:T(8,128)(2,1)S(1)} %shard_map.110.refs_0_), channel_id=1, source_target_pairs={{0,3},{1,2},{2,1},{3,0},{4,7},{5,6},{6,5},{7,4},{8,11},{9,10},{10,... | collective-permute-start | bytes 221192 | tf_op jit(solution)/shard_map/ppermute | solution.py:290
  74.2 4.4 %collective-permute-start.16 = (bf16[2,24,768]{2,1,0:T(8,128)(2,1)S(1)}, bf16[2,24,768]{2,1,0:T(8,128)(2,1)S(1)}, u32[]{:S(2)}, u32[]{:S(2)}) collective-permute-start(bf16[2,24,768]{2,1,0:T(8,128)(2,1)S(1)} %shard_map.110.refs_0_), channel_id=1, source_target_pairs={{0,2},{1,3},{2,0},{3,1},{4,6},{5,7},{6,4},{7,5},{8,10},{9,11},{10,... | collective-permute-start | bytes 221192 | tf_op jit(solution)/shard_map/ppermute | solution.py:290
  74.2 4.4 %collective-permute-start.15 = (bf16[2,24,768]{2,1,0:T(8,128)(2,1)S(1)}, bf16[2,24,768]{2,1,0:T(8,128)(2,1)S(1)}, u32[]{:S(2)}, u32[]{:S(2)}) collective-permute-start(bf16[2,24,768]{2,1,0:T(8,128)(2,1)S(1)} %shard_map.110.refs_0_), channel_id=1, source_target_pairs={{0,1},{1,0},{2,3},{3,2},{4,5},{5,4},{6,7},{7,6},{8,9},{9,8},{10,11... | collective-permute-start | bytes 221192 | tf_op jit(solution)/shard_map/ppermute | solution.py:290

commit v4 on v3

--- a/solution.py
+++ b/solution.py
@@ -12,9 +12,10 @@
 DILATION_TWO = 4096
 TILE = 256
 CHUNK = 32
-MAX_PERMUTES = 8
+MAX_PERMUTES = 4
 NEED = ((1,), (2,), (3,))
-GATE = (1, 2,)
+ORDER = (2, 3, 1)
+GATE = (3,)
 BF16 = jnp.bfloat16
 F32 = jnp.float32
 VMEM = pl.BlockSpec(memory_space=pltpu.VMEM)
@@ -40,14 +41,6 @@
 
 def position(hop):
     return lax.axis_index("seq") // hop
-
-
-def behind(me, k, count):
-    return lax.rem(me + (count - k), count)
-
-
-def ahead(me, k, count):
-    return lax.rem(me + k, count)
 
 
 def call(kernel, out_shapes, scratch, args, after=(), mib=8):
@@ -71,7 +64,7 @@
     size = pieces[0].shape[0]
     me = position(hop)
     for k, piece in enumerate(pieces):
-        at = pl.multiple_of(ahead(me, k, count) * size, size)
+        at = pl.multiple_of((me ^ k) * size, size)
         piece[...] = block[pl.ds(at, size), :]
 
 
@@ -83,7 +76,7 @@
     size = rows_ref.shape[0] // count
     me = position(hop)
     for k, part in enumerate(parts):
-        at = pl.multiple_of(behind(me, k, count) * size, size)
+        at = pl.multiple_of((me ^ k) * size, size)
         rows_ref[pl.ds(at, size), :] = part[...]
 
 
@@ -95,7 +88,7 @@
     size = rows_ref.shape[0] // count
     me = position(hop)
     for k, part in enumerate(parts):
-        at = pl.multiple_of(ahead(me, k, count) * size, size)
+        at = pl.multiple_of(lax.rem(me + k, count) * size, size)
         part[...] = rows_ref[pl.ds(at, size), :]
 
 
@@ -270,7 +263,13 @@
 
 
 def collect_kernel(hop, *refs):
-    place(refs[:-1], refs[-1], hop)
+    *parts, rows_ref = refs
+    count = len(parts)
+    size = rows_ref.shape[0] // count
+    me = position(hop)
+    for k, part in enumerate(parts):
+        at = pl.multiple_of(lax.rem(me + (count - k), count) * size, size)
+        rows_ref[pl.ds(at, size), :] = part[...]
 
 
 def send_ahead(block, hop, k):
@@ -305,7 +304,7 @@
 def to_columns(block, hop, after=()):
     count = lax.axis_size("seq") // hop
     rows, channels = block.shape
-    if count > MAX_PERMUTES:
+    if count != MAX_PERMUTES:
         return [exchange_all(block, hop)]
     pieces = call(
         functools.partial(cut_kernel, hop), [((rows // count, channels), BF16)] * count, [], [block], mib=2
@@ -316,11 +315,8 @@
 
 
 def forward_pieces(pieces, hop):
-    return [pieces[0]] + [send_ahead(pieces[k], hop, k) for k in range(1, len(pieces))]
-
-
-def once(block, after):
-    return lax.optimization_barrier((block, after))[0]
+    sent = {k: mirrored(pieces[k], 0, k * hop) for k in ORDER[: len(pieces) - 1]}
+    return [pieces[0]] + [sent[k] for k in sorted(sent)]
 
 
 def reduce_weights(keep, send, grads, hop, scale):
@@ -330,19 +326,16 @@
     half = (n_blocks, rows // 2, lanes)
     fourth = (n_blocks, rows // 4, lanes)
     received = mirrored(send, 1, 0)
-    back = dict.fromkeys(range(count))
-
-    def send_home(ks, after=None):
-        for k in ks:
-            back[k] = send_ahead(grads[k] if after is None else once(grads[k], after), hop, k)
-        return [back[k] for k in ks]
-
-    if count == 4:
+    back = {}
+
+
+    if count == MAX_PERMUTES:
         back[0] = grads[0]
-        send_home((1, 2, 3))
+        for k in range(1, count):
+            back[k] = send_ahead(grads[k], hop, k)
     pieces = call(split_kernel, [(half, F32)] + [(half, BF16)] * 3, [], [keep, received])
     arrived = [pieces[0]] + [mirrored(pieces[k], 2 * (k // 2), k % 2) for k in range(1, 4)]
-    if count == 4:
+    if count == MAX_PERMUTES:
         keep, send = call(
             functools.partial(halve_kernel, hop), [(fourth, F32), (fourth, BF16)], [(half, F32)], arrived,
             [back[k] for k in NEED[0]],
@@ -355,7 +348,7 @@
         (plane,) = call(sum_kernel, [(half, F32)], [], arrived)
         own = lax.psum(plane, "seq", axis_index_groups=column_groups(hop)).astype(BF16)
         parts = [own, mirrored(own, 0, 1)]
-        back = [exchange_all(grads[0], hop)] if len(grads) == 1 else forward_pieces(grads, hop)
+        back = [exchange_all(grads[0], hop)]
     outs = call(
         functools.partial(finish_kernel, scale, hop, n_blocks),
         [((3, rows, width), F32), ((width, rows), F32)] * n_blocks,

time: 79.9 us -> 78.2 us (0.979)
  starting transfers between devices: 35.7 us -> 34 us
    ppermute x9 -> x3, starting transfers between devices: 22.3 us -> 8.16 us  [send_ahead(): return lax.ppermute(block, 'seq', route)]
    ppermute x9 -> x15, waiting for transfers between devices: 7.63 us -> 20.5 us  [mirrored(): return lax.ppermute(block, ('dp', 'seq'), route)]
    ppermute x9 -> x3, waiting for transfers between devices: 16.7 us -> 3.89 us  [send_ahead(): return lax.ppermute(block, 'seq', route)]
    ppermute x9 -> x15, starting transfers between devices: 13.4 us -> 25.8 us  [mirrored(): return lax.ppermute(block, ('dp', 'seq'), route)]
  transfers between devices with their start and end apart: 18 -> 18, of which waited for: 11 -> 10; matrix products, arithmetic and copies ran while one was open for 0% -> 0% of each run, Pallas kernels for 12% -> 13%
where the time goes in v4:
time: 78.2 us; the launch traced here: 78 us
  starting transfers between devices  34 us (43%)
  waiting for transfers between devices  24.4 us (31%)
  Pallas kernels  15.6 us (20%)
  local copies, waits for them, and re-layouts  3.26 us (4%)
    ppermute x15, starting transfers between devices, mirrored(): return lax.ppermute(block, ('dp', 'seq'), route)  25.8 us
    ppermute x15, waiting for transfers between devices, mirrored(): return lax.ppermute(block, ('dp', 'seq'), route)  20.5 us
    pallas_call x11, Pallas kernels, call(): pl.pallas_call(body, out_shape=[jax.ShapeDtypeStruct(s, d) for s, d in ou...  15.6 us
    ppermute x3, starting transfers between devices, send_ahead(): return lax.ppermute(block, 'seq', route)  8.16 us
    ppermute x3, waiting for transfers between devices, send_ahead(): return lax.ppermute(block, 'seq', route)  3.89 us
    unnamed x12, local copies, waits for them, and re-layouts  3.26 us
  transfers between devices with their start and end apart: 18, of which 10 were waited for; matrix products, arithmetic and copies ran while one was open for 0% of the time, Pallas kernels for 13%

profile of v4, /device:TPU:0, one launch (start us, length us, event | category | flops | bytes accessed | tf_op | source)
XLA Modules:
  0.0 78.0 jit_solution(5094827816752463109)
XLA Ops:
  0.6 0.0 copy-start.1
  0.6 0.0 copy-start
  0.7 0.0 copy-start.2
  0.7 1.2 %copy-done.2 = bf16[1,1024,384]{2,1,0:T(8,128)(2,1)S(1)} copy-done((bf16[1,1024,384]{2,1,0:T(8,128)(2,1)S(1)}, bf16[1,1024,384]{2,1,0:T(8,128)(2,1)}, u32[]{:S(2)}) %copy-start.2) | copy-done | bytes 786456
  1.9 0.1 shard_map.102
  1.9 5.1 %collective-permute-start = (bf16[256,384]{1,0:T(8,128)(2,1)S(1)}, bf16[256,384]{1,0:T(8,128)(2,1)S(1)}, u32[]{:S(2)}, u32[]{:S(2)}) collective-permute-start(bf16[256,384]{1,0:T(8,128)(2,1)S(1)} %get-tuple-element.49), channel_id=1, source_target_pairs={{0,6},{1,7},{2,4},{3,5},{4,2},{5,3},{6,0},{7,1},{8,14},{9,15},{10,... | collective-permute-start | bytes 589832 | tf_op jit(solution)/shard_map/ppermute | solution.py:289
  7.0 0.0 collective-permute-start.4
  7.1 0.6 collective-permute-start.5
  7.7 0.0 copy-start.3
  7.7 1.1 %copy-done.3 = bf16[1,1024,384]{2,1,0:T(8,128)(2,1)S(1)} copy-done((bf16[1,1024,384]{2,1,0:T(8,128)(2,1)S(1)}, bf16[1,1024,384]{2,1,0:T(8,128)(2,1)}, u32[]{:S(2)}) %copy-start.3) | copy-done | bytes 786456
  8.8 0.0 copy-start.5
  8.8 0.1 shard_map.101
  8.9 3.9 %collective-permute-done.refs_3_ = bf16[256,384]{1,0:T(8,128)(2,1)S(1)} collective-permute-done((bf16[256,384]{1,0:T(8,128)(2,1)S(1)}, bf16[256,384]{1,0:T(8,128)(2,1)S(1)}, u32[]{:S(2)}, u32[]{:S(2)}) %collective-permute-start) | collective-permute-done | bytes 196640 | tf_op jit(solution)/shard_map/ppermute | solution.py:289
  12.8 4.9 %collective-permute-start.1 = (bf16[256,384]{1,0:T(8,128)(2,1)S(1)}, bf16[256,384]{1,0:T(8,128)(2,1)S(1)}, u32[]{:S(2)}, u32[]{:S(2)}) collective-permute-start(bf16[256,384]{1,0:T(8,128)(2,1)S(1)} %get-tuple-element.51), channel_id=1, source_target_pairs={{0,2},{1,3},{2,0},{3,1},{4,6},{5,7},{6,4},{7,5},{8,10},{9,11},{10,... | collective-permute-start | bytes 589832 | tf_op jit(solution)/shard_map/ppermute | solution.py:289
  17.7 0.7 collective-permute-start.2
  18.3 1.7 %collective-permute-start.3 = (bf16[256,384]{1,0:T(8,128)(2,1)S(1)}, bf16[256,384]{1,0:T(8,128)(2,1)S(1)}, u32[]{:S(2)}, u32[]{:S(2)}) collective-permute-start(bf16[256,384]{1,0:T(8,128)(2,1)S(1)} %get-tuple-element.53), channel_id=1, source_target_pairs={{0,6},{1,7},{2,4},{3,5},{4,2},{5,3},{6,0},{7,1},{8,14},{9,15},{10,... | collective-permute-start | bytes 589832 | tf_op jit(solution)/shard_map/ppermute | solution.py:289
  20.0 0.0 collective-permute-done.4.refs_1_
  20.0 5.6 %collective-permute-done.5.refs_2_ = bf16[256,384]{1,0:T(8,128)(2,1)S(1)} collective-permute-done((bf16[256,384]{1,0:T(8,128)(2,1)S(1)}, bf16[256,384]{1,0:T(8,128)(2,1)S(1)}, u32[]{:S(2)}, u32[]{:S(2)}) %collective-permute-start.5) | collective-permute-done | bytes 196640 | tf_op jit(solution)/shard_map/ppermute | solution.py:289
  25.7 0.0 copy-done.1
  25.7 0.0 copy-done
  25.7 0.0 copy-start.4
  25.7 0.9 %copy-done.4 = bf16[192,384]{1,0:T(8,128)(2,1)S(1)} copy-done((bf16[192,384]{1,0:T(8,128)(2,1)S(1)}, bf16[192,384]{1,0:T(8,128)(2,1)}, u32[]{:S(2)}) %copy-start.4) | copy-done | bytes 147480
  26.6 8.6 %shard_map.103 = (bf16[384,1024]{1,0:T(8,128)(2,1)S(1)}, bf16[192,1024]{1,0:T(8,128)(2,1)S(1)}, f32[1024,384]{1,0:T(8,128)S(1)}, f32[1024,192]{1,0:T(8,128)S(1)}...) custom-call(bf16[256,384]{1,0:T(8,128)(2,1)S(1)} %get-tuple-element., ...), custom_call_target="tpu_custom_call" | custom-call | tf_op jit(solution)/shard_map/pallas_call | solution.py:52
  35.2 0.0 collective-permute-done.1.refs_1_
  35.2 2.1 %collective-permute-done.2.refs_2_ = bf16[256,384]{1,0:T(8,128)(2,1)S(1)} collective-permute-done((bf16[256,384]{1,0:T(8,128)(2,1)S(1)}, bf16[256,384]{1,0:T(8,128)(2,1)S(1)}, u32[]{:S(2)}, u32[]{:S(2)}) %collective-permute-start.2) | collective-permute-done | bytes 196640 | tf_op jit(solution)/shard_map/ppermute | solution.py:289
  37.4 0.0 collective-permute-done.3.refs_3_
  37.4 0.0 copy-done.5
  37.4 2.2 %shard_map.104 = (bf16[256,384]{1,0:T(8,128)(2,1)S(1)}, bf16[256,384]{1,0:T(8,128)(2,1)S(1)}, bf16[256,384]{1,0:T(8,128)(2,1)S(1)}, bf16[256,384]{1,0:T(8,128)(2...) custom-call(bf16[256,384]{1,0:T(8,128)(2,1)S(1)} %get-tuple-element., ...), custom_call_target="tpu_custom_call" | custom-call | tf_op jit(solution)/shard_map/pallas_call | solution.py:52
  39.6 2.3 %shard_map.106 = (bf16[2,2,96,768]{3,2,1,0:T(8,128)(2,1)S(1)}, bf16[2,2,96,768]{3,2,1,0:T(8,128)(2,1)S(1)}) custom-call(bf16[384,1024]{1,0:T(8,128)(2,1)S(1)} %get-tuple-element.65.refs_0_, bf16[192,1024]{1,0:T(8,128)(2,1)S(1)} %get-tuple-element.66.refs_1_, bf16[2048,192]{1,0:T(8,128)(2,1)S(1)} %get-tuple-element.67.refs_2_, ...), custom_call_target="tpu_custom_call" | custom-call | tf_op jit(solution)/shard_map/pallas_call | solution.py:52
  41.9 0.1 collective-permute-start.9
  42.0 3.9 %collective-permute-start.6 = (bf16[256,384]{1,0:T(8,128)(2,1)S(1)}, bf16[256,384]{1,0:T(8,128)(2,1)S(1)}, u32[]{:S(2)}, u32[]{:S(2)}) collective-permute-start(bf16[256,384]{1,0:T(8,128)(2,1)S(1)} %get-tuple-element.62), channel_id=1, source_target_pairs={{0,2},{1,3},{2,4},{3,5},{4,6},{5,7},{6,0},{7,1},{8,10},{9,11},{10,... | collective-permute-start | bytes 589832 | tf_op jit(solution)/shard_map/ppermute | solution.py:279
  45.9 0.0 collective-permute-done.9.refs_1_
  45.9 0.1 shard_map.107
  46.0 1.6 %collective-permute-start.10 = (bf16[2,48,768]{2,1,0:T(8,128)(2,1)S(1)}, bf16[2,48,768]{2,1,0:T(8,128)(2,1)S(1)}, u32[]{:S(2)}, u32[]{:S(2)}) collective-permute-start(bf16[2,48,768]{2,1,0:T(8,128)(2,1)S(1)} %get-tuple-element.76), channel_id=1, source_target_pairs={{0,1},{1,0},{2,3},{3,2},{4,5},{5,4},{6,7},{7,6},{8,9},{9,8},{10,11... | collective-permute-start | bytes 442376 | tf_op jit(solution)/shard_map/ppermute | solution.py:289
  47.6 1.5 %collective-permute-start.11 = (bf16[2,48,768]{2,1,0:T(8,128)(2,1)S(1)}, bf16[2,48,768]{2,1,0:T(8,128)(2,1)S(1)}, u32[]{:S(2)}, u32[]{:S(2)}) collective-permute-start(bf16[2,48,768]{2,1,0:T(8,128)(2,1)S(1)} %get-tuple-element.77), channel_id=1, source_target_pairs={{0,16},{1,17},{2,18},{3,19},{4,20},{5,21},{6,22},{7,23},{8,24},{9,... | collective-permute-start | bytes 442376 | tf_op jit(solution)/shard_map/ppermute | solution.py:289
  49.1 0.5 collective-permute-start.12
  49.6 3.0 %collective-permute-start.7 = (bf16[256,384]{1,0:T(8,128)(2,1)S(1)}, bf16[256,384]{1,0:T(8,128)(2,1)S(1)}, u32[]{:S(2)}, u32[]{:S(2)}) collective-permute-start(bf16[256,384]{1,0:T(8,128)(2,1)S(1)} %get-tuple-element.63), channel_id=1, source_target_pairs={{0,4},{1,5},{2,6},{3,7},{4,0},{5,1},{6,2},{7,3},{8,12},{9,13},{10,... | collective-permute-start | bytes 589832 | tf_op jit(solution)/shard_map/ppermute | solution.py:279
  52.5 0.0 collective-permute-done.6.refs_1_.refs_4_
  52.5 1.3 %collective-permute-start.8 = (bf16[256,384]{1,0:T(8,128)(2,1)S(1)}, bf16[256,384]{1,0:T(8,128)(2,1)S(1)}, u32[]{:S(2)}, u32[]{:S(2)}) collective-permute-start(bf16[256,384]{1,0:T(8,128)(2,1)S(1)} %get-tuple-element.64), channel_id=1, source_target_pairs={{0,6},{1,7},{2,0},{3,1},{4,2},{5,3},{6,4},{7,5},{8,14},{9,15},{10,... | collective-permute-start | bytes 589832 | tf_op jit(solution)/shard_map/ppermute | solution.py:279
  53.9 0.0 collective-permute-done.10.refs_1_
  53.9 0.5 collective-permute-done.11.refs_2_
  54.3 2.0 %collective-permute-done.12.refs_3_ = bf16[2,48,768]{2,1,0:T(8,128)(2,1)S(1)} collective-permute-done((bf16[2,48,768]{2,1,0:T(8,128)(2,1)S(1)}, bf16[2,48,768]{2,1,0:T(8,128)(2,1)S(1)}, u32[]{:S(2)}, u32[]{:S(2)}) %collective-permute-start.12) | collective-permute-done | bytes 147488 | tf_op jit(solution)/shard_map/ppermute | solution.py:289
  56.3 0.1 shard_map.108
  56.4 2.0 %collective-permute-start.13 = (bf16[2,24,768]{2,1,0:T(8,128)(2,1)S(1)}, bf16[2,24,768]{2,1,0:T(8,128)(2,1)S(1)}, u32[]{:S(2)}, u32[]{:S(2)}) collective-permute-start(bf16[2,24,768]{2,1,0:T(8,128)(2,1)S(1)} %get-tuple-element.80), channel_id=1, source_target_pairs={{0,2},{1,3},{2,0},{3,1},{4,6},{5,7},{6,4},{7,5},{8,10},{9,11},{10,... | collective-permute-start | bytes 221192 | tf_op jit(solution)/shard_map/ppermute | solution.py:289
  58.4 3.9 %collective-permute-done.7.refs_2_ = bf16[256,384]{1,0:T(8,128)(2,1)S(1)} collective-permute-done((bf16[256,384]{1,0:T(8,128)(2,1)S(1)}, bf16[256,384]{1,0:T(8,128)(2,1)S(1)}, u32[]{:S(2)}, u32[]{:S(2)}) %collective-permute-start.7) | collective-permute-done | bytes 196640 | tf_op jit(solution)/shard_map/ppermute | solution.py:279
  62.3 0.7 collective-permute-done.13.refs_1_
  63.0 3.7 %collective-permute-start.14 = (bf16[2,24,768]{2,1,0:T(8,128)(2,1)S(1)}, bf16[2,24,768]{2,1,0:T(8,128)(2,1)S(1)}, u32[]{:S(2)}, u32[]{:S(2)}) collective-permute-start(bf16[2,24,768]{2,1,0:T(8,128)(2,1)S(1)} %shard_map.109.refs_0_), channel_id=1, source_target_pairs={{0,4},{1,5},{2,6},{3,7},{4,0},{5,1},{6,2},{7,3},{8,12},{9,13},{10,... | collective-permute-start | bytes 221192 | tf_op jit(solution)/shard_map/ppermute | solution.py:289
  66.7 0.0 collective-permute-done.8.refs_3_.refs_2_
  66.7 3.1 %collective-permute-done.14.refs_1_ = bf16[2,24,768]{2,1,0:T(8,128)(2,1)S(1)} collective-permute-done((bf16[2,24,768]{2,1,0:T(8,128)(2,1)S(1)}, bf16[2,24,768]{2,1,0:T(8,128)(2,1)S(1)}, u32[]{:S(2)}, u32[]{:S(2)}) %collective-permute-start.14) | collective-permute-done | bytes 73760 | tf_op jit(solution)/shard_map/ppermute | solution.py:289
  69.8 2.7 %collective-permute-start.17 = (bf16[2,24,768]{2,1,0:T(8,128)(2,1)S(1)}, bf16[2,24,768]{2,1,0:T(8,128)(2,1)S(1)}, u32[]{:S(2)}, u32[]{:S(2)}) collective-permute-start(bf16[2,24,768]{2,1,0:T(8,128)(2,1)S(1)} %shard_map.110.refs_0_), channel_id=1, source_target_pairs={{0,3},{1,2},{2,1},{3,0},{4,7},{5,6},{6,5},{7,4},{8,11},{9,10},{10,... | collective-permute-start | bytes 221192 | tf_op jit(solution)/shard_map/ppermute | solution.py:289
  72.5 0.0 collective-permute-start.16
  72.6 0.8 %collective-permute-start.15 = (bf16[2,24,768]{2,1,0:T(8,128)(2,1)S(1)}, bf16[2,24,768]{2,1,0:T(8,128)(2,1)S(1)}, u32[]{:S(2)}, u32[]{:S(2)}) collective-permute-start(bf16[2,24,768]{2,1,0:T(8,128)(2,1)S(1)} %shard_map.110.refs_0_), channel_id=1, source_target_pairs={{0,1},{1,0},{2,3},{3,2},{4,5},{5,4},{6,7},{7,6},{8,9},{9,8},{10,11... | collective-permute-start | bytes 221192 | tf_op jit(solution)/shard_map/ppermute | solution.py:289
  73.4 1.0 %shard_map.105 = bf16[1024,384]{1,0:T(8,128)(2,1)} custom-call(bf16[256,384]{1,0:T(8,128)(2,1)S(1)} %get-tuple-element.61.refs_0_, bf16[256,384]{1,0:T(8,128)(2,1)S(1)} %collective-permute-done.6.refs_1_.refs_4_, bf16[256,384]{1,0:T(8,128)(2,1)S(1)} %collective-permute-done.7.refs_2_, bf16[256,384]{1,0:T(8,128)(2,1)S(1)} %collective-permute-done.8.refs_3_.refs_2_), custom_call_target="tpu_custom_call" | custom-call | tf_op jit(solution)/shard_map/pallas_call | solution.py:52
  74.3 0.8 %collective-permute-done.17.refs_3_ = bf16[2,24,768]{2,1,0:T(8,128)(2,1)S(1)} collective-permute-done((bf16[2,24,768]{2,1,0:T(8,128)(2,1)S(1)}, bf16[2,24,768]{2,1,0:T(8,128)(2,1)S(1)}, u32[]{:S(2)}, u32[]{:S(2)}) %collective-permute-start.17) | collective-permute-done | bytes 73760 | tf_op jit(solution)/shard_map/ppermute | solution.py:289
  75.1 1.8 %collective-permute-done.16.refs_2_ = bf16[2,24,768]{2,1,0:T(8,128)(2,1)S(1)} collective-permute-done((bf16[2,24,768]{2,1,0:T(8,128)(2,1)S(1)}, bf16[2,24,768]{2,1,0:T(8,128)(2,1)S(1)}, u32[]{:S(2)}, u32[]{:S(2)}) %collective-permute-start.16) | collective-permute-done | bytes 73760 | tf_op jit(solution)/shard_map/ppermute | solution.py:289
  76.9 0.0 collective-permute-done.15.refs_1_
  76.9 1.1 %shard_map.111 = (f32[3,96,192]{2,1,0:T(8,128)}, f32[192,96]{1,0:T(8,128)}, f32[3,96,192]{2,1,0:T(8,128)}, f32[192,96]{1,0:T(8,128)}) custom-call(bf16[2,24,768]{2,1,0:T(8,128)(2,1)S(1)} %shard_map.110.refs_0_, bf16[2,24,768]{2,1,0:T(8,128)(2,1)S(1)} %collective-permute-done.15.refs_1_, bf16[2,24,768]{2,1,0:T(8,128)(2,1)S(1)} %collective-permute-done.16.refs_2_, ...), custom_call_target="tpu_custom_call" | custom-call | tf_op jit(solution)/shard_map/pallas_call | solution.py:52
  (2 shorter events, 0.0 us)
Async XLA Ops:
  0.6 25.1 %copy-start.1 = (bf16[3,384,192]{1,2,0:T(8,128)(2,1)S(1)}, bf16[3,384,192]{1,2,0:T(8,128)(2,1)}, u32[]{:S(2)}) copy-start(bf16[3,384,192]{1,2,0:T(8,128)(2,1)} %param.10) | copy-start | bytes 1327108
  0.6 25.0 %copy-start = (bf16[3,384,192]{1,2,0:T(8,128)(2,1)S(1)}, bf16[3,384,192]{1,2,0:T(8,128)(2,1)}, u32[]{:S(2)}) copy-start(bf16[3,384,192]{1,2,0:T(8,128)(2,1)} %param.8) | copy-start | bytes 1327108
  0.7 1.2 %copy-start.2 = (bf16[1,1024,384]{2,1,0:T(8,128)(2,1)S(1)}, bf16[1,1024,384]{2,1,0:T(8,128)(2,1)}, u32[]{:S(2)}) copy-start(bf16[1,1024,384]{2,1,0:T(8,128)(2,1)} %param.6) | copy-start | bytes 2359300
  1.9 10.9 %collective-permute-start = (bf16[256,384]{1,0:T(8,128)(2,1)S(1)}, bf16[256,384]{1,0:T(8,128)(2,1)S(1)}, u32[]{:S(2)}, u32[]{:S(2)}) collective-permute-start(bf16[256,384]{1,0:T(8,128)(2,1)S(1)} %get-tuple-element.49), channel_id=1, source_target_pairs={{0,6},{1,7},{2,4},{3,5},{4,2},{5,3},{6,0},{7,1},{8,14},{9,15},{10,... | collective-permute-start | bytes 589832 | tf_op jit(solution)/shard_map/ppermute | solution.py:289
  7.0 13.0 %collective-permute-start.4 = (bf16[256,384]{1,0:T(8,128)(2,1)S(1)}, bf16[256,384]{1,0:T(8,128)(2,1)S(1)}, u32[]{:S(2)}, u32[]{:S(2)}) collective-permute-start(bf16[256,384]{1,0:T(8,128)(2,1)S(1)} %get-tuple-element.55), channel_id=1, source_target_pairs={{0,2},{1,3},{2,0},{3,1},{4,6},{5,7},{6,4},{7,5},{8,10},{9,11},{10,... | collective-permute-start | bytes 589832 | tf_op jit(solution)/shard_map/ppermute | solution.py:289
  7.1 18.6 %collective-permute-start.5 = (bf16[256,384]{1,0:T(8,128)(2,1)S(1)}, bf16[256,384]{1,0:T(8,128)(2,1)S(1)}, u32[]{:S(2)}, u32[]{:S(2)}) collective-permute-start(bf16[256,384]{1,0:T(8,128)(2,1)S(1)} %get-tuple-element.56), channel_id=1, source_target_pairs={{0,4},{1,5},{2,6},{3,7},{4,0},{5,1},{6,2},{7,3},{8,12},{9,13},{10,... | collective-permute-start | bytes 589832 | tf_op jit(solution)/shard_map/ppermute | solution.py:289
  7.7 1.1 %copy-start.3 = (bf16[1,1024,384]{2,1,0:T(8,128)(2,1)S(1)}, bf16[1,1024,384]{2,1,0:T(8,128)(2,1)}, u32[]{:S(2)}) copy-start(bf16[1,1024,384]{2,1,0:T(8,128)(2,1)} %param.7) | copy-start | bytes 2359300
  8.8 28.6 %copy-start.5 = (bf16[192,384]{1,0:T(8,128)(2,1)S(1)}, bf16[192,384]{1,0:T(8,128)(2,1)}, u32[]{:S(2)}) copy-start(bf16[192,384]{1,0:T(8,128)(2,1)} %refs_11_.1) | copy-start | bytes 442372
  12.8 22.4 %collective-permute-start.1 = (bf16[256,384]{1,0:T(8,128)(2,1)S(1)}, bf16[256,384]{1,0:T(8,128)(2,1)S(1)}, u32[]{:S(2)}, u32[]{:S(2)}) collective-permute-start(bf16[256,384]{1,0:T(8,128)(2,1)S(1)} %get-tuple-element.51), channel_id=1, source_target_pairs={{0,2},{1,3},{2,0},{3,1},{4,6},{5,7},{6,4},{7,5},{8,10},{9,11},{10,... | collective-permute-start | bytes 589832 | tf_op jit(solution)/shard_map/ppermute | solution.py:289
  17.7 19.7 %collective-permute-start.2 = (bf16[256,384]{1,0:T(8,128)(2,1)S(1)}, bf16[256,384]{1,0:T(8,128)(2,1)S(1)}, u32[]{:S(2)}, u32[]{:S(2)}) collective-permute-start(bf16[256,384]{1,0:T(8,128)(2,1)S(1)} %get-tuple-element.52), channel_id=1, source_target_pairs={{0,4},{1,5},{2,6},{3,7},{4,0},{5,1},{6,2},{7,3},{8,12},{9,13},{10,... | collective-permute-start | bytes 589832 | tf_op jit(solution)/shard_map/ppermute | solution.py:289
  18.3 19.1 %collective-permute-start.3 = (bf16[256,384]{1,0:T(8,128)(2,1)S(1)}, bf16[256,384]{1,0:T(8,128)(2,1)S(1)}, u32[]{:S(2)}, u32[]{:S(2)}) collective-permute-start(bf16[256,384]{1,0:T(8,128)(2,1)S(1)} %get-tuple-element.53), channel_id=1, source_target_pairs={{0,6},{1,7},{2,4},{3,5},{4,2},{5,3},{6,0},{7,1},{8,14},{9,15},{10,... | collective-permute-start | bytes 589832 | tf_op jit(solution)/shard_map/ppermute | solution.py:289
  25.7 0.9 %copy-start.4 = (bf16[192,384]{1,0:T(8,128)(2,1)S(1)}, bf16[192,384]{1,0:T(8,128)(2,1)}, u32[]{:S(2)}) copy-start(bf16[192,384]{1,0:T(8,128)(2,1)} %refs_9_.1) | copy-start | bytes 442372
  41.9 3.9 %collective-permute-start.9 = (bf16[2,2,96,768]{3,2,1,0:T(8,128)(2,1)S(1)}, bf16[2,2,96,768]{3,2,1,0:T(8,128)(2,1)S(1)}, u32[]{:S(2)}, u32[]{:S(2)}) collective-permute-start(bf16[2,2,96,768]{3,2,1,0:T(8,128)(2,1)S(1)} %get-tuple-element.74), channel_id=1, source_target_pairs={{0,8},{1,9},{2,10},{3,11},{4,12},{5,13},{6,14},{7,15},{8,0},{9,1},... | collective-permute-start | bytes 1769480 | tf_op jit(solution)/shard_map/ppermute | solution.py:289
  42.0 10.5 %collective-permute-start.6 = (bf16[256,384]{1,0:T(8,128)(2,1)S(1)}, bf16[256,384]{1,0:T(8,128)(2,1)S(1)}, u32[]{:S(2)}, u32[]{:S(2)}) collective-permute-start(bf16[256,384]{1,0:T(8,128)(2,1)S(1)} %get-tuple-element.62), channel_id=1, source_target_pairs={{0,2},{1,3},{2,4},{3,5},{4,6},{5,7},{6,0},{7,1},{8,10},{9,11},{10,... | collective-permute-start | bytes 589832 | tf_op jit(solution)/shard_map/ppermute | solution.py:279
  46.0 7.9 %collective-permute-start.10 = (bf16[2,48,768]{2,1,0:T(8,128)(2,1)S(1)}, bf16[2,48,768]{2,1,0:T(8,128)(2,1)S(1)}, u32[]{:S(2)}, u32[]{:S(2)}) collective-permute-start(bf16[2,48,768]{2,1,0:T(8,128)(2,1)S(1)} %get-tuple-element.76), channel_id=1, source_target_pairs={{0,1},{1,0},{2,3},{3,2},{4,5},{5,4},{6,7},{7,6},{8,9},{9,8},{10,11... | collective-permute-start | bytes 442376 | tf_op jit(solution)/shard_map/ppermute | solution.py:289
  47.6 6.7 %collective-permute-start.11 = (bf16[2,48,768]{2,1,0:T(8,128)(2,1)S(1)}, bf16[2,48,768]{2,1,0:T(8,128)(2,1)S(1)}, u32[]{:S(2)}, u32[]{:S(2)}) collective-permute-start(bf16[2,48,768]{2,1,0:T(8,128)(2,1)S(1)} %get-tuple-element.77), channel_id=1, source_target_pairs={{0,16},{1,17},{2,18},{3,19},{4,20},{5,21},{6,22},{7,23},{8,24},{9,... | collective-permute-start | bytes 442376 | tf_op jit(solution)/shard_map/ppermute | solution.py:289
  49.1 7.2 %collective-permute-start.12 = (bf16[2,48,768]{2,1,0:T(8,128)(2,1)S(1)}, bf16[2,48,768]{2,1,0:T(8,128)(2,1)S(1)}, u32[]{:S(2)}, u32[]{:S(2)}) collective-permute-start(bf16[2,48,768]{2,1,0:T(8,128)(2,1)S(1)} %get-tuple-element.78), channel_id=1, source_target_pairs={{0,17},{1,16},{2,19},{3,18},{4,21},{5,20},{6,23},{7,22},{8,25},{9,... | collective-permute-start | bytes 442376 | tf_op jit(solution)/shard_map/ppermute | solution.py:289
  49.6 12.7 %collective-permute-start.7 = (bf16[256,384]{1,0:T(8,128)(2,1)S(1)}, bf16[256,384]{1,0:T(8,128)(2,1)S(1)}, u32[]{:S(2)}, u32[]{:S(2)}) collective-permute-start(bf16[256,384]{1,0:T(8,128)(2,1)S(1)} %get-tuple-element.63), channel_id=1, source_target_pairs={{0,4},{1,5},{2,6},{3,7},{4,0},{5,1},{6,2},{7,3},{8,12},{9,13},{10,... | collective-permute-start | bytes 589832 | tf_op jit(solution)/shard_map/ppermute | solution.py:279
  52.5 14.2 %collective-permute-start.8 = (bf16[256,384]{1,0:T(8,128)(2,1)S(1)}, bf16[256,384]{1,0:T(8,128)(2,1)S(1)}, u32[]{:S(2)}, u32[]{:S(2)}) collective-permute-start(bf16[256,384]{1,0:T(8,128)(2,1)S(1)} %get-tuple-element.64), channel_id=1, source_target_pairs={{0,6},{1,7},{2,0},{3,1},{4,2},{5,3},{6,4},{7,5},{8,14},{9,15},{10,... | collective-permute-start | bytes 589832 | tf_op jit(solution)/shard_map/ppermute | solution.py:279
  56.4 6.5 %collective-permute-start.13 = (bf16[2,24,768]{2,1,0:T(8,128)(2,1)S(1)}, bf16[2,24,768]{2,1,0:T(8,128)(2,1)S(1)}, u32[]{:S(2)}, u32[]{:S(2)}) collective-permute-start(bf16[2,24,768]{2,1,0:T(8,128)(2,1)S(1)} %get-tuple-element.80), channel_id=1, source_target_pairs={{0,2},{1,3},{2,0},{3,1},{4,6},{5,7},{6,4},{7,5},{8,10},{9,11},{10,... | collective-permute-start | bytes 221192 | tf_op jit(solution)/shard_map/ppermute | solution.py:289
  63.0 6.8 %collective-permute-start.14 = (bf16[2,24,768]{2,1,0:T(8,128)(2,1)S(1)}, bf16[2,24,768]{2,1,0:T(8,128)(2,1)S(1)}, u32[]{:S(2)}, u32[]{:S(2)}) collective-permute-start(bf16[2,24,768]{2,1,0:T(8,128)(2,1)S(1)} %shard_map.109.refs_0_), channel_id=1, source_target_pairs={{0,4},{1,5},{2,6},{3,7},{4,0},{5,1},{6,2},{7,3},{8,12},{9,13},{10,... | collective-permute-start | bytes 221192 | tf_op jit(solution)/shard_map/ppermute | solution.py:289
  69.8 5.3 %collective-permute-start.17 = (bf16[2,24,768]{2,1,0:T(8,128)(2,1)S(1)}, bf16[2,24,768]{2,1,0:T(8,128)(2,1)S(1)}, u32[]{:S(2)}, u32[]{:S(2)}) collective-permute-start(bf16[2,24,768]{2,1,0:T(8,128)(2,1)S(1)} %shard_map.110.refs_0_), channel_id=1, source_target_pairs={{0,3},{1,2},{2,1},{3,0},{4,7},{5,6},{6,5},{7,4},{8,11},{9,10},{10,... | collective-permute-start | bytes 221192 | tf_op jit(solution)/shard_map/ppermute | solution.py:289
  72.5 4.4 %collective-permute-start.16 = (bf16[2,24,768]{2,1,0:T(8,128)(2,1)S(1)}, bf16[2,24,768]{2,1,0:T(8,128)(2,1)S(1)}, u32[]{:S(2)}, u32[]{:S(2)}) collective-permute-start(bf16[2,24,768]{2,1,0:T(8,128)(2,1)S(1)} %shard_map.110.refs_0_), channel_id=1, source_target_pairs={{0,2},{1,3},{2,0},{3,1},{4,6},{5,7},{6,4},{7,5},{8,10},{9,11},{10,... | collective-permute-start | bytes 221192 | tf_op jit(solution)/shard_map/ppermute | solution.py:289
  72.6 4.4 %collective-permute-start.15 = (bf16[2,24,768]{2,1,0:T(8,128)(2,1)S(1)}, bf16[2,24,768]{2,1,0:T(8,128)(2,1)S(1)}, u32[]{:S(2)}, u32[]{:S(2)}) collective-permute-start(bf16[2,24,768]{2,1,0:T(8,128)(2,1)S(1)} %shard_map.110.refs_0_), channel_id=1, source_target_pairs={{0,1},{1,0},{2,3},{3,2},{4,5},{5,4},{6,7},{7,6},{8,9},{9,8},{10,11... | collective-permute-start | bytes 221192 | tf_op jit(solution)/shard_map/ppermute | solution.py:289

commit v5 on v4

--- a/solution.py
+++ b/solution.py
@@ -163,24 +163,32 @@
         mid2_t[:, pl.ds(start, TILE)] = narrow[...].astype(BF16).T
 
 
-def chain_kernel(shifts, hop, n_in, n_out, *refs):
+def chain_kernel(shifts, hop, n_in, *refs):
     parts = refs[:n_in]
-    s_x, s_p1, s_h, s_p2, k1t, p1, k2t, p2 = refs[n_in : n_in + 8]
-    outs = refs[n_in + 8 : n_in + 8 + n_out]
-    g2_rows, pad2, g1_rows, pad1, x_rows = refs[n_in + 8 + n_out :]
+    s_p1, s_h, s_p2, k2t, p1, p2, act1_t, mid1_t, act2_t, mid2_t = refs[n_in : n_in + 10]
+    s_x, k1t = refs[n_in + 10 : n_in + 12]
+    outs = refs[n_in + 12 : -8]
+    keep, send, g1_rows, pad1, g2_rows, pad2, grads, x_rows = refs[-8:]
     place(parts, g2_rows, hop)
-    backward_rows(shifts[1], g2_rows, pad2, s_p2, s_h, k2t, p2, g1_rows)
-    backward_rows(shifts[0], g1_rows, pad1, s_p1, s_x, k1t, p1, x_rows)
+    middle_rows(shifts[1], g2_rows, pad2, s_p2, p2)
+    outer_rows(shifts[1], g2_rows, pad2, s_h, k2t, g1_rows)
+    middle_rows(shifts[0], g1_rows, pad1, s_p1, p1)
+    weights_kernel(
+        shifts[::-1], act2_t, mid2_t, pad2, g2_rows, act1_t, mid1_t, pad1, g1_rows, keep, send, grads
+    )
+    outer_rows(shifts[0], g1_rows, pad1, s_x, k1t, x_rows)
     hand_out(x_rows, outs, hop)
 
 
-def backward_rows(shift, g_rows, pad, s_pre, s_state, kt, point, x_rows):
-    rows = g_rows.shape[0]
+def middle_rows(shift, g_rows, pad, s_pre, point):
     clear_edges(pad, shift)
-    for start in range(0, rows, TILE):
+    for start in range(0, g_rows.shape[0], TILE):
         mid_grad = dot_nt(g_rows[pl.ds(start, TILE), :], point[...])
         pad[pl.ds(start + shift, TILE), :] = (mid_grad * s_pre[pl.ds(start, TILE), :]).astype(BF16)
-    for start in range(0, rows, TILE):
+
+
+def outer_rows(shift, g_rows, pad, s_state, kt, x_rows):
+    for start in range(0, g_rows.shape[0], TILE):
         act_grad = tap_sum(pad, shift, start, TILE, lambda k: kt[2 - k], dot)
         x_rows[pl.ds(start, TILE), :] = (
             g_rows[pl.ds(start, TILE), :].astype(F32) + act_grad * s_state[pl.ds(start, TILE), :]
@@ -195,11 +203,12 @@
         act_t, mid_t, pad, g_rows = refs[4 * i : 4 * i + 4]
         rows = g_rows.shape[0]
         act = act_t[...]
+        near = rows - shift if shift % 128 == 0 else rows
         grads[...] = jnp.concatenate(
             [
-                dot(act, pad[pl.ds(2 * shift, rows), :]),
+                dot(act[:, :near], pad[pl.ds(2 * shift, near), :]),
                 dot(act, pad[pl.ds(shift, rows), :]),
-                dot(act, pad[pl.ds(0, rows), :]),
+                dot(act[:, rows - near :], pad[pl.ds(rows - near, near), :]),
                 dot(mid_t[...], g_rows[...]).T,
             ],
             axis=1,
@@ -396,19 +405,12 @@
         list(x_parts) + [k1t, p1, k2t],
         mib=16,
     )
-    *x_grads, g2_rows, pad2, g1_rows, pad1 = call(
-        functools.partial(chain_kernel, shifts, hop, n_parts, n_parts),
-        [(x_parts[0].shape, BF16)] * n_parts + [whole, pads[1], whole, pads[0]],
-        [whole],
-        list(g_parts) + [s_x, s_p1, s_h, s_p2, k1t, p1, k2t, p2],
-        mib=16,
-    )
     quarters = ((2, 2, channels // 4, 4 * width), BF16)
-    keep, send = call(
-        functools.partial(weights_kernel, (shifts[1], shifts[0])),
-        [quarters, quarters],
-        [((channels, 4 * width), F32)],
-        [act2_t, mid2_t, pad2, g2_rows, act1_t, mid1_t, pad1, g1_rows],
+    *x_grads, keep, send = call(
+        functools.partial(chain_kernel, shifts, hop, n_parts),
+        [(x_parts[0].shape, BF16)] * n_parts + [quarters, quarters],
+        [whole, pads[0], whole, pads[1], ((channels, 4 * width), F32), whole],
+        list(g_parts) + [s_p1, s_h, s_p2, k2t, p1, p2, act1_t, mid1_t, act2_t, mid2_t, s_x, k1t],
         mib=16,
     )
     back, ((conv2, point2), (conv1, point1)) = reduce_weights(keep, send, x_grads, hop, scale)

time: 78.2 us -> 77.5 us (level)
    pallas_call x11 -> x10, Pallas kernels: 15.6 us -> 14.9 us  [call(): pl.pallas_call(body, out_shape=[jax.ShapeDtypeStruct(s, d) for s, d in ou...]
where the time goes in v5:
time: 77.5 us; the launch traced here: 77.3 us
  starting transfers between devices  34 us (44%)
  waiting for transfers between devices  24.4 us (31%)
  Pallas kernels  14.9 us (19%)
  local copies, waits for them, and re-layouts  3.26 us (4%)
    ppermute x15, starting transfers between devices, mirrored(): return lax.ppermute(block, ('dp', 'seq'), route)  25.8 us
    ppermute x15, waiting for transfers between devices, mirrored(): return lax.ppermute(block, ('dp', 'seq'), route)  20.5 us
    pallas_call x10, Pallas kernels, call(): pl.pallas_call(body, out_shape=[jax.ShapeDtypeStruct(s, d) for s, d in ou...  14.9 us
    ppermute x3, starting transfers between devices, send_ahead(): return lax.ppermute(block, 'seq', route)  8.16 us
    ppermute x3, waiting for transfers between devices, send_ahead(): return lax.ppermute(block, 'seq', route)  3.89 us
    unnamed x12, local copies, waits for them, and re-layouts  3.26 us
  transfers between devices with their start and end apart: 18, of which 10 were waited for; matrix products, arithmetic and copies ran while one was open for 0% of the time, Pallas kernels for 13%

profile of v5, /device:TPU:0, one launch (start us, length us, event | category | flops | bytes accessed | tf_op | source)
XLA Modules:
  0.0 77.3 jit_solution(13323171240711325108)
XLA Ops:
  0.6 0.0 copy-start.1
  0.6 0.0 copy-start
  0.7 0.0 copy-start.2
  0.7 1.2 %copy-done.2 = bf16[1,1024,384]{2,1,0:T(8,128)(2,1)S(1)} copy-done((bf16[1,1024,384]{2,1,0:T(8,128)(2,1)S(1)}, bf16[1,1024,384]{2,1,0:T(8,128)(2,1)}, u32[]{:S(2)}) %copy-start.2) | copy-done | bytes 786456
  1.9 0.1 shard_map.102
  1.9 5.1 %collective-permute-start = (bf16[256,384]{1,0:T(8,128)(2,1)S(1)}, bf16[256,384]{1,0:T(8,128)(2,1)S(1)}, u32[]{:S(2)}, u32[]{:S(2)}) collective-permute-start(bf16[256,384]{1,0:T(8,128)(2,1)S(1)} %get-tuple-element.45), channel_id=1, source_target_pairs={{0,6},{1,7},{2,4},{3,5},{4,2},{5,3},{6,0},{7,1},{8,14},{9,15},{10,... | collective-permute-start | bytes 589832 | tf_op jit(solution)/shard_map/ppermute | solution.py:298
  7.0 0.0 collective-permute-start.4
  7.1 0.6 collective-permute-start.5
  7.7 0.0 copy-start.3
  7.7 1.1 %copy-done.3 = bf16[1,1024,384]{2,1,0:T(8,128)(2,1)S(1)} copy-done((bf16[1,1024,384]{2,1,0:T(8,128)(2,1)S(1)}, bf16[1,1024,384]{2,1,0:T(8,128)(2,1)}, u32[]{:S(2)}) %copy-start.3) | copy-done | bytes 786456
  8.8 0.0 copy-start.5
  8.8 0.1 shard_map.101
  8.9 3.9 %collective-permute-done.refs_3_ = bf16[256,384]{1,0:T(8,128)(2,1)S(1)} collective-permute-done((bf16[256,384]{1,0:T(8,128)(2,1)S(1)}, bf16[256,384]{1,0:T(8,128)(2,1)S(1)}, u32[]{:S(2)}, u32[]{:S(2)}) %collective-permute-start) | collective-permute-done | bytes 196640 | tf_op jit(solution)/shard_map/ppermute | solution.py:298
  12.8 4.9 %collective-permute-start.1 = (bf16[256,384]{1,0:T(8,128)(2,1)S(1)}, bf16[256,384]{1,0:T(8,128)(2,1)S(1)}, u32[]{:S(2)}, u32[]{:S(2)}) collective-permute-start(bf16[256,384]{1,0:T(8,128)(2,1)S(1)} %get-tuple-element.47), channel_id=1, source_target_pairs={{0,2},{1,3},{2,0},{3,1},{4,6},{5,7},{6,4},{7,5},{8,10},{9,11},{10,... | collective-permute-start | bytes 589832 | tf_op jit(solution)/shard_map/ppermute | solution.py:298
  17.7 0.7 collective-permute-start.2
  18.3 1.7 %collective-permute-start.3 = (bf16[256,384]{1,0:T(8,128)(2,1)S(1)}, bf16[256,384]{1,0:T(8,128)(2,1)S(1)}, u32[]{:S(2)}, u32[]{:S(2)}) collective-permute-start(bf16[256,384]{1,0:T(8,128)(2,1)S(1)} %get-tuple-element.49), channel_id=1, source_target_pairs={{0,6},{1,7},{2,4},{3,5},{4,2},{5,3},{6,0},{7,1},{8,14},{9,15},{10,... | collective-permute-start | bytes 589832 | tf_op jit(solution)/shard_map/ppermute | solution.py:298
  20.0 0.0 collective-permute-done.4.refs_1_
  20.0 5.6 %collective-permute-done.5.refs_2_ = bf16[256,384]{1,0:T(8,128)(2,1)S(1)} collective-permute-done((bf16[256,384]{1,0:T(8,128)(2,1)S(1)}, bf16[256,384]{1,0:T(8,128)(2,1)S(1)}, u32[]{:S(2)}, u32[]{:S(2)}) %collective-permute-start.5) | collective-permute-done | bytes 196640 | tf_op jit(solution)/shard_map/ppermute | solution.py:298
  25.7 0.0 copy-done.1
  25.7 0.0 copy-done
  25.7 0.0 copy-start.4
  25.7 0.9 %copy-done.4 = bf16[192,384]{1,0:T(8,128)(2,1)S(1)} copy-done((bf16[192,384]{1,0:T(8,128)(2,1)S(1)}, bf16[192,384]{1,0:T(8,128)(2,1)}, u32[]{:S(2)}) %copy-start.4) | copy-done | bytes 147480
  26.6 8.6 %shard_map.103 = (bf16[384,1024]{1,0:T(8,128)(2,1)S(1)}, bf16[192,1024]{1,0:T(8,128)(2,1)S(1)}, f32[1024,384]{1,0:T(8,128)S(1)}, f32[1024,192]{1,0:T(8,128)S(1)}...) custom-call(bf16[256,384]{1,0:T(8,128)(2,1)S(1)} %get-tuple-element., ...), custom_call_target="tpu_custom_call" | custom-call | tf_op jit(solution)/shard_map/pallas_call | solution.py:52
  35.2 0.0 collective-permute-done.1.refs_1_
  35.2 2.1 %collective-permute-done.2.refs_2_ = bf16[256,384]{1,0:T(8,128)(2,1)S(1)} collective-permute-done((bf16[256,384]{1,0:T(8,128)(2,1)S(1)}, bf16[256,384]{1,0:T(8,128)(2,1)S(1)}, u32[]{:S(2)}, u32[]{:S(2)}) %collective-permute-start.2) | collective-permute-done | bytes 196640 | tf_op jit(solution)/shard_map/ppermute | solution.py:298
  37.4 0.0 collective-permute-done.3.refs_3_
  37.4 0.0 copy-done.5
  37.4 3.8 %shard_map.104 = (bf16[256,384]{1,0:T(8,128)(2,1)S(1)}, bf16[256,384]{1,0:T(8,128)(2,1)S(1)}, bf16[256,384]{1,0:T(8,128)(2,1)S(1)}, bf16[256,384]{1,0:T(8,128)(2...) custom-call(bf16[256,384]{1,0:T(8,128)(2,1)S(1)} %get-tuple-element.46.refs_0_, ...), custom_call_target="tpu_custom_call" | custom-call | tf_op jit(solution)/shard_map/pallas_call | solution.py:52
  41.2 0.1 collective-permute-start.9
  41.3 3.9 %collective-permute-start.6 = (bf16[256,384]{1,0:T(8,128)(2,1)S(1)}, bf16[256,384]{1,0:T(8,128)(2,1)S(1)}, u32[]{:S(2)}, u32[]{:S(2)}) collective-permute-start(bf16[256,384]{1,0:T(8,128)(2,1)S(1)} %get-tuple-element.62), channel_id=1, source_target_pairs={{0,2},{1,3},{2,4},{3,5},{4,6},{5,7},{6,0},{7,1},{8,10},{9,11},{10,... | collective-permute-start | bytes 589832 | tf_op jit(solution)/shard_map/ppermute | solution.py:288
  45.1 0.0 collective-permute-done.9.refs_1_
  45.1 0.1 shard_map.106
  45.3 1.6 %collective-permute-start.10 = (bf16[2,48,768]{2,1,0:T(8,128)(2,1)S(1)}, bf16[2,48,768]{2,1,0:T(8,128)(2,1)S(1)}, u32[]{:S(2)}, u32[]{:S(2)}) collective-permute-start(bf16[2,48,768]{2,1,0:T(8,128)(2,1)S(1)} %get-tuple-element.68), channel_id=1, source_target_pairs={{0,1},{1,0},{2,3},{3,2},{4,5},{5,4},{6,7},{7,6},{8,9},{9,8},{10,11... | collective-permute-start | bytes 442376 | tf_op jit(solution)/shard_map/ppermute | solution.py:298
  46.9 1.5 %collective-permute-start.11 = (bf16[2,48,768]{2,1,0:T(8,128)(2,1)S(1)}, bf16[2,48,768]{2,1,0:T(8,128)(2,1)S(1)}, u32[]{:S(2)}, u32[]{:S(2)}) collective-permute-start(bf16[2,48,768]{2,1,0:T(8,128)(2,1)S(1)} %get-tuple-element.69), channel_id=1, source_target_pairs={{0,16},{1,17},{2,18},{3,19},{4,20},{5,21},{6,22},{7,23},{8,24},{9,... | collective-permute-start | bytes 442376 | tf_op jit(solution)/shard_map/ppermute | solution.py:298
  48.4 0.5 collective-permute-start.12
  48.8 2.9 %collective-permute-start.7 = (bf16[256,384]{1,0:T(8,128)(2,1)S(1)}, bf16[256,384]{1,0:T(8,128)(2,1)S(1)}, u32[]{:S(2)}, u32[]{:S(2)}) collective-permute-start(bf16[256,384]{1,0:T(8,128)(2,1)S(1)} %get-tuple-element.63), channel_id=1, source_target_pairs={{0,4},{1,5},{2,6},{3,7},{4,0},{5,1},{6,2},{7,3},{8,12},{9,13},{10,... | collective-permute-start | bytes 589832 | tf_op jit(solution)/shard_map/ppermute | solution.py:288
  51.8 0.0 collective-permute-done.6.refs_1_.refs_4_
  51.8 1.3 %collective-permute-start.8 = (bf16[256,384]{1,0:T(8,128)(2,1)S(1)}, bf16[256,384]{1,0:T(8,128)(2,1)S(1)}, u32[]{:S(2)}, u32[]{:S(2)}) collective-permute-start(bf16[256,384]{1,0:T(8,128)(2,1)S(1)} %get-tuple-element.64), channel_id=1, source_target_pairs={{0,6},{1,7},{2,0},{3,1},{4,2},{5,3},{6,4},{7,5},{8,14},{9,15},{10,... | collective-permute-start | bytes 589832 | tf_op jit(solution)/shard_map/ppermute | solution.py:288
  53.1 0.0 collective-permute-done.10.refs_1_
  53.1 0.5 collective-permute-done.11.refs_2_
  53.6 2.0 %collective-permute-done.12.refs_3_ = bf16[2,48,768]{2,1,0:T(8,128)(2,1)S(1)} collective-permute-done((bf16[2,48,768]{2,1,0:T(8,128)(2,1)S(1)}, bf16[2,48,768]{2,1,0:T(8,128)(2,1)S(1)}, u32[]{:S(2)}, u32[]{:S(2)}) %collective-permute-start.12) | collective-permute-done | bytes 147488 | tf_op jit(solution)/shard_map/ppermute | solution.py:298
  55.6 0.1 shard_map.107
  55.7 2.0 %collective-permute-start.13 = (bf16[2,24,768]{2,1,0:T(8,128)(2,1)S(1)}, bf16[2,24,768]{2,1,0:T(8,128)(2,1)S(1)}, u32[]{:S(2)}, u32[]{:S(2)}) collective-permute-start(bf16[2,24,768]{2,1,0:T(8,128)(2,1)S(1)} %get-tuple-element.72), channel_id=1, source_target_pairs={{0,2},{1,3},{2,0},{3,1},{4,6},{5,7},{6,4},{7,5},{8,10},{9,11},{10,... | collective-permute-start | bytes 221192 | tf_op jit(solution)/shard_map/ppermute | solution.py:298
  57.7 3.9 %collective-permute-done.7.refs_2_ = bf16[256,384]{1,0:T(8,128)(2,1)S(1)} collective-permute-done((bf16[256,384]{1,0:T(8,128)(2,1)S(1)}, bf16[256,384]{1,0:T(8,128)(2,1)S(1)}, u32[]{:S(2)}, u32[]{:S(2)}) %collective-permute-start.7) | collective-permute-done | bytes 196640 | tf_op jit(solution)/shard_map/ppermute | solution.py:288
  61.6 0.7 collective-permute-done.13.refs_1_
  62.2 3.7 %collective-permute-start.14 = (bf16[2,24,768]{2,1,0:T(8,128)(2,1)S(1)}, bf16[2,24,768]{2,1,0:T(8,128)(2,1)S(1)}, u32[]{:S(2)}, u32[]{:S(2)}) collective-permute-start(bf16[2,24,768]{2,1,0:T(8,128)(2,1)S(1)} %shard_map.108.refs_0_), channel_id=1, source_target_pairs={{0,4},{1,5},{2,6},{3,7},{4,0},{5,1},{6,2},{7,3},{8,12},{9,13},{10,... | collective-permute-start | bytes 221192 | tf_op jit(solution)/shard_map/ppermute | solution.py:298
  65.9 0.0 collective-permute-done.8.refs_3_.refs_2_
  65.9 3.1 %collective-permute-done.14.refs_1_ = bf16[2,24,768]{2,1,0:T(8,128)(2,1)S(1)} collective-permute-done((bf16[2,24,768]{2,1,0:T(8,128)(2,1)S(1)}, bf16[2,24,768]{2,1,0:T(8,128)(2,1)S(1)}, u32[]{:S(2)}, u32[]{:S(2)}) %collective-permute-start.14) | collective-permute-done | bytes 73760 | tf_op jit(solution)/shard_map/ppermute | solution.py:298
  69.1 2.7 %collective-permute-start.17 = (bf16[2,24,768]{2,1,0:T(8,128)(2,1)S(1)}, bf16[2,24,768]{2,1,0:T(8,128)(2,1)S(1)}, u32[]{:S(2)}, u32[]{:S(2)}) collective-permute-start(bf16[2,24,768]{2,1,0:T(8,128)(2,1)S(1)} %shard_map.109.refs_0_), channel_id=1, source_target_pairs={{0,3},{1,2},{2,1},{3,0},{4,7},{5,6},{6,5},{7,4},{8,11},{9,10},{10,... | collective-permute-start | bytes 221192 | tf_op jit(solution)/shard_map/ppermute | solution.py:298
  71.8 0.0 collective-permute-start.16
  71.8 0.8 %collective-permute-start.15 = (bf16[2,24,768]{2,1,0:T(8,128)(2,1)S(1)}, bf16[2,24,768]{2,1,0:T(8,128)(2,1)S(1)}, u32[]{:S(2)}, u32[]{:S(2)}) collective-permute-start(bf16[2,24,768]{2,1,0:T(8,128)(2,1)S(1)} %shard_map.109.refs_0_), channel_id=1, source_target_pairs={{0,1},{1,0},{2,3},{3,2},{4,5},{5,4},{6,7},{7,6},{8,9},{9,8},{10,11... | collective-permute-start | bytes 221192 | tf_op jit(solution)/shard_map/ppermute | solution.py:298
  72.6 1.0 %shard_map.105 = bf16[1024,384]{1,0:T(8,128)(2,1)} custom-call(bf16[256,384]{1,0:T(8,128)(2,1)S(1)} %get-tuple-element.61.refs_0_, bf16[256,384]{1,0:T(8,128)(2,1)S(1)} %collective-permute-done.6.refs_1_.refs_4_, bf16[256,384]{1,0:T(8,128)(2,1)S(1)} %collective-permute-done.7.refs_2_, bf16[256,384]{1,0:T(8,128)(2,1)S(1)} %collective-permute-done.8.refs_3_.refs_2_), custom_call_target="tpu_custom_call" | custom-call | tf_op jit(solution)/shard_map/pallas_call | solution.py:52
  73.6 0.8 %collective-permute-done.17.refs_3_ = bf16[2,24,768]{2,1,0:T(8,128)(2,1)S(1)} collective-permute-done((bf16[2,24,768]{2,1,0:T(8,128)(2,1)S(1)}, bf16[2,24,768]{2,1,0:T(8,128)(2,1)S(1)}, u32[]{:S(2)}, u32[]{:S(2)}) %collective-permute-start.17) | collective-permute-done | bytes 73760 | tf_op jit(solution)/shard_map/ppermute | solution.py:298
  74.4 1.8 %collective-permute-done.16.refs_2_ = bf16[2,24,768]{2,1,0:T(8,128)(2,1)S(1)} collective-permute-done((bf16[2,24,768]{2,1,0:T(8,128)(2,1)S(1)}, bf16[2,24,768]{2,1,0:T(8,128)(2,1)S(1)}, u32[]{:S(2)}, u32[]{:S(2)}) %collective-permute-start.16) | collective-permute-done | bytes 73760 | tf_op jit(solution)/shard_map/ppermute | solution.py:298
  76.2 0.0 collective-permute-done.15.refs_1_
  76.2 1.1 %shard_map.110 = (f32[3,96,192]{2,1,0:T(8,128)}, f32[192,96]{1,0:T(8,128)}, f32[3,96,192]{2,1,0:T(8,128)}, f32[192,96]{1,0:T(8,128)}) custom-call(bf16[2,24,768]{2,1,0:T(8,128)(2,1)S(1)} %shard_map.109.refs_0_, bf16[2,24,768]{2,1,0:T(8,128)(2,1)S(1)} %collective-permute-done.15.refs_1_, bf16[2,24,768]{2,1,0:T(8,128)(2,1)S(1)} %collective-permute-done.16.refs_2_, ...), custom_call_target="tpu_custom_call" | custom-call | tf_op jit(solution)/shard_map/pallas_call | solution.py:52
  (2 shorter events, 0.0 us)
Async XLA Ops:
  0.6 25.1 %copy-start.1 = (bf16[3,384,192]{1,2,0:T(8,128)(2,1)S(1)}, bf16[3,384,192]{1,2,0:T(8,128)(2,1)}, u32[]{:S(2)}) copy-start(bf16[3,384,192]{1,2,0:T(8,128)(2,1)} %param.10) | copy-start | bytes 1327108
  0.6 25.0 %copy-start = (bf16[3,384,192]{1,2,0:T(8,128)(2,1)S(1)}, bf16[3,384,192]{1,2,0:T(8,128)(2,1)}, u32[]{:S(2)}) copy-start(bf16[3,384,192]{1,2,0:T(8,128)(2,1)} %param.8) | copy-start | bytes 1327108
  0.7 1.2 %copy-start.2 = (bf16[1,1024,384]{2,1,0:T(8,128)(2,1)S(1)}, bf16[1,1024,384]{2,1,0:T(8,128)(2,1)}, u32[]{:S(2)}) copy-start(bf16[1,1024,384]{2,1,0:T(8,128)(2,1)} %param.6) | copy-start | bytes 2359300
  1.9 10.9 %collective-permute-start = (bf16[256,384]{1,0:T(8,128)(2,1)S(1)}, bf16[256,384]{1,0:T(8,128)(2,1)S(1)}, u32[]{:S(2)}, u32[]{:S(2)}) collective-permute-start(bf16[256,384]{1,0:T(8,128)(2,1)S(1)} %get-tuple-element.45), channel_id=1, source_target_pairs={{0,6},{1,7},{2,4},{3,5},{4,2},{5,3},{6,0},{7,1},{8,14},{9,15},{10,... | collective-permute-start | bytes 589832 | tf_op jit(solution)/shard_map/ppermute | solution.py:298
  7.0 13.0 %collective-permute-start.4 = (bf16[256,384]{1,0:T(8,128)(2,1)S(1)}, bf16[256,384]{1,0:T(8,128)(2,1)S(1)}, u32[]{:S(2)}, u32[]{:S(2)}) collective-permute-start(bf16[256,384]{1,0:T(8,128)(2,1)S(1)} %get-tuple-element.51), channel_id=1, source_target_pairs={{0,2},{1,3},{2,0},{3,1},{4,6},{5,7},{6,4},{7,5},{8,10},{9,11},{10,... | collective-permute-start | bytes 589832 | tf_op jit(solution)/shard_map/ppermute | solution.py:298
  7.1 18.6 %collective-permute-start.5 = (bf16[256,384]{1,0:T(8,128)(2,1)S(1)}, bf16[256,384]{1,0:T(8,128)(2,1)S(1)}, u32[]{:S(2)}, u32[]{:S(2)}) collective-permute-start(bf16[256,384]{1,0:T(8,128)(2,1)S(1)} %get-tuple-element.52), channel_id=1, source_target_pairs={{0,4},{1,5},{2,6},{3,7},{4,0},{5,1},{6,2},{7,3},{8,12},{9,13},{10,... | collective-permute-start | bytes 589832 | tf_op jit(solution)/shard_map/ppermute | solution.py:298
  7.7 1.1 %copy-start.3 = (bf16[1,1024,384]{2,1,0:T(8,128)(2,1)S(1)}, bf16[1,1024,384]{2,1,0:T(8,128)(2,1)}, u32[]{:S(2)}) copy-start(bf16[1,1024,384]{2,1,0:T(8,128)(2,1)} %param.7) | copy-start | bytes 2359300
  8.8 28.6 %copy-start.5 = (bf16[192,384]{1,0:T(8,128)(2,1)S(1)}, bf16[192,384]{1,0:T(8,128)(2,1)}, u32[]{:S(2)}) copy-start(bf16[192,384]{1,0:T(8,128)(2,1)} %refs_9_.1) | copy-start | bytes 442372
  12.8 22.4 %collective-permute-start.1 = (bf16[256,384]{1,0:T(8,128)(2,1)S(1)}, bf16[256,384]{1,0:T(8,128)(2,1)S(1)}, u32[]{:S(2)}, u32[]{:S(2)}) collective-permute-start(bf16[256,384]{1,0:T(8,128)(2,1)S(1)} %get-tuple-element.47), channel_id=1, source_target_pairs={{0,2},{1,3},{2,0},{3,1},{4,6},{5,7},{6,4},{7,5},{8,10},{9,11},{10,... | collective-permute-start | bytes 589832 | tf_op jit(solution)/shard_map/ppermute | solution.py:298
  17.7 19.7 %collective-permute-start.2 = (bf16[256,384]{1,0:T(8,128)(2,1)S(1)}, bf16[256,384]{1,0:T(8,128)(2,1)S(1)}, u32[]{:S(2)}, u32[]{:S(2)}) collective-permute-start(bf16[256,384]{1,0:T(8,128)(2,1)S(1)} %get-tuple-element.48), channel_id=1, source_target_pairs={{0,4},{1,5},{2,6},{3,7},{4,0},{5,1},{6,2},{7,3},{8,12},{9,13},{10,... | collective-permute-start | bytes 589832 | tf_op jit(solution)/shard_map/ppermute | solution.py:298
  18.3 19.1 %collective-permute-start.3 = (bf16[256,384]{1,0:T(8,128)(2,1)S(1)}, bf16[256,384]{1,0:T(8,128)(2,1)S(1)}, u32[]{:S(2)}, u32[]{:S(2)}) collective-permute-start(bf16[256,384]{1,0:T(8,128)(2,1)S(1)} %get-tuple-element.49), channel_id=1, source_target_pairs={{0,6},{1,7},{2,4},{3,5},{4,2},{5,3},{6,0},{7,1},{8,14},{9,15},{10,... | collective-permute-start | bytes 589832 | tf_op jit(solution)/shard_map/ppermute | solution.py:298
  25.7 0.9 %copy-start.4 = (bf16[192,384]{1,0:T(8,128)(2,1)S(1)}, bf16[192,384]{1,0:T(8,128)(2,1)}, u32[]{:S(2)}) copy-start(bf16[192,384]{1,0:T(8,128)(2,1)} %refs_8_.1) | copy-start | bytes 442372
  41.2 3.9 %collective-permute-start.9 = (bf16[2,2,96,768]{3,2,1,0:T(8,128)(2,1)S(1)}, bf16[2,2,96,768]{3,2,1,0:T(8,128)(2,1)S(1)}, u32[]{:S(2)}, u32[]{:S(2)}) collective-permute-start(bf16[2,2,96,768]{3,2,1,0:T(8,128)(2,1)S(1)} %get-tuple-element.66), channel_id=1, source_target_pairs={{0,8},{1,9},{2,10},{3,11},{4,12},{5,13},{6,14},{7,15},{8,0},{9,1},... | collective-permute-start | bytes 1769480 | tf_op jit(solution)/shard_map/ppermute | solution.py:298
  41.3 10.5 %collective-permute-start.6 = (bf16[256,384]{1,0:T(8,128)(2,1)S(1)}, bf16[256,384]{1,0:T(8,128)(2,1)S(1)}, u32[]{:S(2)}, u32[]{:S(2)}) collective-permute-start(bf16[256,384]{1,0:T(8,128)(2,1)S(1)} %get-tuple-element.62), channel_id=1, source_target_pairs={{0,2},{1,3},{2,4},{3,5},{4,6},{5,7},{6,0},{7,1},{8,10},{9,11},{10,... | collective-permute-start | bytes 589832 | tf_op jit(solution)/shard_map/ppermute | solution.py:288
  45.3 7.9 %collective-permute-start.10 = (bf16[2,48,768]{2,1,0:T(8,128)(2,1)S(1)}, bf16[2,48,768]{2,1,0:T(8,128)(2,1)S(1)}, u32[]{:S(2)}, u32[]{:S(2)}) collective-permute-start(bf16[2,48,768]{2,1,0:T(8,128)(2,1)S(1)} %get-tuple-element.68), channel_id=1, source_target_pairs={{0,1},{1,0},{2,3},{3,2},{4,5},{5,4},{6,7},{7,6},{8,9},{9,8},{10,11... | collective-permute-start | bytes 442376 | tf_op jit(solution)/shard_map/ppermute | solution.py:298
  46.9 6.7 %collective-permute-start.11 = (bf16[2,48,768]{2,1,0:T(8,128)(2,1)S(1)}, bf16[2,48,768]{2,1,0:T(8,128)(2,1)S(1)}, u32[]{:S(2)}, u32[]{:S(2)}) collective-permute-start(bf16[2,48,768]{2,1,0:T(8,128)(2,1)S(1)} %get-tuple-element.69), channel_id=1, source_target_pairs={{0,16},{1,17},{2,18},{3,19},{4,20},{5,21},{6,22},{7,23},{8,24},{9,... | collective-permute-start | bytes 442376 | tf_op jit(solution)/shard_map/ppermute | solution.py:298
  48.4 7.2 %collective-permute-start.12 = (bf16[2,48,768]{2,1,0:T(8,128)(2,1)S(1)}, bf16[2,48,768]{2,1,0:T(8,128)(2,1)S(1)}, u32[]{:S(2)}, u32[]{:S(2)}) collective-permute-start(bf16[2,48,768]{2,1,0:T(8,128)(2,1)S(1)} %get-tuple-element.70), channel_id=1, source_target_pairs={{0,17},{1,16},{2,19},{3,18},{4,21},{5,20},{6,23},{7,22},{8,25},{9,... | collective-permute-start | bytes 442376 | tf_op jit(solution)/shard_map/ppermute | solution.py:298
  48.8 12.7 %collective-permute-start.7 = (bf16[256,384]{1,0:T(8,128)(2,1)S(1)}, bf16[256,384]{1,0:T(8,128)(2,1)S(1)}, u32[]{:S(2)}, u32[]{:S(2)}) collective-permute-start(bf16[256,384]{1,0:T(8,128)(2,1)S(1)} %get-tuple-element.63), channel_id=1, source_target_pairs={{0,4},{1,5},{2,6},{3,7},{4,0},{5,1},{6,2},{7,3},{8,12},{9,13},{10,... | collective-permute-start | bytes 589832 | tf_op jit(solution)/shard_map/ppermute | solution.py:288
  51.8 14.2 %collective-permute-start.8 = (bf16[256,384]{1,0:T(8,128)(2,1)S(1)}, bf16[256,384]{1,0:T(8,128)(2,1)S(1)}, u32[]{:S(2)}, u32[]{:S(2)}) collective-permute-start(bf16[256,384]{1,0:T(8,128)(2,1)S(1)} %get-tuple-element.64), channel_id=1, source_target_pairs={{0,6},{1,7},{2,0},{3,1},{4,2},{5,3},{6,4},{7,5},{8,14},{9,15},{10,... | collective-permute-start | bytes 589832 | tf_op jit(solution)/shard_map/ppermute | solution.py:288
  55.7 6.5 %collective-permute-start.13 = (bf16[2,24,768]{2,1,0:T(8,128)(2,1)S(1)}, bf16[2,24,768]{2,1,0:T(8,128)(2,1)S(1)}, u32[]{:S(2)}, u32[]{:S(2)}) collective-permute-start(bf16[2,24,768]{2,1,0:T(8,128)(2,1)S(1)} %get-tuple-element.72), channel_id=1, source_target_pairs={{0,2},{1,3},{2,0},{3,1},{4,6},{5,7},{6,4},{7,5},{8,10},{9,11},{10,... | collective-permute-start | bytes 221192 | tf_op jit(solution)/shard_map/ppermute | solution.py:298
  62.2 6.8 %collective-permute-start.14 = (bf16[2,24,768]{2,1,0:T(8,128)(2,1)S(1)}, bf16[2,24,768]{2,1,0:T(8,128)(2,1)S(1)}, u32[]{:S(2)}, u32[]{:S(2)}) collective-permute-start(bf16[2,24,768]{2,1,0:T(8,128)(2,1)S(1)} %shard_map.108.refs_0_), channel_id=1, source_target_pairs={{0,4},{1,5},{2,6},{3,7},{4,0},{5,1},{6,2},{7,3},{8,12},{9,13},{10,... | collective-permute-start | bytes 221192 | tf_op jit(solution)/shard_map/ppermute | solution.py:298
  69.1 5.3 %collective-permute-start.17 = (bf16[2,24,768]{2,1,0:T(8,128)(2,1)S(1)}, bf16[2,24,768]{2,1,0:T(8,128)(2,1)S(1)}, u32[]{:S(2)}, u32[]{:S(2)}) collective-permute-start(bf16[2,24,768]{2,1,0:T(8,128)(2,1)S(1)} %shard_map.109.refs_0_), channel_id=1, source_target_pairs={{0,3},{1,2},{2,1},{3,0},{4,7},{5,6},{6,5},{7,4},{8,11},{9,10},{10,... | collective-permute-start | bytes 221192 | tf_op jit(solution)/shard_map/ppermute | solution.py:298
  71.8 4.4 %collective-permute-start.16 = (bf16[2,24,768]{2,1,0:T(8,128)(2,1)S(1)}, bf16[2,24,768]{2,1,0:T(8,128)(2,1)S(1)}, u32[]{:S(2)}, u32[]{:S(2)}) collective-permute-start(bf16[2,24,768]{2,1,0:T(8,128)(2,1)S(1)} %shard_map.109.refs_0_), channel_id=1, source_target_pairs={{0,2},{1,3},{2,0},{3,1},{4,6},{5,7},{6,4},{7,5},{8,10},{9,11},{10,... | collective-permute-start | bytes 221192 | tf_op jit(solution)/shard_map/ppermute | solution.py:298
  71.8 4.4 %collective-permute-start.15 = (bf16[2,24,768]{2,1,0:T(8,128)(2,1)S(1)}, bf16[2,24,768]{2,1,0:T(8,128)(2,1)S(1)}, u32[]{:S(2)}, u32[]{:S(2)}) collective-permute-start(bf16[2,24,768]{2,1,0:T(8,128)(2,1)S(1)} %shard_map.109.refs_0_), channel_id=1, source_target_pairs={{0,1},{1,0},{2,3},{3,2},{4,5},{5,4},{6,7},{7,6},{8,9},{9,8},{10,11... | collective-permute-start | bytes 221192 | tf_op jit(solution)/shard_map/ppermute | solution.py:298

commit v6 on v5

--- a/solution.py
+++ b/solution.py
@@ -11,9 +11,10 @@
 DILATION_ONE = 2048
 DILATION_TWO = 4096
 TILE = 256
+WIDE_TILE = 512
 CHUNK = 32
 MAX_PERMUTES = 4
-NEED = ((1,), (2,), (3,))
+NEED = ((3,), (1,), (2,))
 ORDER = (2, 3, 1)
 GATE = (3,)
 BF16 = jnp.bfloat16
@@ -103,6 +104,8 @@
 
 
 def clear_edges(padded_ref, shift):
+    if shift % TILE == 0:
+        return
     rows = padded_ref.shape[0]
     zeros = jnp.zeros((shift, padded_ref.shape[1]), padded_ref.dtype)
     padded_ref[pl.ds(0, shift), :] = zeros
@@ -182,9 +185,9 @@
 
 def middle_rows(shift, g_rows, pad, s_pre, point):
     clear_edges(pad, shift)
-    for start in range(0, g_rows.shape[0], TILE):
-        mid_grad = dot_nt(g_rows[pl.ds(start, TILE), :], point[...])
-        pad[pl.ds(start + shift, TILE), :] = (mid_grad * s_pre[pl.ds(start, TILE), :]).astype(BF16)
+    for start in range(0, g_rows.shape[0], WIDE_TILE):
+        mid_grad = dot_nt(g_rows[pl.ds(start, WIDE_TILE), :], point[...])
+        pad[pl.ds(start + shift, WIDE_TILE), :] = (mid_grad * s_pre[pl.ds(start, WIDE_TILE), :]).astype(BF16)
 
 
 def outer_rows(shift, g_rows, pad, s_state, kt, x_rows):

time: 77.5 us -> 77.2 us (level)
  waiting for transfers between devices: 24.4 us -> 22.4 us
  starting transfers between devices: 34 us -> 35.8 us
    ppermute x3, waiting for transfers between devices: 3.89 us -> 2.44 us  [send_ahead(): return lax.ppermute(block, 'seq', route)]
    ppermute x15, starting transfers between devices: 25.8 us -> 26.9 us  [mirrored(): return lax.ppermute(block, ('dp', 'seq'), route)]
where the time goes in v6:
time: 77.2 us; the launch traced here: 77 us
  starting transfers between devices  35.8 us (46%)
  waiting for transfers between devices  22.4 us (29%)
  Pallas kernels  14.7 us (19%)
  local copies, waits for them, and re-layouts  3.26 us (4%)
    ppermute x15, starting transfers between devices, mirrored(): return lax.ppermute(block, ('dp', 'seq'), route)  26.9 us
    ppermute x15, waiting for transfers between devices, mirrored(): return lax.ppermute(block, ('dp', 'seq'), route)  20 us
    pallas_call x10, Pallas kernels, call(): pl.pallas_call(body, out_shape=[jax.ShapeDtypeStruct(s, d) for s, d in ou...  14.7 us
    ppermute x3, starting transfers between devices, send_ahead(): return lax.ppermute(block, 'seq', route)  8.88 us
    unnamed x12, local copies, waits for them, and re-layouts  3.26 us
    ppermute x3, waiting for transfers between devices, send_ahead(): return lax.ppermute(block, 'seq', route)  2.44 us
  transfers between devices with their start and end apart: 18, of which 10 were waited for; matrix products, arithmetic and copies ran while one was open for 0% of the time, Pallas kernels for 13%

profile of v6, /device:TPU:0, one launch (start us, length us, event | category | flops | bytes accessed | tf_op | source)
XLA Modules:
  0.0 77.0 jit_solution(6731689890877519351)
XLA Ops:
  0.6 0.0 copy-start.1
  0.6 0.0 copy-start
  0.7 0.0 copy-start.2
  0.7 1.2 %copy-done.2 = bf16[1,1024,384]{2,1,0:T(8,128)(2,1)S(1)} copy-done((bf16[1,1024,384]{2,1,0:T(8,128)(2,1)S(1)}, bf16[1,1024,384]{2,1,0:T(8,128)(2,1)}, u32[]{:S(2)}) %copy-start.2) | copy-done | bytes 786456
  1.9 0.1 shard_map.102
  1.9 5.1 %collective-permute-start = (bf16[256,384]{1,0:T(8,128)(2,1)S(1)}, bf16[256,384]{1,0:T(8,128)(2,1)S(1)}, u32[]{:S(2)}, u32[]{:S(2)}) collective-permute-start(bf16[256,384]{1,0:T(8,128)(2,1)S(1)} %get-tuple-element.45), channel_id=1, source_target_pairs={{0,6},{1,7},{2,4},{3,5},{4,2},{5,3},{6,0},{7,1},{8,14},{9,15},{10,... | collective-permute-start | bytes 589832 | tf_op jit(solution)/shard_map/ppermute | solution.py:301
  7.0 0.0 collective-permute-start.4
  7.1 0.6 collective-permute-start.5
  7.7 0.0 copy-start.3
  7.7 1.1 %copy-done.3 = bf16[1,1024,384]{2,1,0:T(8,128)(2,1)S(1)} copy-done((bf16[1,1024,384]{2,1,0:T(8,128)(2,1)S(1)}, bf16[1,1024,384]{2,1,0:T(8,128)(2,1)}, u32[]{:S(2)}) %copy-start.3) | copy-done | bytes 786456
  8.8 0.0 copy-start.5
  8.8 0.1 shard_map.101
  8.9 3.9 %collective-permute-done.refs_3_ = bf16[256,384]{1,0:T(8,128)(2,1)S(1)} collective-permute-done((bf16[256,384]{1,0:T(8,128)(2,1)S(1)}, bf16[256,384]{1,0:T(8,128)(2,1)S(1)}, u32[]{:S(2)}, u32[]{:S(2)}) %collective-permute-start) | collective-permute-done | bytes 196640 | tf_op jit(solution)/shard_map/ppermute | solution.py:301
  12.8 4.9 %collective-permute-start.1 = (bf16[256,384]{1,0:T(8,128)(2,1)S(1)}, bf16[256,384]{1,0:T(8,128)(2,1)S(1)}, u32[]{:S(2)}, u32[]{:S(2)}) collective-permute-start(bf16[256,384]{1,0:T(8,128)(2,1)S(1)} %get-tuple-element.47), channel_id=1, source_target_pairs={{0,2},{1,3},{2,0},{3,1},{4,6},{5,7},{6,4},{7,5},{8,10},{9,11},{10,... | collective-permute-start | bytes 589832 | tf_op jit(solution)/shard_map/ppermute | solution.py:301
  17.7 0.7 collective-permute-start.2
  18.3 1.7 %collective-permute-start.3 = (bf16[256,384]{1,0:T(8,128)(2,1)S(1)}, bf16[256,384]{1,0:T(8,128)(2,1)S(1)}, u32[]{:S(2)}, u32[]{:S(2)}) collective-permute-start(bf16[256,384]{1,0:T(8,128)(2,1)S(1)} %get-tuple-element.49), channel_id=1, source_target_pairs={{0,6},{1,7},{2,4},{3,5},{4,2},{5,3},{6,0},{7,1},{8,14},{9,15},{10,... | collective-permute-start | bytes 589832 | tf_op jit(solution)/shard_map/ppermute | solution.py:301
  20.0 0.0 collective-permute-done.4.refs_1_
  20.0 5.6 %collective-permute-done.5.refs_2_ = bf16[256,384]{1,0:T(8,128)(2,1)S(1)} collective-permute-done((bf16[256,384]{1,0:T(8,128)(2,1)S(1)}, bf16[256,384]{1,0:T(8,128)(2,1)S(1)}, u32[]{:S(2)}, u32[]{:S(2)}) %collective-permute-start.5) | collective-permute-done | bytes 196640 | tf_op jit(solution)/shard_map/ppermute | solution.py:301
  25.7 0.0 copy-done.1
  25.7 0.0 copy-done
  25.7 0.0 copy-start.4
  25.7 0.9 %copy-done.4 = bf16[192,384]{1,0:T(8,128)(2,1)S(1)} copy-done((bf16[192,384]{1,0:T(8,128)(2,1)S(1)}, bf16[192,384]{1,0:T(8,128)(2,1)}, u32[]{:S(2)}) %copy-start.4) | copy-done | bytes 147480
  26.6 8.6 %shard_map.103 = (bf16[384,1024]{1,0:T(8,128)(2,1)S(1)}, bf16[192,1024]{1,0:T(8,128)(2,1)S(1)}, f32[1024,384]{1,0:T(8,128)S(1)}, f32[1024,192]{1,0:T(8,128)S(1)}...) custom-call(bf16[256,384]{1,0:T(8,128)(2,1)S(1)} %get-tuple-element., ...), custom_call_target="tpu_custom_call" | custom-call | tf_op jit(solution)/shard_map/pallas_call | solution.py:53
  35.2 0.0 collective-permute-done.1.refs_1_
  35.2 2.1 %collective-permute-done.2.refs_2_ = bf16[256,384]{1,0:T(8,128)(2,1)S(1)} collective-permute-done((bf16[256,384]{1,0:T(8,128)(2,1)S(1)}, bf16[256,384]{1,0:T(8,128)(2,1)S(1)}, u32[]{:S(2)}, u32[]{:S(2)}) %collective-permute-start.2) | collective-permute-done | bytes 196640 | tf_op jit(solution)/shard_map/ppermute | solution.py:301
  37.4 0.0 collective-permute-done.3.refs_3_
  37.4 0.0 copy-done.5
  37.4 3.6 %shard_map.104 = (bf16[256,384]{1,0:T(8,128)(2,1)S(1)}, bf16[256,384]{1,0:T(8,128)(2,1)S(1)}, bf16[256,384]{1,0:T(8,128)(2,1)S(1)}, bf16[256,384]{1,0:T(8,128)(2...) custom-call(bf16[256,384]{1,0:T(8,128)(2,1)S(1)} %get-tuple-element.46.refs_0_, ...), custom_call_target="tpu_custom_call" | custom-call | tf_op jit(solution)/shard_map/pallas_call | solution.py:53
  41.0 0.1 collective-permute-start.9
  41.1 2.7 %collective-permute-start.8 = (bf16[256,384]{1,0:T(8,128)(2,1)S(1)}, bf16[256,384]{1,0:T(8,128)(2,1)S(1)}, u32[]{:S(2)}, u32[]{:S(2)}) collective-permute-start(bf16[256,384]{1,0:T(8,128)(2,1)S(1)} %get-tuple-element.64), channel_id=1, source_target_pairs={{0,6},{1,7},{2,0},{3,1},{4,2},{5,3},{6,4},{7,5},{8,14},{9,15},{10,... | collective-permute-start | bytes 589832 | tf_op jit(solution)/shard_map/ppermute | solution.py:291
  43.8 0.0 collective-permute-done.9.refs_1_
  43.8 0.1 shard_map.106
  44.0 1.6 %collective-permute-start.10 = (bf16[2,48,768]{2,1,0:T(8,128)(2,1)S(1)}, bf16[2,48,768]{2,1,0:T(8,128)(2,1)S(1)}, u32[]{:S(2)}, u32[]{:S(2)}) collective-permute-start(bf16[2,48,768]{2,1,0:T(8,128)(2,1)S(1)} %get-tuple-element.68), channel_id=1, source_target_pairs={{0,1},{1,0},{2,3},{3,2},{4,5},{5,4},{6,7},{7,6},{8,9},{9,8},{10,11... | collective-permute-start | bytes 442376 | tf_op jit(solution)/shard_map/ppermute | solution.py:301
  45.6 1.5 %collective-permute-start.11 = (bf16[2,48,768]{2,1,0:T(8,128)(2,1)S(1)}, bf16[2,48,768]{2,1,0:T(8,128)(2,1)S(1)}, u32[]{:S(2)}, u32[]{:S(2)}) collective-permute-start(bf16[2,48,768]{2,1,0:T(8,128)(2,1)S(1)} %get-tuple-element.69), channel_id=1, source_target_pairs={{0,16},{1,17},{2,18},{3,19},{4,20},{5,21},{6,22},{7,23},{8,24},{9,... | collective-permute-start | bytes 442376 | tf_op jit(solution)/shard_map/ppermute | solution.py:301
  47.0 0.5 collective-permute-start.12
  47.5 3.1 %collective-permute-start.6 = (bf16[256,384]{1,0:T(8,128)(2,1)S(1)}, bf16[256,384]{1,0:T(8,128)(2,1)S(1)}, u32[]{:S(2)}, u32[]{:S(2)}) collective-permute-start(bf16[256,384]{1,0:T(8,128)(2,1)S(1)} %get-tuple-element.62), channel_id=1, source_target_pairs={{0,2},{1,3},{2,4},{3,5},{4,6},{5,7},{6,0},{7,1},{8,10},{9,11},{10,... | collective-permute-start | bytes 589832 | tf_op jit(solution)/shard_map/ppermute | solution.py:291
  50.6 0.0 collective-permute-done.8.refs_3_.refs_4_
  50.6 3.1 %collective-permute-start.7 = (bf16[256,384]{1,0:T(8,128)(2,1)S(1)}, bf16[256,384]{1,0:T(8,128)(2,1)S(1)}, u32[]{:S(2)}, u32[]{:S(2)}) collective-permute-start(bf16[256,384]{1,0:T(8,128)(2,1)S(1)} %get-tuple-element.63), channel_id=1, source_target_pairs={{0,4},{1,5},{2,6},{3,7},{4,0},{5,1},{6,2},{7,3},{8,12},{9,13},{10,... | collective-permute-start | bytes 589832 | tf_op jit(solution)/shard_map/ppermute | solution.py:291
  53.7 0.0 collective-permute-done.10.refs_1_
  53.7 0.0 collective-permute-done.11.refs_2_
  53.7 0.6 collective-permute-done.12.refs_3_
  54.3 0.1 shard_map.107
  54.4 3.1 %collective-permute-start.13 = (bf16[2,24,768]{2,1,0:T(8,128)(2,1)S(1)}, bf16[2,24,768]{2,1,0:T(8,128)(2,1)S(1)}, u32[]{:S(2)}, u32[]{:S(2)}) collective-permute-start(bf16[2,24,768]{2,1,0:T(8,128)(2,1)S(1)} %get-tuple-element.72), channel_id=1, source_target_pairs={{0,2},{1,3},{2,0},{3,1},{4,6},{5,7},{6,4},{7,5},{8,10},{9,11},{10,... | collective-permute-start | bytes 221192 | tf_op jit(solution)/shard_map/ppermute | solution.py:301
  57.5 0.0 collective-permute-done.6.refs_1_.refs_2_
  57.5 2.5 %collective-permute-done.13.refs_1_ = bf16[2,24,768]{2,1,0:T(8,128)(2,1)S(1)} collective-permute-done((bf16[2,24,768]{2,1,0:T(8,128)(2,1)S(1)}, bf16[2,24,768]{2,1,0:T(8,128)(2,1)S(1)}, u32[]{:S(2)}, u32[]{:S(2)}) %collective-permute-start.13) | collective-permute-done | bytes 73760 | tf_op jit(solution)/shard_map/ppermute | solution.py:301
  60.1 3.7 %collective-permute-start.14 = (bf16[2,24,768]{2,1,0:T(8,128)(2,1)S(1)}, bf16[2,24,768]{2,1,0:T(8,128)(2,1)S(1)}, u32[]{:S(2)}, u32[]{:S(2)}) collective-permute-start(bf16[2,24,768]{2,1,0:T(8,128)(2,1)S(1)} %shard_map.108.refs_0_), channel_id=1, source_target_pairs={{0,4},{1,5},{2,6},{3,7},{4,0},{5,1},{6,2},{7,3},{8,12},{9,13},{10,... | collective-permute-start | bytes 221192 | tf_op jit(solution)/shard_map/ppermute | solution.py:301
  63.8 2.4 %collective-permute-done.7.refs_2_ = bf16[256,384]{1,0:T(8,128)(2,1)S(1)} collective-permute-done((bf16[256,384]{1,0:T(8,128)(2,1)S(1)}, bf16[256,384]{1,0:T(8,128)(2,1)S(1)}, u32[]{:S(2)}, u32[]{:S(2)}) %collective-permute-start.7) | collective-permute-done | bytes 196640 | tf_op jit(solution)/shard_map/ppermute | solution.py:291
  66.2 2.3 %collective-permute-done.14.refs_1_ = bf16[2,24,768]{2,1,0:T(8,128)(2,1)S(1)} collective-permute-done((bf16[2,24,768]{2,1,0:T(8,128)(2,1)S(1)}, bf16[2,24,768]{2,1,0:T(8,128)(2,1)S(1)}, u32[]{:S(2)}, u32[]{:S(2)}) %collective-permute-start.14) | collective-permute-done | bytes 73760 | tf_op jit(solution)/shard_map/ppermute | solution.py:301
  68.5 0.5 collective-permute-start.17
  69.0 2.5 %collective-permute-start.16 = (bf16[2,24,768]{2,1,0:T(8,128)(2,1)S(1)}, bf16[2,24,768]{2,1,0:T(8,128)(2,1)S(1)}, u32[]{:S(2)}, u32[]{:S(2)}) collective-permute-start(bf16[2,24,768]{2,1,0:T(8,128)(2,1)S(1)} %shard_map.109.refs_0_), channel_id=1, source_target_pairs={{0,2},{1,3},{2,0},{3,1},{4,6},{5,7},{6,4},{7,5},{8,10},{9,11},{10,... | collective-permute-start | bytes 221192 | tf_op jit(solution)/shard_map/ppermute | solution.py:301
  71.5 0.5 collective-permute-start.15
  72.1 1.0 %shard_map.105 = bf16[1024,384]{1,0:T(8,128)(2,1)} custom-call(bf16[256,384]{1,0:T(8,128)(2,1)S(1)} %get-tuple-element.61.refs_0_, bf16[256,384]{1,0:T(8,128)(2,1)S(1)} %collective-permute-done.6.refs_1_.refs_2_, bf16[256,384]{1,0:T(8,128)(2,1)S(1)} %collective-permute-done.7.refs_2_, bf16[256,384]{1,0:T(8,128)(2,1)S(1)} %collective-permute-done.8.refs_3_.refs_4_), custom_call_target="tpu_custom_call" | custom-call | tf_op jit(solution)/shard_map/pallas_call | solution.py:53
  73.0 1.5 %collective-permute-done.17.refs_3_ = bf16[2,24,768]{2,1,0:T(8,128)(2,1)S(1)} collective-permute-done((bf16[2,24,768]{2,1,0:T(8,128)(2,1)S(1)}, bf16[2,24,768]{2,1,0:T(8,128)(2,1)S(1)}, u32[]{:S(2)}, u32[]{:S(2)}) %collective-permute-start.17) | collective-permute-done | bytes 73760 | tf_op jit(solution)/shard_map/ppermute | solution.py:301
  74.6 0.7 collective-permute-done.16.refs_2_
  75.3 0.6 collective-permute-done.15.refs_1_
  75.9 1.1 %shard_map.110 = (f32[3,96,192]{2,1,0:T(8,128)}, f32[192,96]{1,0:T(8,128)}, f32[3,96,192]{2,1,0:T(8,128)}, f32[192,96]{1,0:T(8,128)}) custom-call(bf16[2,24,768]{2,1,0:T(8,128)(2,1)S(1)} %shard_map.109.refs_0_, bf16[2,24,768]{2,1,0:T(8,128)(2,1)S(1)} %collective-permute-done.15.refs_1_, bf16[2,24,768]{2,1,0:T(8,128)(2,1)S(1)} %collective-permute-done.16.refs_2_, ...), custom_call_target="tpu_custom_call" | custom-call | tf_op jit(solution)/shard_map/pallas_call | solution.py:53
  (2 shorter events, 0.0 us)
Async XLA Ops:
  0.6 25.1 %copy-start.1 = (bf16[3,384,192]{1,2,0:T(8,128)(2,1)S(1)}, bf16[3,384,192]{1,2,0:T(8,128)(2,1)}, u32[]{:S(2)}) copy-start(bf16[3,384,192]{1,2,0:T(8,128)(2,1)} %param.10) | copy-start | bytes 1327108
  0.6 25.0 %copy-start = (bf16[3,384,192]{1,2,0:T(8,128)(2,1)S(1)}, bf16[3,384,192]{1,2,0:T(8,128)(2,1)}, u32[]{:S(2)}) copy-start(bf16[3,384,192]{1,2,0:T(8,128)(2,1)} %param.8) | copy-start | bytes 1327108
  0.7 1.2 %copy-start.2 = (bf16[1,1024,384]{2,1,0:T(8,128)(2,1)S(1)}, bf16[1,1024,384]{2,1,0:T(8,128)(2,1)}, u32[]{:S(2)}) copy-start(bf16[1,1024,384]{2,1,0:T(8,128)(2,1)} %param.6) | copy-start | bytes 2359300
  1.9 10.9 %collective-permute-start = (bf16[256,384]{1,0:T(8,128)(2,1)S(1)}, bf16[256,384]{1,0:T(8,128)(2,1)S(1)}, u32[]{:S(2)}, u32[]{:S(2)}) collective-permute-start(bf16[256,384]{1,0:T(8,128)(2,1)S(1)} %get-tuple-element.45), channel_id=1, source_target_pairs={{0,6},{1,7},{2,4},{3,5},{4,2},{5,3},{6,0},{7,1},{8,14},{9,15},{10,... | collective-permute-start | bytes 589832 | tf_op jit(solution)/shard_map/ppermute | solution.py:301
  7.0 13.0 %collective-permute-start.4 = (bf16[256,384]{1,0:T(8,128)(2,1)S(1)}, bf16[256,384]{1,0:T(8,128)(2,1)S(1)}, u32[]{:S(2)}, u32[]{:S(2)}) collective-permute-start(bf16[256,384]{1,0:T(8,128)(2,1)S(1)} %get-tuple-element.51), channel_id=1, source_target_pairs={{0,2},{1,3},{2,0},{3,1},{4,6},{5,7},{6,4},{7,5},{8,10},{9,11},{10,... | collective-permute-start | bytes 589832 | tf_op jit(solution)/shard_map/ppermute | solution.py:301
  7.1 18.6 %collective-permute-start.5 = (bf16[256,384]{1,0:T(8,128)(2,1)S(1)}, bf16[256,384]{1,0:T(8,128)(2,1)S(1)}, u32[]{:S(2)}, u32[]{:S(2)}) collective-permute-start(bf16[256,384]{1,0:T(8,128)(2,1)S(1)} %get-tuple-element.52), channel_id=1, source_target_pairs={{0,4},{1,5},{2,6},{3,7},{4,0},{5,1},{6,2},{7,3},{8,12},{9,13},{10,... | collective-permute-start | bytes 589832 | tf_op jit(solution)/shard_map/ppermute | solution.py:301
  7.7 1.1 %copy-start.3 = (bf16[1,1024,384]{2,1,0:T(8,128)(2,1)S(1)}, bf16[1,1024,384]{2,1,0:T(8,128)(2,1)}, u32[]{:S(2)}) copy-start(bf16[1,1024,384]{2,1,0:T(8,128)(2,1)} %param.7) | copy-start | bytes 2359300
  8.8 28.6 %copy-start.5 = (bf16[192,384]{1,0:T(8,128)(2,1)S(1)}, bf16[192,384]{1,0:T(8,128)(2,1)}, u32[]{:S(2)}) copy-start(bf16[192,384]{1,0:T(8,128)(2,1)} %refs_9_.1) | copy-start | bytes 442372
  12.8 22.4 %collective-permute-start.1 = (bf16[256,384]{1,0:T(8,128)(2,1)S(1)}, bf16[256,384]{1,0:T(8,128)(2,1)S(1)}, u32[]{:S(2)}, u32[]{:S(2)}) collective-permute-start(bf16[256,384]{1,0:T(8,128)(2,1)S(1)} %get-tuple-element.47), channel_id=1, source_target_pairs={{0,2},{1,3},{2,0},{3,1},{4,6},{5,7},{6,4},{7,5},{8,10},{9,11},{10,... | collective-permute-start | bytes 589832 | tf_op jit(solution)/shard_map/ppermute | solution.py:301
  17.7 19.7 %collective-permute-start.2 = (bf16[256,384]{1,0:T(8,128)(2,1)S(1)}, bf16[256,384]{1,0:T(8,128)(2,1)S(1)}, u32[]{:S(2)}, u32[]{:S(2)}) collective-permute-start(bf16[256,384]{1,0:T(8,128)(2,1)S(1)} %get-tuple-element.48), channel_id=1, source_target_pairs={{0,4},{1,5},{2,6},{3,7},{4,0},{5,1},{6,2},{7,3},{8,12},{9,13},{10,... | collective-permute-start | bytes 589832 | tf_op jit(solution)/shard_map/ppermute | solution.py:301
  18.3 19.1 %collective-permute-start.3 = (bf16[256,384]{1,0:T(8,128)(2,1)S(1)}, bf16[256,384]{1,0:T(8,128)(2,1)S(1)}, u32[]{:S(2)}, u32[]{:S(2)}) collective-permute-start(bf16[256,384]{1,0:T(8,128)(2,1)S(1)} %get-tuple-element.49), channel_id=1, source_target_pairs={{0,6},{1,7},{2,4},{3,5},{4,2},{5,3},{6,0},{7,1},{8,14},{9,15},{10,... | collective-permute-start | bytes 589832 | tf_op jit(solution)/shard_map/ppermute | solution.py:301
  25.7 0.9 %copy-start.4 = (bf16[192,384]{1,0:T(8,128)(2,1)S(1)}, bf16[192,384]{1,0:T(8,128)(2,1)}, u32[]{:S(2)}) copy-start(bf16[192,384]{1,0:T(8,128)(2,1)} %refs_8_.1) | copy-start | bytes 442372
  41.0 2.8 %collective-permute-start.9 = (bf16[2,2,96,768]{3,2,1,0:T(8,128)(2,1)S(1)}, bf16[2,2,96,768]{3,2,1,0:T(8,128)(2,1)S(1)}, u32[]{:S(2)}, u32[]{:S(2)}) collective-permute-start(bf16[2,2,96,768]{3,2,1,0:T(8,128)(2,1)S(1)} %get-tuple-element.66), channel_id=1, source_target_pairs={{0,8},{1,9},{2,10},{3,11},{4,12},{5,13},{6,14},{7,15},{8,0},{9,1},... | collective-permute-start | bytes 1769480 | tf_op jit(solution)/shard_map/ppermute | solution.py:301
  41.1 9.5 %collective-permute-start.8 = (bf16[256,384]{1,0:T(8,128)(2,1)S(1)}, bf16[256,384]{1,0:T(8,128)(2,1)S(1)}, u32[]{:S(2)}, u32[]{:S(2)}) collective-permute-start(bf16[256,384]{1,0:T(8,128)(2,1)S(1)} %get-tuple-element.64), channel_id=1, source_target_pairs={{0,6},{1,7},{2,0},{3,1},{4,2},{5,3},{6,4},{7,5},{8,14},{9,15},{10,... | collective-permute-start | bytes 589832 | tf_op jit(solution)/shard_map/ppermute | solution.py:291
  44.0 9.7 %collective-permute-start.10 = (bf16[2,48,768]{2,1,0:T(8,128)(2,1)S(1)}, bf16[2,48,768]{2,1,0:T(8,128)(2,1)S(1)}, u32[]{:S(2)}, u32[]{:S(2)}) collective-permute-start(bf16[2,48,768]{2,1,0:T(8,128)(2,1)S(1)} %get-tuple-element.68), channel_id=1, source_target_pairs={{0,1},{1,0},{2,3},{3,2},{4,5},{5,4},{6,7},{7,6},{8,9},{9,8},{10,11... | collective-permute-start | bytes 442376 | tf_op jit(solution)/shard_map/ppermute | solution.py:301
  45.6 8.1 %collective-permute-start.11 = (bf16[2,48,768]{2,1,0:T(8,128)(2,1)S(1)}, bf16[2,48,768]{2,1,0:T(8,128)(2,1)S(1)}, u32[]{:S(2)}, u32[]{:S(2)}) collective-permute-start(bf16[2,48,768]{2,1,0:T(8,128)(2,1)S(1)} %get-tuple-element.69), channel_id=1, source_target_pairs={{0,16},{1,17},{2,18},{3,19},{4,20},{5,21},{6,22},{7,23},{8,24},{9,... | collective-permute-start | bytes 442376 | tf_op jit(solution)/shard_map/ppermute | solution.py:301
  47.0 7.3 %collective-permute-start.12 = (bf16[2,48,768]{2,1,0:T(8,128)(2,1)S(1)}, bf16[2,48,768]{2,1,0:T(8,128)(2,1)S(1)}, u32[]{:S(2)}, u32[]{:S(2)}) collective-permute-start(bf16[2,48,768]{2,1,0:T(8,128)(2,1)S(1)} %get-tuple-element.70), channel_id=1, source_target_pairs={{0,17},{1,16},{2,19},{3,18},{4,21},{5,20},{6,23},{7,22},{8,25},{9,... | collective-permute-start | bytes 442376 | tf_op jit(solution)/shard_map/ppermute | solution.py:301
  47.5 10.0 %collective-permute-start.6 = (bf16[256,384]{1,0:T(8,128)(2,1)S(1)}, bf16[256,384]{1,0:T(8,128)(2,1)S(1)}, u32[]{:S(2)}, u32[]{:S(2)}) collective-permute-start(bf16[256,384]{1,0:T(8,128)(2,1)S(1)} %get-tuple-element.62), channel_id=1, source_target_pairs={{0,2},{1,3},{2,4},{3,5},{4,6},{5,7},{6,0},{7,1},{8,10},{9,11},{10,... | collective-permute-start | bytes 589832 | tf_op jit(solution)/shard_map/ppermute | solution.py:291
  50.6 15.6 %collective-permute-start.7 = (bf16[256,384]{1,0:T(8,128)(2,1)S(1)}, bf16[256,384]{1,0:T(8,128)(2,1)S(1)}, u32[]{:S(2)}, u32[]{:S(2)}) collective-permute-start(bf16[256,384]{1,0:T(8,128)(2,1)S(1)} %get-tuple-element.63), channel_id=1, source_target_pairs={{0,4},{1,5},{2,6},{3,7},{4,0},{5,1},{6,2},{7,3},{8,12},{9,13},{10,... | collective-permute-start | bytes 589832 | tf_op jit(solution)/shard_map/ppermute | solution.py:291
  54.4 5.7 %collective-permute-start.13 = (bf16[2,24,768]{2,1,0:T(8,128)(2,1)S(1)}, bf16[2,24,768]{2,1,0:T(8,128)(2,1)S(1)}, u32[]{:S(2)}, u32[]{:S(2)}) collective-permute-start(bf16[2,24,768]{2,1,0:T(8,128)(2,1)S(1)} %get-tuple-element.72), channel_id=1, source_target_pairs={{0,2},{1,3},{2,0},{3,1},{4,6},{5,7},{6,4},{7,5},{8,10},{9,11},{10,... | collective-permute-start | bytes 221192 | tf_op jit(solution)/shard_map/ppermute | solution.py:301
  60.1 8.4 %collective-permute-start.14 = (bf16[2,24,768]{2,1,0:T(8,128)(2,1)S(1)}, bf16[2,24,768]{2,1,0:T(8,128)(2,1)S(1)}, u32[]{:S(2)}, u32[]{:S(2)}) collective-permute-start(bf16[2,24,768]{2,1,0:T(8,128)(2,1)S(1)} %shard_map.108.refs_0_), channel_id=1, source_target_pairs={{0,4},{1,5},{2,6},{3,7},{4,0},{5,1},{6,2},{7,3},{8,12},{9,13},{10,... | collective-permute-start | bytes 221192 | tf_op jit(solution)/shard_map/ppermute | solution.py:301
  68.5 6.1 %collective-permute-start.17 = (bf16[2,24,768]{2,1,0:T(8,128)(2,1)S(1)}, bf16[2,24,768]{2,1,0:T(8,128)(2,1)S(1)}, u32[]{:S(2)}, u32[]{:S(2)}) collective-permute-start(bf16[2,24,768]{2,1,0:T(8,128)(2,1)S(1)} %shard_map.109.refs_0_), channel_id=1, source_target_pairs={{0,3},{1,2},{2,1},{3,0},{4,7},{5,6},{6,5},{7,4},{8,11},{9,10},{10,... | collective-permute-start | bytes 221192 | tf_op jit(solution)/shard_map/ppermute | solution.py:301
  69.0 6.2 %collective-permute-start.16 = (bf16[2,24,768]{2,1,0:T(8,128)(2,1)S(1)}, bf16[2,24,768]{2,1,0:T(8,128)(2,1)S(1)}, u32[]{:S(2)}, u32[]{:S(2)}) collective-permute-start(bf16[2,24,768]{2,1,0:T(8,128)(2,1)S(1)} %shard_map.109.refs_0_), channel_id=1, source_target_pairs={{0,2},{1,3},{2,0},{3,1},{4,6},{5,7},{6,4},{7,5},{8,10},{9,11},{10,... | collective-permute-start | bytes 221192 | tf_op jit(solution)/shard_map/ppermute | solution.py:301
  71.5 4.4 %collective-permute-start.15 = (bf16[2,24,768]{2,1,0:T(8,128)(2,1)S(1)}, bf16[2,24,768]{2,1,0:T(8,128)(2,1)S(1)}, u32[]{:S(2)}, u32[]{:S(2)}) collective-permute-start(bf16[2,24,768]{2,1,0:T(8,128)(2,1)S(1)} %shard_map.109.refs_0_), channel_id=1, source_target_pairs={{0,1},{1,0},{2,3},{3,2},{4,5},{5,4},{6,7},{7,6},{8,9},{9,8},{10,11... | collective-permute-start | bytes 221192 | tf_op jit(solution)/shard_map/ppermute | solution.py:301

commit v7 on v6

--- a/solution.py
+++ b/solution.py
@@ -14,7 +14,7 @@
 WIDE_TILE = 512
 CHUNK = 32
 MAX_PERMUTES = 4
-NEED = ((3,), (1,), (2,))
+NEED = ((3,), (), (1, 2))
 ORDER = (2, 3, 1)
 GATE = (3,)
 BF16 = jnp.bfloat16

time: 77.2 us -> 77.2 us (level)
  no operation moved by 1% of the time
where the time goes in v7:
time: 77.2 us; the launch traced here: 77 us
  starting transfers between devices  35.4 us (46%)
  waiting for transfers between devices  22.8 us (30%)
  Pallas kernels  14.7 us (19%)
  local copies, waits for them, and re-layouts  3.26 us (4%)
    ppermute x15, starting transfers between devices, mirrored(): return lax.ppermute(block, ('dp', 'seq'), route)  26.6 us
    ppermute x15, waiting for transfers between devices, mirrored(): return lax.ppermute(block, ('dp', 'seq'), route)  20 us
    pallas_call x10, Pallas kernels, call(): pl.pallas_call(body, out_shape=[jax.ShapeDtypeStruct(s, d) for s, d in ou...  14.7 us
    ppermute x3, starting transfers between devices, send_ahead(): return lax.ppermute(block, 'seq', route)  8.88 us
    unnamed x12, local copies, waits for them, and re-layouts  3.26 us
    ppermute x3, waiting for transfers between devices, send_ahead(): return lax.ppermute(block, 'seq', route)  2.83 us
  transfers between devices with their start and end apart: 18, of which 10 were waited for; matrix products, arithmetic and copies ran while one was open for 0% of the time, Pallas kernels for 13%

profile of v7, /device:TPU:0, one launch (start us, length us, event | category | flops | bytes accessed | tf_op | source)
XLA Modules:
  0.0 77.0 jit_solution(17151399779620342328)
XLA Ops:
  0.6 0.0 copy-start.1
  0.6 0.0 copy-start
  0.7 0.0 copy-start.2
  0.7 1.2 %copy-done.2 = bf16[1,1024,384]{2,1,0:T(8,128)(2,1)S(1)} copy-done((bf16[1,1024,384]{2,1,0:T(8,128)(2,1)S(1)}, bf16[1,1024,384]{2,1,0:T(8,128)(2,1)}, u32[]{:S(2)}) %copy-start.2) | copy-done | bytes 786456
  1.9 0.1 shard_map.102
  1.9 5.1 %collective-permute-start = (bf16[256,384]{1,0:T(8,128)(2,1)S(1)}, bf16[256,384]{1,0:T(8,128)(2,1)S(1)}, u32[]{:S(2)}, u32[]{:S(2)}) collective-permute-start(bf16[256,384]{1,0:T(8,128)(2,1)S(1)} %get-tuple-element.45), channel_id=1, source_target_pairs={{0,6},{1,7},{2,4},{3,5},{4,2},{5,3},{6,0},{7,1},{8,14},{9,15},{10,... | collective-permute-start | bytes 589832 | tf_op jit(solution)/shard_map/ppermute | solution.py:301
  7.0 0.0 collective-permute-start.4
  7.1 0.6 collective-permute-start.5
  7.7 0.0 copy-start.3
  7.7 1.1 %copy-done.3 = bf16[1,1024,384]{2,1,0:T(8,128)(2,1)S(1)} copy-done((bf16[1,1024,384]{2,1,0:T(8,128)(2,1)S(1)}, bf16[1,1024,384]{2,1,0:T(8,128)(2,1)}, u32[]{:S(2)}) %copy-start.3) | copy-done | bytes 786456
  8.8 0.0 copy-start.5
  8.8 0.1 shard_map.101
  8.9 3.9 %collective-permute-done.refs_3_ = bf16[256,384]{1,0:T(8,128)(2,1)S(1)} collective-permute-done((bf16[256,384]{1,0:T(8,128)(2,1)S(1)}, bf16[256,384]{1,0:T(8,128)(2,1)S(1)}, u32[]{:S(2)}, u32[]{:S(2)}) %collective-permute-start) | collective-permute-done | bytes 196640 | tf_op jit(solution)/shard_map/ppermute | solution.py:301
  12.8 4.9 %collective-permute-start.1 = (bf16[256,384]{1,0:T(8,128)(2,1)S(1)}, bf16[256,384]{1,0:T(8,128)(2,1)S(1)}, u32[]{:S(2)}, u32[]{:S(2)}) collective-permute-start(bf16[256,384]{1,0:T(8,128)(2,1)S(1)} %get-tuple-element.47), channel_id=1, source_target_pairs={{0,2},{1,3},{2,0},{3,1},{4,6},{5,7},{6,4},{7,5},{8,10},{9,11},{10,... | collective-permute-start | bytes 589832 | tf_op jit(solution)/shard_map/ppermute | solution.py:301
  17.7 0.7 collective-permute-start.2
  18.3 1.7 %collective-permute-start.3 = (bf16[256,384]{1,0:T(8,128)(2,1)S(1)}, bf16[256,384]{1,0:T(8,128)(2,1)S(1)}, u32[]{:S(2)}, u32[]{:S(2)}) collective-permute-start(bf16[256,384]{1,0:T(8,128)(2,1)S(1)} %get-tuple-element.49), channel_id=1, source_target_pairs={{0,6},{1,7},{2,4},{3,5},{4,2},{5,3},{6,0},{7,1},{8,14},{9,15},{10,... | collective-permute-start | bytes 589832 | tf_op jit(solution)/shard_map/ppermute | solution.py:301
  20.0 0.0 collective-permute-done.4.refs_1_
  20.0 5.6 %collective-permute-done.5.refs_2_ = bf16[256,384]{1,0:T(8,128)(2,1)S(1)} collective-permute-done((bf16[256,384]{1,0:T(8,128)(2,1)S(1)}, bf16[256,384]{1,0:T(8,128)(2,1)S(1)}, u32[]{:S(2)}, u32[]{:S(2)}) %collective-permute-start.5) | collective-permute-done | bytes 196640 | tf_op jit(solution)/shard_map/ppermute | solution.py:301
  25.7 0.0 copy-done.1
  25.7 0.0 copy-done
  25.7 0.0 copy-start.4
  25.7 0.9 %copy-done.4 = bf16[192,384]{1,0:T(8,128)(2,1)S(1)} copy-done((bf16[192,384]{1,0:T(8,128)(2,1)S(1)}, bf16[192,384]{1,0:T(8,128)(2,1)}, u32[]{:S(2)}) %copy-start.4) | copy-done | bytes 147480
  26.6 8.6 %shard_map.103 = (bf16[384,1024]{1,0:T(8,128)(2,1)S(1)}, bf16[192,1024]{1,0:T(8,128)(2,1)S(1)}, f32[1024,384]{1,0:T(8,128)S(1)}, f32[1024,192]{1,0:T(8,128)S(1)}...) custom-call(bf16[256,384]{1,0:T(8,128)(2,1)S(1)} %get-tuple-element., ...), custom_call_target="tpu_custom_call" | custom-call | tf_op jit(solution)/shard_map/pallas_call | solution.py:53
  35.2 0.0 collective-permute-done.1.refs_1_
  35.2 2.1 %collective-permute-done.2.refs_2_ = bf16[256,384]{1,0:T(8,128)(2,1)S(1)} collective-permute-done((bf16[256,384]{1,0:T(8,128)(2,1)S(1)}, bf16[256,384]{1,0:T(8,128)(2,1)S(1)}, u32[]{:S(2)}, u32[]{:S(2)}) %collective-permute-start.2) | collective-permute-done | bytes 196640 | tf_op jit(solution)/shard_map/ppermute | solution.py:301
  37.4 0.0 collective-permute-done.3.refs_3_
  37.4 0.0 copy-done.5
  37.4 3.6 %shard_map.104 = (bf16[256,384]{1,0:T(8,128)(2,1)S(1)}, bf16[256,384]{1,0:T(8,128)(2,1)S(1)}, bf16[256,384]{1,0:T(8,128)(2,1)S(1)}, bf16[256,384]{1,0:T(8,128)(2...) custom-call(bf16[256,384]{1,0:T(8,128)(2,1)S(1)} %get-tuple-element.46.refs_0_, ...), custom_call_target="tpu_custom_call" | custom-call | tf_op jit(solution)/shard_map/pallas_call | solution.py:53
  41.0 0.1 collective-permute-start.9
  41.1 2.7 %collective-permute-start.8 = (bf16[256,384]{1,0:T(8,128)(2,1)S(1)}, bf16[256,384]{1,0:T(8,128)(2,1)S(1)}, u32[]{:S(2)}, u32[]{:S(2)}) collective-permute-start(bf16[256,384]{1,0:T(8,128)(2,1)S(1)} %get-tuple-element.64), channel_id=1, source_target_pairs={{0,6},{1,7},{2,0},{3,1},{4,2},{5,3},{6,4},{7,5},{8,14},{9,15},{10,... | collective-permute-start | bytes 589832 | tf_op jit(solution)/shard_map/ppermute | solution.py:291
  43.8 0.0 collective-permute-done.9.refs_1_
  43.8 0.1 shard_map.106
  44.0 1.6 %collective-permute-start.10 = (bf16[2,48,768]{2,1,0:T(8,128)(2,1)S(1)}, bf16[2,48,768]{2,1,0:T(8,128)(2,1)S(1)}, u32[]{:S(2)}, u32[]{:S(2)}) collective-permute-start(bf16[2,48,768]{2,1,0:T(8,128)(2,1)S(1)} %get-tuple-element.68), channel_id=1, source_target_pairs={{0,1},{1,0},{2,3},{3,2},{4,5},{5,4},{6,7},{7,6},{8,9},{9,8},{10,11... | collective-permute-start | bytes 442376 | tf_op jit(solution)/shard_map/ppermute | solution.py:301
  45.6 1.5 %collective-permute-start.11 = (bf16[2,48,768]{2,1,0:T(8,128)(2,1)S(1)}, bf16[2,48,768]{2,1,0:T(8,128)(2,1)S(1)}, u32[]{:S(2)}, u32[]{:S(2)}) collective-permute-start(bf16[2,48,768]{2,1,0:T(8,128)(2,1)S(1)} %get-tuple-element.69), channel_id=1, source_target_pairs={{0,16},{1,17},{2,18},{3,19},{4,20},{5,21},{6,22},{7,23},{8,24},{9,... | collective-permute-start | bytes 442376 | tf_op jit(solution)/shard_map/ppermute | solution.py:301
  47.0 0.5 collective-permute-start.12
  47.5 3.1 %collective-permute-start.6 = (bf16[256,384]{1,0:T(8,128)(2,1)S(1)}, bf16[256,384]{1,0:T(8,128)(2,1)S(1)}, u32[]{:S(2)}, u32[]{:S(2)}) collective-permute-start(bf16[256,384]{1,0:T(8,128)(2,1)S(1)} %get-tuple-element.62), channel_id=1, source_target_pairs={{0,2},{1,3},{2,4},{3,5},{4,6},{5,7},{6,0},{7,1},{8,10},{9,11},{10,... | collective-permute-start | bytes 589832 | tf_op jit(solution)/shard_map/ppermute | solution.py:291
  50.6 0.0 collective-permute-done.8.refs_3_.refs_4_
  50.6 3.1 %collective-permute-start.7 = (bf16[256,384]{1,0:T(8,128)(2,1)S(1)}, bf16[256,384]{1,0:T(8,128)(2,1)S(1)}, u32[]{:S(2)}, u32[]{:S(2)}) collective-permute-start(bf16[256,384]{1,0:T(8,128)(2,1)S(1)} %get-tuple-element.63), channel_id=1, source_target_pairs={{0,4},{1,5},{2,6},{3,7},{4,0},{5,1},{6,2},{7,3},{8,12},{9,13},{10,... | collective-permute-start | bytes 589832 | tf_op jit(solution)/shard_map/ppermute | solution.py:291
  53.7 0.0 collective-permute-done.10.refs_1_
  53.7 0.0 collective-permute-done.11.refs_2_
  53.7 0.6 collective-permute-done.12.refs_3_
  54.3 0.1 shard_map.107
  54.4 3.1 %collective-permute-start.13 = (bf16[2,24,768]{2,1,0:T(8,128)(2,1)S(1)}, bf16[2,24,768]{2,1,0:T(8,128)(2,1)S(1)}, u32[]{:S(2)}, u32[]{:S(2)}) collective-permute-start(bf16[2,24,768]{2,1,0:T(8,128)(2,1)S(1)} %get-tuple-element.72), channel_id=1, source_target_pairs={{0,2},{1,3},{2,0},{3,1},{4,6},{5,7},{6,4},{7,5},{8,10},{9,11},{10,... | collective-permute-start | bytes 221192 | tf_op jit(solution)/shard_map/ppermute | solution.py:301
  57.5 2.5 %collective-permute-done.13.refs_1_ = bf16[2,24,768]{2,1,0:T(8,128)(2,1)S(1)} collective-permute-done((bf16[2,24,768]{2,1,0:T(8,128)(2,1)S(1)}, bf16[2,24,768]{2,1,0:T(8,128)(2,1)S(1)}, u32[]{:S(2)}, u32[]{:S(2)}) %collective-permute-start.13) | collective-permute-done | bytes 73760 | tf_op jit(solution)/shard_map/ppermute | solution.py:301
  60.1 3.3 %collective-permute-start.14 = (bf16[2,24,768]{2,1,0:T(8,128)(2,1)S(1)}, bf16[2,24,768]{2,1,0:T(8,128)(2,1)S(1)}, u32[]{:S(2)}, u32[]{:S(2)}) collective-permute-start(bf16[2,24,768]{2,1,0:T(8,128)(2,1)S(1)} %shard_map.108.refs_0_), channel_id=1, source_target_pairs={{0,4},{1,5},{2,6},{3,7},{4,0},{5,1},{6,2},{7,3},{8,12},{9,13},{10,... | collective-permute-start | bytes 221192 | tf_op jit(solution)/shard_map/ppermute | solution.py:301
  63.4 0.0 collective-permute-done.6.refs_1_.refs_2_
  63.4 2.8 %collective-permute-done.7.refs_2_.refs_3_ = bf16[256,384]{1,0:T(8,128)(2,1)S(1)} collective-permute-done((bf16[256,384]{1,0:T(8,128)(2,1)S(1)}, bf16[256,384]{1,0:T(8,128)(2,1)S(1)}, u32[]{:S(2)}, u32[]{:S(2)}) %collective-permute-start.7) | collective-permute-done | bytes 196640 | tf_op jit(solution)/shard_map/ppermute | solution.py:291
  66.2 2.3 %collective-permute-done.14.refs_1_ = bf16[2,24,768]{2,1,0:T(8,128)(2,1)S(1)} collective-permute-done((bf16[2,24,768]{2,1,0:T(8,128)(2,1)S(1)}, bf16[2,24,768]{2,1,0:T(8,128)(2,1)S(1)}, u32[]{:S(2)}, u32[]{:S(2)}) %collective-permute-start.14) | collective-permute-done | bytes 73760 | tf_op jit(solution)/shard_map/ppermute | solution.py:301
  68.5 0.5 collective-permute-start.17
  69.0 2.5 %collective-permute-start.16 = (bf16[2,24,768]{2,1,0:T(8,128)(2,1)S(1)}, bf16[2,24,768]{2,1,0:T(8,128)(2,1)S(1)}, u32[]{:S(2)}, u32[]{:S(2)}) collective-permute-start(bf16[2,24,768]{2,1,0:T(8,128)(2,1)S(1)} %shard_map.109.refs_0_), channel_id=1, source_target_pairs={{0,2},{1,3},{2,0},{3,1},{4,6},{5,7},{6,4},{7,5},{8,10},{9,11},{10,... | collective-permute-start | bytes 221192 | tf_op jit(solution)/shard_map/ppermute | solution.py:301
  71.5 0.5 collective-permute-start.15
  72.1 1.0 %shard_map.105 = bf16[1024,384]{1,0:T(8,128)(2,1)} custom-call(bf16[256,384]{1,0:T(8,128)(2,1)S(1)} %get-tuple-element.61.refs_0_, bf16[256,384]{1,0:T(8,128)(2,1)S(1)} %collective-permute-done.6.refs_1_.refs_2_, bf16[256,384]{1,0:T(8,128)(2,1)S(1)} %collective-permute-done.7.refs_2_.refs_3_, bf16[256,384]{1,0:T(8,128)(2,1)S(1)} %collective-permute-done.8.refs_3_.refs_4_), custom_call_target="tpu_custom_call" | custom-call | tf_op jit(solution)/shard_map/pallas_call | solution.py:53
  73.0 1.5 %collective-permute-done.17.refs_3_ = bf16[2,24,768]{2,1,0:T(8,128)(2,1)S(1)} collective-permute-done((bf16[2,24,768]{2,1,0:T(8,128)(2,1)S(1)}, bf16[2,24,768]{2,1,0:T(8,128)(2,1)S(1)}, u32[]{:S(2)}, u32[]{:S(2)}) %collective-permute-start.17) | collective-permute-done | bytes 73760 | tf_op jit(solution)/shard_map/ppermute | solution.py:301
  74.6 0.7 collective-permute-done.16.refs_2_
  75.3 0.6 collective-permute-done.15.refs_1_
  75.9 1.1 %shard_map.110 = (f32[3,96,192]{2,1,0:T(8,128)}, f32[192,96]{1,0:T(8,128)}, f32[3,96,192]{2,1,0:T(8,128)}, f32[192,96]{1,0:T(8,128)}) custom-call(bf16[2,24,768]{2,1,0:T(8,128)(2,1)S(1)} %shard_map.109.refs_0_, bf16[2,24,768]{2,1,0:T(8,128)(2,1)S(1)} %collective-permute-done.15.refs_1_, bf16[2,24,768]{2,1,0:T(8,128)(2,1)S(1)} %collective-permute-done.16.refs_2_, ...), custom_call_target="tpu_custom_call" | custom-call | tf_op jit(solution)/shard_map/pallas_call | solution.py:53
  (2 shorter events, 0.0 us)
Async XLA Ops:
  0.6 25.1 %copy-start.1 = (bf16[3,384,192]{1,2,0:T(8,128)(2,1)S(1)}, bf16[3,384,192]{1,2,0:T(8,128)(2,1)}, u32[]{:S(2)}) copy-start(bf16[3,384,192]{1,2,0:T(8,128)(2,1)} %param.10) | copy-start | bytes 1327108
  0.6 25.0 %copy-start = (bf16[3,384,192]{1,2,0:T(8,128)(2,1)S(1)}, bf16[3,384,192]{1,2,0:T(8,128)(2,1)}, u32[]{:S(2)}) copy-start(bf16[3,384,192]{1,2,0:T(8,128)(2,1)} %param.8) | copy-start | bytes 1327108
  0.7 1.2 %copy-start.2 = (bf16[1,1024,384]{2,1,0:T(8,128)(2,1)S(1)}, bf16[1,1024,384]{2,1,0:T(8,128)(2,1)}, u32[]{:S(2)}) copy-start(bf16[1,1024,384]{2,1,0:T(8,128)(2,1)} %param.6) | copy-start | bytes 2359300
  1.9 10.9 %collective-permute-start = (bf16[256,384]{1,0:T(8,128)(2,1)S(1)}, bf16[256,384]{1,0:T(8,128)(2,1)S(1)}, u32[]{:S(2)}, u32[]{:S(2)}) collective-permute-start(bf16[256,384]{1,0:T(8,128)(2,1)S(1)} %get-tuple-element.45), channel_id=1, source_target_pairs={{0,6},{1,7},{2,4},{3,5},{4,2},{5,3},{6,0},{7,1},{8,14},{9,15},{10,... | collective-permute-start | bytes 589832 | tf_op jit(solution)/shard_map/ppermute | solution.py:301
  7.0 13.0 %collective-permute-start.4 = (bf16[256,384]{1,0:T(8,128)(2,1)S(1)}, bf16[256,384]{1,0:T(8,128)(2,1)S(1)}, u32[]{:S(2)}, u32[]{:S(2)}) collective-permute-start(bf16[256,384]{1,0:T(8,128)(2,1)S(1)} %get-tuple-element.51), channel_id=1, source_target_pairs={{0,2},{1,3},{2,0},{3,1},{4,6},{5,7},{6,4},{7,5},{8,10},{9,11},{10,... | collective-permute-start | bytes 589832 | tf_op jit(solution)/shard_map/ppermute | solution.py:301
  7.1 18.6 %collective-permute-start.5 = (bf16[256,384]{1,0:T(8,128)(2,1)S(1)}, bf16[256,384]{1,0:T(8,128)(2,1)S(1)}, u32[]{:S(2)}, u32[]{:S(2)}) collective-permute-start(bf16[256,384]{1,0:T(8,128)(2,1)S(1)} %get-tuple-element.52), channel_id=1, source_target_pairs={{0,4},{1,5},{2,6},{3,7},{4,0},{5,1},{6,2},{7,3},{8,12},{9,13},{10,... | collective-permute-start | bytes 589832 | tf_op jit(solution)/shard_map/ppermute | solution.py:301
  7.7 1.1 %copy-start.3 = (bf16[1,1024,384]{2,1,0:T(8,128)(2,1)S(1)}, bf16[1,1024,384]{2,1,0:T(8,128)(2,1)}, u32[]{:S(2)}) copy-start(bf16[1,1024,384]{2,1,0:T(8,128)(2,1)} %param.7) | copy-start | bytes 2359300
  8.8 28.6 %copy-start.5 = (bf16[192,384]{1,0:T(8,128)(2,1)S(1)}, bf16[192,384]{1,0:T(8,128)(2,1)}, u32[]{:S(2)}) copy-start(bf16[192,384]{1,0:T(8,128)(2,1)} %refs_9_.1) | copy-start | bytes 442372
  12.8 22.4 %collective-permute-start.1 = (bf16[256,384]{1,0:T(8,128)(2,1)S(1)}, bf16[256,384]{1,0:T(8,128)(2,1)S(1)}, u32[]{:S(2)}, u32[]{:S(2)}) collective-permute-start(bf16[256,384]{1,0:T(8,128)(2,1)S(1)} %get-tuple-element.47), channel_id=1, source_target_pairs={{0,2},{1,3},{2,0},{3,1},{4,6},{5,7},{6,4},{7,5},{8,10},{9,11},{10,... | collective-permute-start | bytes 589832 | tf_op jit(solution)/shard_map/ppermute | solution.py:301
  17.7 19.7 %collective-permute-start.2 = (bf16[256,384]{1,0:T(8,128)(2,1)S(1)}, bf16[256,384]{1,0:T(8,128)(2,1)S(1)}, u32[]{:S(2)}, u32[]{:S(2)}) collective-permute-start(bf16[256,384]{1,0:T(8,128)(2,1)S(1)} %get-tuple-element.48), channel_id=1, source_target_pairs={{0,4},{1,5},{2,6},{3,7},{4,0},{5,1},{6,2},{7,3},{8,12},{9,13},{10,... | collective-permute-start | bytes 589832 | tf_op jit(solution)/shard_map/ppermute | solution.py:301
  18.3 19.1 %collective-permute-start.3 = (bf16[256,384]{1,0:T(8,128)(2,1)S(1)}, bf16[256,384]{1,0:T(8,128)(2,1)S(1)}, u32[]{:S(2)}, u32[]{:S(2)}) collective-permute-start(bf16[256,384]{1,0:T(8,128)(2,1)S(1)} %get-tuple-element.49), channel_id=1, source_target_pairs={{0,6},{1,7},{2,4},{3,5},{4,2},{5,3},{6,0},{7,1},{8,14},{9,15},{10,... | collective-permute-start | bytes 589832 | tf_op jit(solution)/shard_map/ppermute | solution.py:301
  25.7 0.9 %copy-start.4 = (bf16[192,384]{1,0:T(8,128)(2,1)S(1)}, bf16[192,384]{1,0:T(8,128)(2,1)}, u32[]{:S(2)}) copy-start(bf16[192,384]{1,0:T(8,128)(2,1)} %refs_8_.1) | copy-start | bytes 442372
  41.0 2.8 %collective-permute-start.9 = (bf16[2,2,96,768]{3,2,1,0:T(8,128)(2,1)S(1)}, bf16[2,2,96,768]{3,2,1,0:T(8,128)(2,1)S(1)}, u32[]{:S(2)}, u32[]{:S(2)}) collective-permute-start(bf16[2,2,96,768]{3,2,1,0:T(8,128)(2,1)S(1)} %get-tuple-element.66), channel_id=1, source_target_pairs={{0,8},{1,9},{2,10},{3,11},{4,12},{5,13},{6,14},{7,15},{8,0},{9,1},... | collective-permute-start | bytes 1769480 | tf_op jit(solution)/shard_map/ppermute | solution.py:301
  41.1 9.5 %collective-permute-start.8 = (bf16[256,384]{1,0:T(8,128)(2,1)S(1)}, bf16[256,384]{1,0:T(8,128)(2,1)S(1)}, u32[]{:S(2)}, u32[]{:S(2)}) collective-permute-start(bf16[256,384]{1,0:T(8,128)(2,1)S(1)} %get-tuple-element.64), channel_id=1, source_target_pairs={{0,6},{1,7},{2,0},{3,1},{4,2},{5,3},{6,4},{7,5},{8,14},{9,15},{10,... | collective-permute-start | bytes 589832 | tf_op jit(solution)/shard_map/ppermute | solution.py:291
  44.0 9.7 %collective-permute-start.10 = (bf16[2,48,768]{2,1,0:T(8,128)(2,1)S(1)}, bf16[2,48,768]{2,1,0:T(8,128)(2,1)S(1)}, u32[]{:S(2)}, u32[]{:S(2)}) collective-permute-start(bf16[2,48,768]{2,1,0:T(8,128)(2,1)S(1)} %get-tuple-element.68), channel_id=1, source_target_pairs={{0,1},{1,0},{2,3},{3,2},{4,5},{5,4},{6,7},{7,6},{8,9},{9,8},{10,11... | collective-permute-start | bytes 442376 | tf_op jit(solution)/shard_map/ppermute | solution.py:301
  45.6 8.1 %collective-permute-start.11 = (bf16[2,48,768]{2,1,0:T(8,128)(2,1)S(1)}, bf16[2,48,768]{2,1,0:T(8,128)(2,1)S(1)}, u32[]{:S(2)}, u32[]{:S(2)}) collective-permute-start(bf16[2,48,768]{2,1,0:T(8,128)(2,1)S(1)} %get-tuple-element.69), channel_id=1, source_target_pairs={{0,16},{1,17},{2,18},{3,19},{4,20},{5,21},{6,22},{7,23},{8,24},{9,... | collective-permute-start | bytes 442376 | tf_op jit(solution)/shard_map/ppermute | solution.py:301
  47.0 7.3 %collective-permute-start.12 = (bf16[2,48,768]{2,1,0:T(8,128)(2,1)S(1)}, bf16[2,48,768]{2,1,0:T(8,128)(2,1)S(1)}, u32[]{:S(2)}, u32[]{:S(2)}) collective-permute-start(bf16[2,48,768]{2,1,0:T(8,128)(2,1)S(1)} %get-tuple-element.70), channel_id=1, source_target_pairs={{0,17},{1,16},{2,19},{3,18},{4,21},{5,20},{6,23},{7,22},{8,25},{9,... | collective-permute-start | bytes 442376 | tf_op jit(solution)/shard_map/ppermute | solution.py:301
  47.5 15.9 %collective-permute-start.6 = (bf16[256,384]{1,0:T(8,128)(2,1)S(1)}, bf16[256,384]{1,0:T(8,128)(2,1)S(1)}, u32[]{:S(2)}, u32[]{:S(2)}) collective-permute-start(bf16[256,384]{1,0:T(8,128)(2,1)S(1)} %get-tuple-element.62), channel_id=1, source_target_pairs={{0,2},{1,3},{2,4},{3,5},{4,6},{5,7},{6,0},{7,1},{8,10},{9,11},{10,... | collective-permute-start | bytes 589832 | tf_op jit(solution)/shard_map/ppermute | solution.py:291
  50.6 15.6 %collective-permute-start.7 = (bf16[256,384]{1,0:T(8,128)(2,1)S(1)}, bf16[256,384]{1,0:T(8,128)(2,1)S(1)}, u32[]{:S(2)}, u32[]{:S(2)}) collective-permute-start(bf16[256,384]{1,0:T(8,128)(2,1)S(1)} %get-tuple-element.63), channel_id=1, source_target_pairs={{0,4},{1,5},{2,6},{3,7},{4,0},{5,1},{6,2},{7,3},{8,12},{9,13},{10,... | collective-permute-start | bytes 589832 | tf_op jit(solution)/shard_map/ppermute | solution.py:291
  54.4 5.7 %collective-permute-start.13 = (bf16[2,24,768]{2,1,0:T(8,128)(2,1)S(1)}, bf16[2,24,768]{2,1,0:T(8,128)(2,1)S(1)}, u32[]{:S(2)}, u32[]{:S(2)}) collective-permute-start(bf16[2,24,768]{2,1,0:T(8,128)(2,1)S(1)} %get-tuple-element.72), channel_id=1, source_target_pairs={{0,2},{1,3},{2,0},{3,1},{4,6},{5,7},{6,4},{7,5},{8,10},{9,11},{10,... | collective-permute-start | bytes 221192 | tf_op jit(solution)/shard_map/ppermute | solution.py:301
  60.1 8.4 %collective-permute-start.14 = (bf16[2,24,768]{2,1,0:T(8,128)(2,1)S(1)}, bf16[2,24,768]{2,1,0:T(8,128)(2,1)S(1)}, u32[]{:S(2)}, u32[]{:S(2)}) collective-permute-start(bf16[2,24,768]{2,1,0:T(8,128)(2,1)S(1)} %shard_map.108.refs_0_), channel_id=1, source_target_pairs={{0,4},{1,5},{2,6},{3,7},{4,0},{5,1},{6,2},{7,3},{8,12},{9,13},{10,... | collective-permute-start | bytes 221192 | tf_op jit(solution)/shard_map/ppermute | solution.py:301
  68.5 6.1 %collective-permute-start.17 = (bf16[2,24,768]{2,1,0:T(8,128)(2,1)S(1)}, bf16[2,24,768]{2,1,0:T(8,128)(2,1)S(1)}, u32[]{:S(2)}, u32[]{:S(2)}) collective-permute-start(bf16[2,24,768]{2,1,0:T(8,128)(2,1)S(1)} %shard_map.109.refs_0_), channel_id=1, source_target_pairs={{0,3},{1,2},{2,1},{3,0},{4,7},{5,6},{6,5},{7,4},{8,11},{9,10},{10,... | collective-permute-start | bytes 221192 | tf_op jit(solution)/shard_map/ppermute | solution.py:301
  69.0 6.2 %collective-permute-start.16 = (bf16[2,24,768]{2,1,0:T(8,128)(2,1)S(1)}, bf16[2,24,768]{2,1,0:T(8,128)(2,1)S(1)}, u32[]{:S(2)}, u32[]{:S(2)}) collective-permute-start(bf16[2,24,768]{2,1,0:T(8,128)(2,1)S(1)} %shard_map.109.refs_0_), channel_id=1, source_target_pairs={{0,2},{1,3},{2,0},{3,1},{4,6},{5,7},{6,4},{7,5},{8,10},{9,11},{10,... | collective-permute-start | bytes 221192 | tf_op jit(solution)/shard_map/ppermute | solution.py:301
  71.5 4.4 %collective-permute-start.15 = (bf16[2,24,768]{2,1,0:T(8,128)(2,1)S(1)}, bf16[2,24,768]{2,1,0:T(8,128)(2,1)S(1)}, u32[]{:S(2)}, u32[]{:S(2)}) collective-permute-start(bf16[2,24,768]{2,1,0:T(8,128)(2,1)S(1)} %shard_map.109.refs_0_), channel_id=1, source_target_pairs={{0,1},{1,0},{2,3},{3,2},{4,5},{5,4},{6,7},{7,6},{8,9},{9,8},{10,11... | collective-permute-start | bytes 221192 | tf_op jit(solution)/shard_map/ppermute | solution.py:301
